TPU v7x, 32 devices: a whole 2x2x4 slice. The times are simulated.
32 devices in a mesh: groups: 2 (over y), section: 2 (over core), sp: 4 (over z), blk: 2 (over x).
Axes of the slice: x: 2, y: 2, z: 4, core: 2. Of those that a mesh axis runs over, the one named last changes fastest.
Arguments:
- latent: float32 [2, 12, 64, 128], P('section', ('groups', 'blk'), 'sp'), parts along dimension 1, may hold values from -6 to 6
- queries: bfloat16 [2, 12, 2, 128, 4096], P('section', ('groups', 'blk'), None, 'sp'), parts along dimension 1
- keys: bfloat16 [2, 12, 2, 128, 4096], P('section', ('groups', 'blk'), None, 'sp'), parts along dimension 1
- values: bfloat16 [2, 12, 2, 128, 4096], P('section', ('groups', 'blk'), None, 'sp'), parts along dimension 1, may hold values from -6 to 6
- head_weight: bfloat16 [2, 64, 4096], P('section'), may hold values from -5 to 5
- step_index: int32 [2, 12], P('section', ('groups', 'blk')), parts along dimension 1, may hold values from 0 to 39, as said below
- skip_flags: int32 [12], P(('groups', 'blk')), parts along dimension 0, may hold values 0 or 1
Outputs:
- velocity: float32 [2, 12, 64, 128], P('section', ('groups', 'blk'), 'sp'), parts along dimension 1
- next_latent: float32 [2, 12, 64, 128], P('section', ('groups', 'blk'), 'sp'), parts along dimension 1
There are 2 independent parts, one for each index of `groups`. A program takes and returns all parts, laid end to end along the dimension named above; an argument that names none is the same for every part. Nothing has to cross between parts.
Inputs may be any that keep to these rules, and one draw needn't show every extreme that they name: `step_index`: row 0 (high-noise section) lies below 25, some videos at 24; row 1 (low-noise section) lies in 25 to 39.
All inputs are finite; a program needn't handle non-finite values. No bound on the sum of `skip_flags` on one device may be relied on, other than what follows from the above.
Results may differ from a plain program's by a relative error of at most 0.0041.
Values may be sent and summed in bfloat16 or wider, within the bound.
No kernel may reach another device: no remote copies, remote signals or barrier semaphores. Data moves between devices by JAX's collectives and lax.ppermute only.
A program may use at most 64 MiB of HBM per device.

v0:
```python
import jax
import jax.numpy as jnp
from jax import lax
from jax.sharding import PartitionSpec as P

HD = 128
CH = 64
STEPS = 40
SWITCH = 25


noise_shift = 12.0
high_guidance = 4.0
low_guidance = 3.0


def shifted(array, axis, by):
    devices = lax.axis_size(axis)
    pairs = [(i, i + by) for i in range(devices) if 0 <= i + by < devices]
    return lax.ppermute(array, axis, pairs)


def noise_level(step_now):
    fraction = 1.0 - step_now.astype(jnp.float32) / STEPS
    return noise_shift * fraction / (1.0 + (noise_shift - 1.0) * fraction)


def attend_heads(query_part, key_part, value_part):
    item_count, length, feature_width = query_part.shape
    head_count = feature_width // HD
    query_view = query_part.reshape(item_count, length, head_count, HD)
    key_view = key_part.reshape(item_count, length, head_count, HD)
    value_view = value_part.reshape(item_count, length, head_count, HD)
    scores = jnp.einsum(
        "iqhd,ikhd->ihqk", query_view, key_view, preferred_element_type=jnp.float32
    ) * HD ** (-0.5)
    row_max = jnp.max(scores, axis=3, keepdims=True)
    exponent = jnp.exp(scores - row_max)
    row_total = jnp.sum(exponent, axis=3, keepdims=True)
    weights = (exponent / row_total).astype(jnp.bfloat16)
    attended = jnp.einsum(
        "ihqk,ikhd->iqhd", weights, value_view, preferred_element_type=jnp.float32
    ).astype(jnp.bfloat16)
    return attended.reshape(item_count, length, feature_width)


def on_device(latent, queries, keys, values, head_weight, step_index, skip_flags):
    section_index = lax.axis_index("section")
    video_count = queries.shape[1]
    token_rows = queries.shape[3]
    feature_all = queries.shape[4]
    items = video_count * 2
    query_local = queries[0].reshape(items, token_rows, feature_all)
    key_local = keys[0].reshape(items, token_rows, feature_all)
    value_local = values[0].reshape(items, token_rows, feature_all)
    weight_local = head_weight[0]
    attended = attend_heads(
        lax.all_to_all(query_local, "sp", split_axis=2, concat_axis=1, tiled=True),
        lax.all_to_all(key_local, "sp", split_axis=2, concat_axis=1, tiled=True),
        lax.all_to_all(value_local, "sp", split_axis=2, concat_axis=1, tiled=True),
    )
    item_count = attended.shape[0]
    returned = lax.all_to_all(attended, "sp", split_axis=1, concat_axis=2, tiled=True)
    projected = lax.dot_general(
        returned, weight_local, (((2,), (1,)), ((), ())), preferred_element_type=jnp.float32
    )
    exchanged = projected.reshape(item_count, token_rows // 2, 2 * CH)
    pass_velocity = exchanged.reshape(video_count, 2, token_rows // 2, 2 * CH)
    conditional = pass_velocity[:, 0]
    unconditional = pass_velocity[:, 1]
    guidance = jnp.where(section_index == 0, jnp.float32(high_guidance), jnp.float32(low_guidance))
    guided = unconditional + guidance * (conditional - unconditional)
    skipping = (section_index == 1) & (skip_flags == 1)
    guided = jnp.where(skipping[:, None, None], conditional, guided)
    step_now = step_index[0]
    step_size = noise_level(step_now + 1) - noise_level(step_now)
    updated = latent[0] + step_size[:, None, None] * guided
    finish_mark = jnp.where(
        (section_index == 0) & (step_now + 1 == SWITCH), jnp.float32(1.0), jnp.float32(0.0)
    )
    arrived, arrived_mark = shifted((updated, finish_mark), "section", 1)
    taking = (section_index == 1) & (arrived_mark > 0.5)
    next_latent = jnp.where(taking[:, None, None], arrived, updated)
    return (guided[None], next_latent[None])


def solution(mesh):
    placed = (
        P("section", ("groups", "blk"), "sp", None),
        P("section", ("groups", "blk"), None, "sp", None),
        P("section", ("groups", "blk"), None, "sp", None),
        P("section", ("groups", "blk"), None, "sp", None),
        P("section", None, None),
        P("section", ("groups", "blk")),
        P(("groups", "blk")),
    )
    return jax.shard_map(
        on_device,
        mesh=mesh,
        in_specs=placed,
        out_specs=(
            P("section", ("groups", "blk"), "sp", None),
            P("section", ("groups", "blk"), "sp", None),
        ),
        check_vma=False,
    )
```

profile of v0, /device:TPU:0, one launch (start us, length us, event | category | flops | bytes accessed | tf_op | source)
XLA Modules:
  0.0 233.9 jit_solution(9079173877737753087)
XLA Ops:
  0.6 8.5 %copy.51 = bf16[6,32,4096]{1,0,2:T(8,128)(2,1)} copy(bf16[6,32,4096]{2,1,0:T(8,128)(2,1)} %bitcast.96) | data formatting | bytes 3145728 | tf_op jit(solution)/shard_map/reshape;squeeze | solution.py:53
  9.1 8.7 %reshape.125 = bf16[4,2,98304]{2,1,0:T(2,128)(2,1)} reshape(bf16[4096,6,32]{2,1,0:T(8,128)(2,1)} %bitcast.84) | data formatting | bytes 3145728
  17.9 6.3 %all-to-all-start = ((bf16[4,2,98304]{2,1,0:T(2,128)(2,1)}), bf16[4,2,98304]{2,1,0:T(2,128)(2,1)S(1)}, u32[]{:S(2)}, u32[]{:S(2)}) async-start(bf16[4,2,98304]{2,1,0:T(2,128)(2,1)} %reshape.125), calls=%async_computation | async-start | bytes 3145728 | tf_op jit(solution)/shard_map/all_to_all | solution.py:58
  24.2 8.4 %copy.54 = bf16[6,32,4096]{1,0,2:T(8,128)(2,1)} copy(bf16[6,32,4096]{2,1,0:T(8,128)(2,1)} %bitcast.97) | data formatting | bytes 3145728 | tf_op jit(solution)/shard_map/reshape;squeeze | solution.py:54
  32.6 8.7 %reshape.123 = bf16[4,2,98304]{2,1,0:T(2,128)(2,1)} reshape(bf16[4096,6,32]{2,1,0:T(8,128)(2,1)} %bitcast.85) | data formatting | bytes 3145728
  41.3 19.8 %all-to-all-done = bf16[4,2,98304]{2,1,0:T(2,128)(2,1)S(1)} async-done(((bf16[4,2,98304]{2,1,0:T(2,128)(2,1)}), bf16[4,2,98304]{2,1,0:T(2,128)(2,1)S(1)}, u32[]{:S(2)}, u32[]{:S(2)}) %all-to-all-start) | async-done | bytes 1572896 | tf_op jit(solution)/shard_map/all_to_all | solution.py:58
  61.1 1.2 copy-done.1
  62.3 4.4 %all-to-all-start.1 = ((bf16[4,2,98304]{2,1,0:T(2,128)(2,1)}), bf16[4,2,98304]{2,1,0:T(2,128)(2,1)}, u32[]{:S(2)}, u32[]{:S(2)}) async-start(bf16[4,2,98304]{2,1,0:T(2,128)(2,1)} %reshape.123), calls=%async_computation.1 | async-start | bytes 3145728 | tf_op jit(solution)/shard_map/all_to_all | solution.py:59
  66.7 8.4 %copy.59 = bf16[6,32,4096]{1,0,2:T(8,128)(2,1)} copy(bf16[6,32,4096]{2,1,0:T(8,128)(2,1)} %bitcast.98) | data formatting | bytes 3145728 | tf_op jit(solution)/shard_map/reshape;squeeze | solution.py:55
  75.1 8.8 %reshape.127 = bf16[4,2,98304]{2,1,0:T(2,128)(2,1)} reshape(bf16[4096,6,32]{2,1,0:T(8,128)(2,1)} %bitcast.86) | data formatting | bytes 3145728
  83.8 19.4 %all-to-all-done.1 = bf16[4,2,98304]{2,1,0:T(2,128)(2,1)} async-done(((bf16[4,2,98304]{2,1,0:T(2,128)(2,1)}), bf16[4,2,98304]{2,1,0:T(2,128)(2,1)}, u32[]{:S(2)}, u32[]{:S(2)}) %all-to-all-start.1) | async-done | bytes 1572896 | tf_op jit(solution)/shard_map/all_to_all | solution.py:59
  103.2 3.7 %all-to-all-start.2 = ((bf16[4,2,98304]{2,1,0:T(2,128)(2,1)}), bf16[4,2,98304]{2,1,0:T(2,128)(2,1)S(1)}, u32[]{:S(2)}, u32[]{:S(2)}) async-start(bf16[4,2,98304]{2,1,0:T(2,128)(2,1)} %reshape.127), calls=%async_computation.2 | async-start | bytes 3145728 | tf_op jit(solution)/shard_map/all_to_all | solution.py:60
  106.9 7.9 %reshape.126 = bf16[4096,6,32]{2,1,0:T(8,128)(2,1)} reshape(bf16[4,2,98304]{2,1,0:T(2,128)(2,1)} %copy-done.1) | data formatting | bytes 3145728
  114.8 9.1 %copy.70 = bf16[6,32,4,1024]{3,2,1,0:T(4,128)(2,1)} copy(bf16[6,32,4,1024]{1,0,3,2:T(8,128)(2,1)} %bitcast.81) | data formatting | bytes 3145728 | tf_op jit(solution)/shard_map/all_to_all | solution.py:58
  123.9 1.9 copy.53
  125.8 1.6 copy.77
  127.4 7.9 %reshape.124 = bf16[4096,6,32]{2,1,0:T(8,128)(2,1)} reshape(bf16[4,2,98304]{2,1,0:T(2,128)(2,1)} %all-to-all-done.1) | data formatting | bytes 3145728
  135.3 9.1 %copy.71 = bf16[6,32,4,1024]{3,2,1,0:T(4,128)(2,1)} copy(bf16[6,32,4,1024]{1,0,3,2:T(8,128)(2,1)} %bitcast.82) | data formatting | bytes 3145728 | tf_op jit(solution)/shard_map/all_to_all | solution.py:59
  144.4 1.9 copy.56
  146.8 1.0 copy-done.2
  147.7 1.2 fusion.5
  148.9 2.5 %fusion.20 = (f32[6,8,128]{2,1,0:T(8,128)S(1)}, f32[6,8,128,128]{2,3,1,0:T(8,128)}) fusion(f32[6,8,128,128]{2,3,1,0:T(8,128)S(1)} %fusion.5), kind=kOutput, calls=%fused_computation.31 | output fusion | flops 3145855 | bytes 6316032 | tf_op jit(solution)/shard_map/sub | solution.py:38
  151.4 6.9 %reshape.128 = bf16[4096,6,32]{2,1,0:T(8,128)(2,1)} reshape(bf16[4,2,98304]{2,1,0:T(2,128)(2,1)S(1)} %all-to-all-done.2) | data formatting | bytes 3145728
  158.4 8.4 %copy.72 = bf16[6,32,4,1024]{3,2,1,0:T(4,128)(2,1)S(1)} copy(bf16[6,32,4,1024]{1,0,3,2:T(8,128)(2,1)} %bitcast.83) | data formatting | bytes 3145728 | tf_op jit(solution)/shard_map/all_to_all | solution.py:60
  167.8 1.4 copy-done.3
  169.9 3.0 %copy.64 = bf16[6,128,1024]{2,0,1:T(8,128)(2,1)} copy(bf16[6,128,1024]{1,2,0:T(8,128)(2,1)S(1)} %bitcast.99) | data formatting | bytes 3145728 | tf_op jit(solution)/shard_map/reshape | solution.py:44
  172.9 5.0 %all-to-all-start.3 = ((bf16[6,128,1024]{2,0,1:T(8,128)(2,1)}), bf16[6,128,1024]{2,0,1:T(8,128)(2,1)S(1)}, u32[]{:S(2)}, u32[]{:S(2)}) async-start(bf16[6,128,1024]{2,0,1:T(8,128)(2,1)} %copy.64), calls=%async_computation.3 | async-start | bytes 4194304 | tf_op jit(solution)/shard_map/all_to_all | solution.py:63
  177.9 1.3 collective-permute-start
  180.0 45.0 %all-to-all-done.3 = bf16[6,128,1024]{2,0,1:T(8,128)(2,1)S(1)} async-done(((bf16[6,128,1024]{2,0,1:T(8,128)(2,1)}), bf16[6,128,1024]{2,0,1:T(8,128)(2,1)S(1)}, u32[]{:S(2)}, u32[]{:S(2)}) %all-to-all-start.3) | async-done | bytes 1572896 | tf_op jit(solution)/shard_map/all_to_all | solution.py:63
  225.0 2.4 %copy.66 = bf16[6,32,4,1024]{3,2,1,0:T(4,128)(2,1)} copy(bf16[6,32,4,1024]{3,0,1,2:T(8,128)(2,1)S(1)} %bitcast.87) | data formatting | bytes 3145728 | tf_op jit(solution)/shard_map/all_to_all | solution.py:63
  227.4 2.8 %all_to_all.58 = bf16[6,32,4096]{2,1,0:T(8,128)(2,1)S(1)} reshape(bf16[6,32,4,1024]{3,2,1,0:T(4,128)(2,1)} %copy.66) | data formatting | bytes 3145728 | tf_op jit(solution)/shard_map/all_to_all | solution.py:63
  231.1 1.3 collective-permute-start.1
  (26 shorter events, 5.2 us)
Async XLA Ops:
  0.6 229.6 %copy-start = (bf16[1,64,4096]{2,1,0:T(8,128)(2,1)S(1)}, bf16[1,64,4096]{2,1,0:T(8,128)(2,1)}, u32[]{:S(2)}) copy-start(bf16[1,64,4096]{2,1,0:T(8,128)(2,1)} %param.11) | copy-start | bytes 1572868
  17.9 43.3 %all-to-all-start = ((bf16[4,2,98304]{2,1,0:T(2,128)(2,1)}), bf16[4,2,98304]{2,1,0:T(2,128)(2,1)S(1)}, u32[]{:S(2)}, u32[]{:S(2)}) async-start(bf16[4,2,98304]{2,1,0:T(2,128)(2,1)} %reshape.125), calls=%async_computation | async-start | bytes 3145728 | tf_op jit(solution)/shard_map/all_to_all | solution.py:58
  61.1 1.2 copy-start.1
  62.3 40.9 %all-to-all-start.1 = ((bf16[4,2,98304]{2,1,0:T(2,128)(2,1)}), bf16[4,2,98304]{2,1,0:T(2,128)(2,1)}, u32[]{:S(2)}, u32[]{:S(2)}) async-start(bf16[4,2,98304]{2,1,0:T(2,128)(2,1)} %reshape.123), calls=%async_computation.1 | async-start | bytes 3145728 | tf_op jit(solution)/shard_map/all_to_all | solution.py:59
  103.2 48.2 %all-to-all-start.2 = ((bf16[4,2,98304]{2,1,0:T(2,128)(2,1)}), bf16[4,2,98304]{2,1,0:T(2,128)(2,1)S(1)}, u32[]{:S(2)}, u32[]{:S(2)}) async-start(bf16[4,2,98304]{2,1,0:T(2,128)(2,1)} %reshape.127), calls=%async_computation.2 | async-start | bytes 3145728 | tf_op jit(solution)/shard_map/all_to_all | solution.py:60
  146.3 1.4 copy-start.2
  167.3 1.9 copy-start.3
  172.9 5.0 %copy-start.5 = (s32[1,3]{1,0:T(1,128)S(1)}, s32[1,3]{1,0:T(1,128)}, u32[]{:S(2)}) copy-start(s32[1,3]{1,0:T(1,128)} %param.12) | copy-start | bytes 40
  172.9 6.3 %copy-start.6 = (s32[3]{0:T(128)S(1)}, s32[3]{0:T(128)}, u32[]{:S(2)}) copy-start(s32[3]{0:T(128)} %param.13) | copy-start | bytes 40
  172.9 52.1 %all-to-all-start.3 = ((bf16[6,128,1024]{2,0,1:T(8,128)(2,1)}), bf16[6,128,1024]{2,0,1:T(8,128)(2,1)S(1)}, u32[]{:S(2)}, u32[]{:S(2)}) async-start(bf16[6,128,1024]{2,0,1:T(8,128)(2,1)} %copy.64), calls=%async_computation.3 | async-start | bytes 4194304 | tf_op jit(solution)/shard_map/all_to_all | solution.py:63
  177.9 2.1 collective-permute-start
  230.3 0.7 copy-start.4
  231.1 2.1 collective-permute-start.1
where the time goes:
time: 236 us; the launch traced here: 234 us
  local copies, waits for them, and re-layouts  120 us (51%)
  waiting for transfers between devices  85.1 us (36%)
  starting transfers between devices  22 us (9%)
  other arithmetic  3.95 us (2%)
  matrix products  2.45 us (1%)
    unnamed x23, local copies, waits for them, and re-layouts  55 us
    all_to_all x1, waiting for transfers between devices, on_device(): lax.all_to_all(attended, 'sp', split_axis=1, concat_axis=2, tiled=True)  45 us
    all_to_all x1, waiting for transfers between devices, on_device(): lax.all_to_all(query_local, 'sp', split_axis=2, concat_axis=1, tiled=True)  19.8 us
    all_to_all x1, waiting for transfers between devices, on_device(): lax.all_to_all(key_local, 'sp', split_axis=2, concat_axis=1, tiled=True)  19.4 us
    all_to_all x2, local copies, waits for them, and re-layouts, on_device(): lax.all_to_all(key_local, 'sp', split_axis=2, concat_axis=1, tiled=True)  11 us
    all_to_all x2, local copies, waits for them, and re-layouts, on_device(): lax.all_to_all(query_local, 'sp', split_axis=2, concat_axis=1, tiled=True)  11 us
    all_to_all x2, local copies, waits for them, and re-layouts, on_device(): lax.all_to_all(value_local, 'sp', split_axis=2, concat_axis=1, tiled=True)  8.94 us
    another operation x1, local copies, waits for them, and re-layouts, on_device(): query_local = queries[0].reshape(items, token_rows, feature_all)  8.47 us
  transfers between devices with their start and end apart: 6, of which 5 were waited for; matrix products, arithmetic and copies ran while one was open for 34% of the time, Pallas kernels for 0%

commit v1 on v0

v1 whole, which is shorter than its diff:
```python
import functools

import jax
import jax.numpy as jnp
from jax import lax
from jax.experimental import pallas as pl
from jax.experimental.pallas import tpu as pltpu
from jax.sharding import PartitionSpec as P

HD = 128
CH = 64
STEPS = 40
SWITCH = 25


noise_shift = 12.0
high_guidance = 4.0
low_guidance = 3.0

VMEM = pl.BlockSpec(memory_space=pltpu.VMEM)
SMEM = pl.BlockSpec(memory_space=pltpu.SMEM)


def noise_level(step_now):
    fraction = 1.0 - step_now.astype(jnp.float32) / STEPS
    return noise_shift * fraction / (1.0 + (noise_shift - 1.0) * fraction)


def lanes(index, width):
    return pl.ds(pl.multiple_of(index * width, width), width)


def pack_kernel(count, width, me_ref, q_ref, k_ref, *out_refs):
    me = me_ref[0]
    for s in range(1, count):
        there = lanes(me ^ s, width)
        out_refs[s - 1][:, :, 0:width] = q_ref[:, :, there]
        out_refs[s - 1][:, :, width : 2 * width] = k_ref[:, :, there]


def project_kernel(count, width, me_ref, v_ref, w_ref, *out_refs):
    me = me_ref[0]
    items, rows, _ = v_ref.shape
    pair = 2 * HD
    for s in range(count):
        for p in range(width // pair):
            start = pl.multiple_of((me ^ s) * width + p * pair, pair)
            there = pl.ds(start, pair)
            weight = w_ref[:, there]
            column = lax.broadcasted_iota(jnp.int32, weight.shape, 1)
            zero = jnp.zeros_like(weight)
            stacked = jnp.concatenate(
                [jnp.where(column < HD, weight, zero), jnp.where(column < HD, zero, weight)],
                axis=0,
            )
            value = v_ref[:, :, there].reshape(items * rows, pair)
            product = lax.dot_general(
                value, stacked, (((1,), (1,)), ((), ())), preferred_element_type=jnp.float32
            )
            out_refs[s][:, :, p * 2 * CH : (p + 1) * 2 * CH] = product.astype(
                jnp.bfloat16
            ).reshape(items, rows, 2 * CH)


def score_kernel(count, width, me_ref, q_ref, k_ref, *refs):
    others, out_ref = refs[:-1], refs[-1]
    me = me_ref[0]
    items = q_ref.shape[0]

    def one(i, carry):
        for h in range(width // HD):
            own = pl.ds(pl.multiple_of(me * width + h * HD, HD), HD)
            query = jnp.concatenate(
                [q_ref[i, :, own]] + [r[i, :, h * HD : (h + 1) * HD] for r in others], axis=0
            )
            key = jnp.concatenate(
                [k_ref[i, :, own]]
                + [r[i, :, width + h * HD : width + (h + 1) * HD] for r in others],
                axis=0,
            )
            scores = lax.dot_general(
                query, key, (((1,), (1,)), ((), ())), preferred_element_type=jnp.float32
            ) * (HD ** (-0.5))
            length = scores.shape[1]
            row_max = jnp.max(scores, axis=1, keepdims=True)
            out_ref[i, :, h * length : (h + 1) * length] = jnp.exp(scores - row_max).astype(
                jnp.bfloat16
            )
        return carry

    lax.fori_loop(0, items, one, 0)


def attend_kernel(count, width, scale_ref, skip_ref, e_ref, *refs):
    vw_refs, out_ref, scratch = refs[:count], refs[count], refs[count + 1]
    videos = out_ref.shape[1]
    rows = vw_refs[0].shape[1]
    length = rows * count
    ones = jnp.ones((length, 2 * CH), jnp.bfloat16)

    def one(v, carry):
        sums = []
        for way in range(2):
            i = 2 * v + way
            halves = [None, None]
            for h in range(width // HD):
                p = h // 2
                value = jnp.concatenate(
                    [r[i, :, p * 2 * CH : (p + 1) * 2 * CH] for r in vw_refs], axis=0
                )
                mixed = jnp.dot(
                    e_ref[i, :, h * length : (h + 1) * length],
                    jnp.concatenate([value, ones], axis=1),
                    preferred_element_type=jnp.float32,
                )
                term = mixed[:, : 2 * CH] / mixed[:, 2 * CH :]
                halves[h % 2] = term if halves[h % 2] is None else halves[h % 2] + term
            sums.append(halves[0] + pltpu.roll(halves[1], CH, 1))
        conditional, unconditional = sums
        guided = unconditional + scale_ref[0] * (conditional - unconditional)
        guided = jnp.where(skip_ref[v] == 1, conditional, guided)
        scratch[...] = guided
        even = scratch[pl.ds(0, length // 2, stride=2), :]
        odd = scratch[pl.ds(1, length // 2, stride=2), :]
        column = lax.broadcasted_iota(jnp.int32, even.shape, 1)
        both = jnp.where(column < CH, even, pltpu.roll(odd, CH, 1))
        for s in range(count):
            out_ref[s, v] = both[s * rows // 2 : (s + 1) * rows // 2]
        return carry

    lax.fori_loop(0, videos, one, 0)


def call(kernel, outs, specs, name, scratch=(), flops=0, moved=0):
    return pl.pallas_call(
        kernel,
        out_shape=outs,
        in_specs=specs,
        out_specs=jax.tree.map(lambda _: VMEM, outs),
        scratch_shapes=scratch,
        name=name,
        compiler_params=pltpu.CompilerParams(vmem_limit_bytes=12 << 20),
        cost_estimate=pl.CostEstimate(flops=flops, bytes_accessed=moved, transcendentals=0),
    )


def on_device(count, latent, queries, keys, values, head_weight, step_index, skip_flags):
    section_index = lax.axis_index("section")
    me = lax.axis_index("sp")[None]
    _, videos, _, rows, feature_all = queries.shape
    items = videos * 2
    width = feature_all // count
    heads = width // HD
    length = rows * count
    query = queries[0].reshape(items, rows, feature_all)
    key = keys[0].reshape(items, rows, feature_all)
    value = values[0].reshape(items, rows, feature_all)

    def exchange(array, s):
        return lax.ppermute(array, "sp", [(i, i ^ s) for i in range(count)])

    pack = call(
        functools.partial(pack_kernel, count, width),
        [jax.ShapeDtypeStruct((items, rows, 2 * width), jnp.bfloat16)] * (count - 1),
        [SMEM, VMEM, VMEM],
        "pack",
        moved=8 * items * rows * feature_all,
    )
    packed = pack(me, query, key)
    arrived = [exchange(packed[s - 1], s) for s in range(1, count)]

    project = call(
        functools.partial(project_kernel, count, width),
        [jax.ShapeDtypeStruct((items, rows, heads * CH), jnp.bfloat16)] * count,
        [SMEM, VMEM, VMEM],
        "project",
        flops=8 * items * rows * feature_all * CH,
        moved=3 * items * rows * feature_all,
    )
    projected = project(me, value, head_weight[0])
    projected = [projected[0]] + [exchange(projected[s], s) for s in range(1, count)]

    score = call(
        functools.partial(score_kernel, count, width),
        jax.ShapeDtypeStruct((items, length, heads * length), jnp.bfloat16),
        [SMEM] + [VMEM] * (count + 1),
        "score",
        flops=2 * items * heads * length * length * HD * 4,
        moved=8 * items * rows * feature_all,
    )
    weights = score(me, query, key, *arrived)

    guidance = jnp.where(section_index == 0, jnp.float32(high_guidance), jnp.float32(low_guidance))
    skipping = jnp.where(section_index == 1, skip_flags, 0)
    attend = call(
        functools.partial(attend_kernel, count, width),
        jax.ShapeDtypeStruct((count, videos, rows // 2, 2 * CH), jnp.float32),
        [SMEM, SMEM] + [VMEM] * (count + 1),
        "attend",
        scratch=[pltpu.VMEM((length, 2 * CH), jnp.float32)],
        flops=2 * items * heads * length * length * HD * 4,
        moved=4 * items * rows * feature_all,
    )
    shares = attend(guidance[None], skipping, weights, *projected)
    guided = shares[0]
    for s in range(1, count):
        guided = guided + exchange(shares[s], s)

    step_now = step_index[0]
    step_size = noise_level(step_now + 1) - noise_level(step_now)
    updated = latent[0] + step_size[:, None, None] * guided
    finish_mark = jnp.where(
        (section_index == 0) & (step_now + 1 == SWITCH), jnp.float32(1.0), jnp.float32(0.0)
    )
    arrived_mark = lax.ppermute(finish_mark, "section", [(0, 1)])
    arrived = lax.ppermute(updated, "section", [(0, 1)])
    taking = (section_index == 1) & (arrived_mark > 0.5)
    next_latent = jnp.where(taking[:, None, None], arrived, updated)
    return (guided[None], next_latent[None])


def solution(mesh):
    placed = (
        P("section", ("groups", "blk"), "sp", None),
        P("section", ("groups", "blk"), None, "sp", None),
        P("section", ("groups", "blk"), None, "sp", None),
        P("section", ("groups", "blk"), None, "sp", None),
        P("section", None, None),
        P("section", ("groups", "blk")),
        P(("groups", "blk")),
    )
    return jax.shard_map(
        functools.partial(on_device, mesh.shape["sp"]),
        mesh=mesh,
        in_specs=placed,
        out_specs=(
            P("section", ("groups", "blk"), "sp", None),
            P("section", ("groups", "blk"), "sp", None),
        ),
        check_vma=False,
    )
```

time: 236 us -> 109 us (0.46)
  local copies, waits for them, and re-layouts: 120 us -> 4.56 us
  waiting for transfers between devices: 85.1 us -> 70 us
  Pallas kernels: 0 us -> 9.51 us
  other arithmetic: 3.95 us -> 1.32 us
  matrix products: 2.45 us -> 0 us
    all_to_all x4 -> x0, waiting for transfers between devices: 84.2 us -> none  [the longest x1 45 us: on_device(): lax.all_to_all(attended, 'sp', split_axis=1, concat_axis=2, tiled=True)]
    ppermute x2 -> x11, waiting for transfers between devices: 0.92 us -> 70 us  [the longest x9 69.2 us: exchange(): return lax.ppermute(array, 'sp', [(i, i ^ s) for i in range(count)])]
    unnamed x23 -> x20, local copies, waits for them, and re-layouts: 55 us -> 4.55 us
    all_to_all x8 -> x0, local copies, waits for them, and re-layouts: 36.2 us -> none  [the longest x2 11 us: on_device(): lax.all_to_all(key_local, 'sp', split_axis=2, concat_axis=1, tiled=True)]
    another operation x4 -> x0, local copies, waits for them, and re-layouts: 25.4 us -> none  [the longest x1 8.47 us: on_device(): query_local = queries[0].reshape(items, token_rows, feature_all)]
    ppermute x2 -> x11, starting transfers between devices: 2.57 us -> 22.9 us  [the longest x9 20.4 us: exchange(): return lax.ppermute(array, 'sp', [(i, i ^ s) for i in range(count)])]
    all_to_all x4 -> x0, starting transfers between devices: 19.4 us -> none  [the longest x1 6.32 us: on_device(): lax.all_to_all(query_local, 'sp', split_axis=2, concat_axis=1, tiled=True)]
    pallas_call x0 -> x4, Pallas kernels: none -> 9.51 us  [the longest x1 4.11 us: on_device(): weights = score(me, query, key, *arrived)]
  transfers between devices with their start and end apart: 6 -> 11, of which waited for: 5 -> 6; matrix products, arithmetic and copies ran while one was open for 34% -> 1% of each run, Pallas kernels for 0% -> 5%
where the time goes in v1:
time: 109 us
  waiting for transfers between devices  70 us (64%)
  starting transfers between devices  22.9 us (21%)
  Pallas kernels  9.51 us (9%)
  local copies, waits for them, and re-layouts  4.56 us (4%)
  other arithmetic  1.32 us (1%)
    ppermute x9, waiting for transfers between devices, exchange(): return lax.ppermute(array, 'sp', [(i, i ^ s) for i in range(count)])  69.2 us
    ppermute x9, starting transfers between devices, exchange(): return lax.ppermute(array, 'sp', [(i, i ^ s) for i in range(count)])  20.4 us
    unnamed x20, local copies, waits for them, and re-layouts  4.55 us
    pallas_call x1, Pallas kernels, on_device(): weights = score(me, query, key, *arrived)  4.11 us
    pallas_call x1, Pallas kernels, on_device(): shares = attend(guidance[None], skipping, weights, *projected)  2.68 us
  transfers between devices with their start and end apart: 11, of which 6 were waited for; matrix products, arithmetic and copies ran while one was open for 1% of the time, Pallas kernels for 5%

profile of v1, /device:TPU:0, one launch (start us, length us, event | category | flops | bytes accessed | tf_op | source)
XLA Modules:
  0.0 109.1 jit_solution(16889263515060881246)
XLA Ops:
  0.6 0.0 copy-start
  0.6 1.4 %copy-done = bf16[1,3,2,32,4096]{4,3,2,1,0:T(8,128)(2,1)S(1)} copy-done((bf16[1,3,2,32,4096]{4,3,2,1,0:T(8,128)(2,1)S(1)}, bf16[1,3,2,32,4096]{4,3,2,1,0:T(8,128)(2,1)}, u32[]{:S(2)}) %copy-start) | copy-done | bytes 1572888
  2.0 1.4 %copy-done.2 = bf16[1,3,2,32,4096]{4,3,2,1,0:T(8,128)(2,1)S(1)} copy-done((bf16[1,3,2,32,4096]{4,3,2,1,0:T(8,128)(2,1)S(1)}, bf16[1,3,2,32,4096]{4,3,2,1,0:T(8,128)(2,1)}, u32[]{:S(2)}) %copy-start.2) | copy-done | bytes 1572888
  3.5 1.5 %pack.1 = (bf16[6,32,2048]{2,1,0:T(8,128)(2,1)}, bf16[6,32,2048]{2,1,0:T(8,128)(2,1)}, bf16[6,32,2048]{2,1,0:T(8,128)(2,1)}) custom-call(s32[1]{0:T(128)} %bitcast.1.me_ref, bf16[6,32,4096]{2,1,0:T(8,128)(2,1)S(1)} %bitcast.30, bf16[6,32,4096]{2,1,0:T(8,128)(2,1)S(1)} %bitcast.32), custom_call_target="tpu_custom_call" | custom-call | bytes 6291456 | tf_op jit(solution)/shard_map/pack/pallas_call | solution.py:169
  5.0 3.0 %collective-permute-start = (bf16[6,32,2048]{2,1,0:T(8,128)(2,1)}, bf16[6,32,2048]{2,1,0:T(8,128)(2,1)}, u32[]{:S(2)}, u32[]{:S(2)}) collective-permute-start(bf16[6,32,2048]{2,1,0:T(8,128)(2,1)} %get-tuple-element.9), channel_id=1, source_target_pairs={{0,2},{2,0},{4,6},{6,4},{1,3},{3,1},{5,7},{7,5},{8,10},{10,8},{12,... | collective-permute-start | bytes 2359304 | tf_op jit(solution)/shard_map/ppermute | solution.py:160
  8.0 2.6 %collective-permute-start.1 = (bf16[6,32,2048]{2,1,0:T(8,128)(2,1)}, bf16[6,32,2048]{2,1,0:T(8,128)(2,1)}, u32[]{:S(2)}, u32[]{:S(2)}) collective-permute-start(bf16[6,32,2048]{2,1,0:T(8,128)(2,1)} %get-tuple-element.10), channel_id=1, source_target_pairs={{0,4},{2,6},{4,0},{6,2},{1,5},{3,7},{5,1},{7,3},{8,12},{10,14},{12... | collective-permute-start | bytes 2359304 | tf_op jit(solution)/shard_map/ppermute | solution.py:160
  10.6 0.0 collective-permute-start.2
  10.6 1.0 copy-done.5
  11.7 1.2 %project.1 = (bf16[6,32,512]{2,1,0:T(8,128)(2,1)S(1)}, bf16[6,32,512]{2,1,0:T(8,128)(2,1)}, bf16[6,32,512]{2,1,0:T(8,128)(2,1)}, bf16[6,32,512]{2,1,0:T(8,128)(2,1)S(1)}) custom-call(s32[1]{0:T(128)} %bitcast.1.me_ref, bf16[6,32,4096]{2,1,0:T(8,128)(2,1)S(1)} %bitcast.34, bf16[64,4096]{1,0:T(8,128)(2,1)S(1)} %bitcast.35), custom_call_target="tpu_custom_call" | custom-call | flops 402653184 | bytes 2359296 | tf_op jit(solution)/shard_map/project/pallas_call | solution.py:180
  12.8 0.7 copy-done.6
  13.5 0.9 collective-permute-start.3
  14.4 3.5 %collective-permute-start.4 = (bf16[6,32,512]{2,1,0:T(8,128)(2,1)}, bf16[6,32,512]{2,1,0:T(8,128)(2,1)}, u32[]{:S(2)}, u32[]{:S(2)}) collective-permute-start(bf16[6,32,512]{2,1,0:T(8,128)(2,1)} %get-tuple-element.14), channel_id=1, source_target_pairs={{0,4},{2,6},{4,0},{6,2},{1,5},{3,7},{5,1},{7,3},{8,12},{10,14},{12... | collective-permute-start | bytes 589832 | tf_op jit(solution)/shard_map/ppermute | solution.py:160
  17.9 24.9 %collective-permute-done.refs_0_ = bf16[6,32,2048]{2,1,0:T(8,128)(2,1)} collective-permute-done((bf16[6,32,2048]{2,1,0:T(8,128)(2,1)}, bf16[6,32,2048]{2,1,0:T(8,128)(2,1)}, u32[]{:S(2)}, u32[]{:S(2)}) %collective-permute-start) | collective-permute-done | bytes 786464 | tf_op jit(solution)/shard_map/ppermute | solution.py:160
  42.8 4.6 %collective-permute-start.5 = (bf16[6,32,512]{2,1,0:T(8,128)(2,1)}, bf16[6,32,512]{2,1,0:T(8,128)(2,1)S(1)}, u32[]{:S(2)}, u32[]{:S(2)}) collective-permute-start(bf16[6,32,512]{2,1,0:T(8,128)(2,1)} %copy-done.6), channel_id=1, source_target_pairs={{0,6},{2,4},{4,2},{6,0},{1,7},{3,5},{5,3},{7,1},{8,14},{10,12},{12... | collective-permute-start | bytes 589832 | tf_op jit(solution)/shard_map/ppermute | solution.py:160
  47.4 16.1 %collective-permute-done.1.refs_1_ = bf16[6,32,2048]{2,1,0:T(8,128)(2,1)} collective-permute-done((bf16[6,32,2048]{2,1,0:T(8,128)(2,1)}, bf16[6,32,2048]{2,1,0:T(8,128)(2,1)}, u32[]{:S(2)}, u32[]{:S(2)}) %collective-permute-start.1) | collective-permute-done | bytes 786464 | tf_op jit(solution)/shard_map/ppermute | solution.py:160
  63.5 0.0 collective-permute-done.2.refs_2_
  63.5 4.1 %score.1.e_ref = bf16[6,128,1024]{2,1,0:T(8,128)(2,1)S(1)} custom-call(s32[1]{0:T(128)} %bitcast.1.me_ref, bf16[6,32,4096]{2,1,0:T(8,128)(2,1)S(1)} %bitcast.31, bf16[6,32,4096]{2,1,0:T(8,128)(2,1)S(1)} %bitcast.33, bf16[6,32,2048]{2,1,0:T(8,128)(2,1)} %collective-permute-done.refs_0_, bf16[6,32,2048]{2,1,0:T(8,128)(2,1)} %collective-permute-done.1.refs_1_, ...), custom_call_target="tpu_custom_call" | custom-call | flops 805306368 | bytes 6291456 | tf_op jit(solution)/shard_map/score/pallas_call | solution.py:191
  67.6 0.0 copy-start.8
  67.6 0.0 copy-start.7
  67.6 0.0 collective-permute-done.3.refs_1_
  67.6 25.3 %collective-permute-done.4.refs_2_ = bf16[6,32,512]{2,1,0:T(8,128)(2,1)} collective-permute-done((bf16[6,32,512]{2,1,0:T(8,128)(2,1)}, bf16[6,32,512]{2,1,0:T(8,128)(2,1)}, u32[]{:S(2)}, u32[]{:S(2)}) %collective-permute-start.4) | collective-permute-done | bytes 196640 | tf_op jit(solution)/shard_map/ppermute | solution.py:160
  93.0 2.7 %attend.1 = f32[4,3,16,128]{3,2,1,0:T(8,128)S(1)} custom-call(f32[1]{0:T(128)} %bitcast.scale_ref, s32[3]{0:T(128)S(1)} %broadcast_select_fusion.skip_ref, bf16[6,128,1024]{2,1,0:T(8,128)(2,1)S(1)} %score.1.e_ref, bf16[6,32,512]{2,1,0:T(8,128)(2,1)S(1)} %get-tuple-element.12.refs_0_, bf16[6,32,512]{2,1,0:T(8,128)(2,1)S(1)} %collective-permute-done.3.refs_1_, ...), custom_call_target="tpu_custom_call" | custom-call | flops 805306368 | bytes 3145728 | tf_op jit(solution)/shard_map/attend/pallas_call | solution.py:204
  95.7 3.3 %collective-permute-start.6 = (f32[3,16,128]{2,1,0:T(8,128)S(1)}, f32[3,16,128]{2,1,0:T(8,128)S(1)}, u32[]{:S(2)}, u32[]{:S(2)}) collective-permute-start(f32[3,16,128]{2,1,0:T(8,128)S(1)} %get-tuple-element.18), channel_id=1, source_target_pairs={{0,2},{2,0},{4,6},{6,4},{1,3},{3,1},{5,7},{7,5},{8,10},{10,8},{12,... | collective-permute-start | bytes 73736 | tf_op jit(solution)/shard_map/ppermute | solution.py:160
  99.0 1.1 %collective-permute-start.7 = (f32[3,16,128]{2,1,0:T(8,128)S(1)}, f32[3,16,128]{2,1,0:T(8,128)S(1)}, u32[]{:S(2)}, u32[]{:S(2)}) collective-permute-start(f32[3,16,128]{2,1,0:T(8,128)S(1)} %get-tuple-element.20), channel_id=1, source_target_pairs={{0,4},{2,6},{4,0},{6,2},{1,5},{3,7},{5,1},{7,3},{8,12},{10,14},{12... | collective-permute-start | bytes 73736 | tf_op jit(solution)/shard_map/ppermute | solution.py:160
  100.1 1.4 %collective-permute-start.8 = (f32[3,16,128]{2,1,0:T(8,128)S(1)}, f32[3,16,128]{2,1,0:T(8,128)S(1)}, u32[]{:S(2)}, u32[]{:S(2)}) collective-permute-start(f32[3,16,128]{2,1,0:T(8,128)S(1)} %get-tuple-element.19), channel_id=1, source_target_pairs={{0,6},{2,4},{4,2},{6,0},{1,7},{3,5},{5,3},{7,1},{8,14},{10,12},{12... | collective-permute-start | bytes 73736 | tf_op jit(solution)/shard_map/ppermute | solution.py:160
  101.5 1.3 %collective-permute-start.9 = (f32[3]{0:T(128)S(1)}, f32[3]{0:T(128)S(1)}, u32[]{:S(2)}, u32[]{:S(2)}) collective-permute-start(f32[3]{0:T(128)S(1)} %get-tuple-element.21), channel_id=1, source_target_pairs={{0,8},{1,9},{2,10},{3,11},{4,12},{5,13},{6,14},{7,15},{16,24},{17,... | collective-permute-start | bytes 44 | tf_op jit(solution)/shard_map/ppermute | solution.py:215
  102.8 1.1 %collective-permute-done.7 = f32[3,16,128]{2,1,0:T(8,128)S(1)} collective-permute-done((f32[3,16,128]{2,1,0:T(8,128)S(1)}, f32[3,16,128]{2,1,0:T(8,128)S(1)}, u32[]{:S(2)}, u32[]{:S(2)}) %collective-permute-start.7) | collective-permute-done | bytes 24608 | tf_op jit(solution)/shard_map/ppermute | solution.py:160
  103.9 1.8 %collective-permute-done.8 = f32[3,16,128]{2,1,0:T(8,128)S(1)} collective-permute-done((f32[3,16,128]{2,1,0:T(8,128)S(1)}, f32[3,16,128]{2,1,0:T(8,128)S(1)}, u32[]{:S(2)}, u32[]{:S(2)}) %collective-permute-start.8) | collective-permute-done | bytes 24608 | tf_op jit(solution)/shard_map/ppermute | solution.py:160
  105.7 0.6 bitcast_add_fusion
  106.3 1.3 %collective-permute-start.10 = (f32[3,16,128]{2,1,0:T(8,128)S(1)}, f32[3,16,128]{2,1,0:T(8,128)S(1)}, u32[]{:S(2)}, u32[]{:S(2)}) collective-permute-start(f32[3,16,128]{2,1,0:T(8,128)S(1)} %get-tuple-element.16), channel_id=1, source_target_pairs={{0,8},{1,9},{2,10},{3,11},{4,12},{5,13},{6,14},{7,15},{16,24},{17,... | collective-permute-start | bytes 73736 | tf_op jit(solution)/shard_map/ppermute | solution.py:216
  107.6 0.8 collective-permute-done.10
  108.4 0.7 select_bitcast_fusion
  (20 shorter events, 0.1 us)
Async XLA Ops:
  0.6 1.4 %copy-start = (bf16[1,3,2,32,4096]{4,3,2,1,0:T(8,128)(2,1)S(1)}, bf16[1,3,2,32,4096]{4,3,2,1,0:T(8,128)(2,1)}, u32[]{:S(2)}) copy-start(bf16[1,3,2,32,4096]{4,3,2,1,0:T(8,128)(2,1)} %param.8) | copy-start | bytes 4718596
  2.0 1.4 %copy-start.2 = (bf16[1,3,2,32,4096]{4,3,2,1,0:T(8,128)(2,1)S(1)}, bf16[1,3,2,32,4096]{4,3,2,1,0:T(8,128)(2,1)}, u32[]{:S(2)}) copy-start(bf16[1,3,2,32,4096]{4,3,2,1,0:T(8,128)(2,1)} %param.9) | copy-start | bytes 4718596
  3.5 7.2 %copy-start.4 = (bf16[1,3,2,32,4096]{4,3,2,1,0:T(8,128)(2,1)S(1)}, bf16[1,3,2,32,4096]{4,3,2,1,0:T(8,128)(2,1)}, u32[]{:S(2)}) copy-start(bf16[1,3,2,32,4096]{4,3,2,1,0:T(8,128)(2,1)} %param.10) | copy-start | bytes 4718596
  3.5 43.9 %copy-start.9 = (s32[3]{0:T(128)S(1)}, s32[3]{0:T(128)}, u32[]{:S(2)}) copy-start(s32[3]{0:T(128)} %param.13) | copy-start | bytes 40
  3.5 60.0 %copy-start.3 = (bf16[1,3,2,32,4096]{4,3,2,1,0:T(8,128)(2,1)S(1)}, bf16[1,3,2,32,4096]{4,3,2,1,0:T(8,128)(2,1)}, u32[]{:S(2)}) copy-start(bf16[1,3,2,32,4096]{4,3,2,1,0:T(8,128)(2,1)} %param.9) | copy-start | bytes 4718596
  5.0 58.5 %copy-start.1 = (bf16[1,3,2,32,4096]{4,3,2,1,0:T(8,128)(2,1)S(1)}, bf16[1,3,2,32,4096]{4,3,2,1,0:T(8,128)(2,1)}, u32[]{:S(2)}) copy-start(bf16[1,3,2,32,4096]{4,3,2,1,0:T(8,128)(2,1)} %param.8) | copy-start | bytes 4718596
  5.0 37.8 %collective-permute-start = (bf16[6,32,2048]{2,1,0:T(8,128)(2,1)}, bf16[6,32,2048]{2,1,0:T(8,128)(2,1)}, u32[]{:S(2)}, u32[]{:S(2)}) collective-permute-start(bf16[6,32,2048]{2,1,0:T(8,128)(2,1)} %get-tuple-element.9), channel_id=1, source_target_pairs={{0,2},{2,0},{4,6},{6,4},{1,3},{3,1},{5,7},{7,5},{8,10},{10,8},{12,... | collective-permute-start | bytes 2359304 | tf_op jit(solution)/shard_map/ppermute | solution.py:160
  8.0 55.4 %collective-permute-start.1 = (bf16[6,32,2048]{2,1,0:T(8,128)(2,1)}, bf16[6,32,2048]{2,1,0:T(8,128)(2,1)}, u32[]{:S(2)}, u32[]{:S(2)}) collective-permute-start(bf16[6,32,2048]{2,1,0:T(8,128)(2,1)} %get-tuple-element.10), channel_id=1, source_target_pairs={{0,4},{2,6},{4,0},{6,2},{1,5},{3,7},{5,1},{7,3},{8,12},{10,14},{12... | collective-permute-start | bytes 2359304 | tf_op jit(solution)/shard_map/ppermute | solution.py:160
  10.6 52.8 %collective-permute-start.2 = (bf16[6,32,2048]{2,1,0:T(8,128)(2,1)}, bf16[6,32,2048]{2,1,0:T(8,128)(2,1)}, u32[]{:S(2)}, u32[]{:S(2)}) collective-permute-start(bf16[6,32,2048]{2,1,0:T(8,128)(2,1)} %get-tuple-element.11), channel_id=1, source_target_pairs={{0,6},{2,4},{4,2},{6,0},{1,7},{3,5},{5,3},{7,1},{8,14},{10,12},{12... | collective-permute-start | bytes 2359304 | tf_op jit(solution)/shard_map/ppermute | solution.py:160
  10.6 1.0 copy-start.5
  12.8 0.7 copy-start.6
  13.5 54.1 %collective-permute-start.3 = (bf16[6,32,512]{2,1,0:T(8,128)(2,1)}, bf16[6,32,512]{2,1,0:T(8,128)(2,1)S(1)}, u32[]{:S(2)}, u32[]{:S(2)}) collective-permute-start(bf16[6,32,512]{2,1,0:T(8,128)(2,1)} %get-tuple-element.13), channel_id=1, source_target_pairs={{0,2},{2,0},{4,6},{6,4},{1,3},{3,1},{5,7},{7,5},{8,10},{10,8},{12,... | collective-permute-start | bytes 589832 | tf_op jit(solution)/shard_map/ppermute | solution.py:160
  14.4 78.5 %collective-permute-start.4 = (bf16[6,32,512]{2,1,0:T(8,128)(2,1)}, bf16[6,32,512]{2,1,0:T(8,128)(2,1)}, u32[]{:S(2)}, u32[]{:S(2)}) collective-permute-start(bf16[6,32,512]{2,1,0:T(8,128)(2,1)} %get-tuple-element.14), channel_id=1, source_target_pairs={{0,4},{2,6},{4,0},{6,2},{1,5},{3,7},{5,1},{7,3},{8,12},{10,14},{12... | collective-permute-start | bytes 589832 | tf_op jit(solution)/shard_map/ppermute | solution.py:160
  42.8 50.2 %collective-permute-start.5 = (bf16[6,32,512]{2,1,0:T(8,128)(2,1)}, bf16[6,32,512]{2,1,0:T(8,128)(2,1)S(1)}, u32[]{:S(2)}, u32[]{:S(2)}) collective-permute-start(bf16[6,32,512]{2,1,0:T(8,128)(2,1)} %copy-done.6), channel_id=1, source_target_pairs={{0,6},{2,4},{4,2},{6,0},{1,7},{3,5},{5,3},{7,1},{8,14},{10,12},{12... | collective-permute-start | bytes 589832 | tf_op jit(solution)/shard_map/ppermute | solution.py:160
  67.6 33.9 %copy-start.8 = (s32[1,3]{1,0:T(1,128)S(1)}, s32[1,3]{1,0:T(1,128)}, u32[]{:S(2)}) copy-start(s32[1,3]{1,0:T(1,128)} %param.12) | copy-start | bytes 40
  67.6 38.1 %copy-start.7 = (f32[1,3,16,128]{3,2,1,0:T(8,128)S(1)}, f32[1,3,16,128]{3,2,1,0:T(8,128)}, u32[]{:S(2)}) copy-start(f32[1,3,16,128]{3,2,1,0:T(8,128)} %param.7) | copy-start | bytes 73732
  95.7 7.1 %collective-permute-start.6 = (f32[3,16,128]{2,1,0:T(8,128)S(1)}, f32[3,16,128]{2,1,0:T(8,128)S(1)}, u32[]{:S(2)}, u32[]{:S(2)}) collective-permute-start(f32[3,16,128]{2,1,0:T(8,128)S(1)} %get-tuple-element.18), channel_id=1, source_target_pairs={{0,2},{2,0},{4,6},{6,4},{1,3},{3,1},{5,7},{7,5},{8,10},{10,8},{12,... | collective-permute-start | bytes 73736 | tf_op jit(solution)/shard_map/ppermute | solution.py:160
  99.0 5.0 %collective-permute-start.7 = (f32[3,16,128]{2,1,0:T(8,128)S(1)}, f32[3,16,128]{2,1,0:T(8,128)S(1)}, u32[]{:S(2)}, u32[]{:S(2)}) collective-permute-start(f32[3,16,128]{2,1,0:T(8,128)S(1)} %get-tuple-element.20), channel_id=1, source_target_pairs={{0,4},{2,6},{4,0},{6,2},{1,5},{3,7},{5,1},{7,3},{8,12},{10,14},{12... | collective-permute-start | bytes 73736 | tf_op jit(solution)/shard_map/ppermute | solution.py:160
  100.1 5.6 %collective-permute-start.8 = (f32[3,16,128]{2,1,0:T(8,128)S(1)}, f32[3,16,128]{2,1,0:T(8,128)S(1)}, u32[]{:S(2)}, u32[]{:S(2)}) collective-permute-start(f32[3,16,128]{2,1,0:T(8,128)S(1)} %get-tuple-element.19), channel_id=1, source_target_pairs={{0,6},{2,4},{4,2},{6,0},{1,7},{3,5},{5,3},{7,1},{8,14},{10,12},{12... | collective-permute-start | bytes 73736 | tf_op jit(solution)/shard_map/ppermute | solution.py:160
  101.5 6.1 %collective-permute-start.9 = (f32[3]{0:T(128)S(1)}, f32[3]{0:T(128)S(1)}, u32[]{:S(2)}, u32[]{:S(2)}) collective-permute-start(f32[3]{0:T(128)S(1)} %get-tuple-element.21), channel_id=1, source_target_pairs={{0,8},{1,9},{2,10},{3,11},{4,12},{5,13},{6,14},{7,15},{16,24},{17,... | collective-permute-start | bytes 44 | tf_op jit(solution)/shard_map/ppermute | solution.py:215
  106.3 2.1 %collective-permute-start.10 = (f32[3,16,128]{2,1,0:T(8,128)S(1)}, f32[3,16,128]{2,1,0:T(8,128)S(1)}, u32[]{:S(2)}, u32[]{:S(2)}) collective-permute-start(f32[3,16,128]{2,1,0:T(8,128)S(1)} %get-tuple-element.16), channel_id=1, source_target_pairs={{0,8},{1,9},{2,10},{3,11},{4,12},{5,13},{6,14},{7,15},{16,24},{17,... | collective-permute-start | bytes 73736 | tf_op jit(solution)/shard_map/ppermute | solution.py:216

commit v2 on v1

v2 whole, which is shorter than its diff:
```python
import functools

import jax
import jax.numpy as jnp
from jax import lax
from jax.experimental import pallas as pl
from jax.experimental.pallas import tpu as pltpu
from jax.sharding import PartitionSpec as P

HD = 128
CH = 64
STEPS = 40
SWITCH = 25


noise_shift = 12.0
high_guidance = 4.0
low_guidance = 3.0

VMEM = pl.BlockSpec(memory_space=pltpu.VMEM)
SMEM = pl.BlockSpec(memory_space=pltpu.SMEM)
PAIR = 2 * HD


def noise_level(step_now):
    fraction = 1.0 - step_now.astype(jnp.float32) / STEPS
    return noise_shift * fraction / (1.0 + (noise_shift - 1.0) * fraction)


def dot_last(left, right):
    return lax.dot_general(
        left, right, (((1,), (1,)), ((), ())), preferred_element_type=jnp.float32
    )


def side_by_side(first, second):
    zero = jnp.zeros_like(first)
    return [
        jnp.concatenate([first, zero], axis=1),
        jnp.concatenate([zero, second], axis=1),
    ]


def pack_kernel(count, group, width, me_ref, q_ref, k_ref, *out_refs):
    me = me_ref[0]
    for s in range(1, count):
        start = pl.multiple_of(((me ^ s) & (group - 1)) * width, width)
        there = pl.ds(start, width)
        out_refs[s - 1][:, :, 0:width] = q_ref[:, :, there]
        if s < group:
            out_refs[s - 1][:, :, width : 2 * width] = k_ref[:, :, there]


def project_kernel(group, width, me_ref, v_ref, w_ref, *out_refs):
    me = me_ref[0]
    videos = out_refs[0].shape[0]
    for s in range(group):
        first = ((me ^ s) & (group - 1)) * width
        for p in range(width // PAIR):
            start = pl.multiple_of(first + p * PAIR, PAIR)
            weight = w_ref[:, pl.ds(start, PAIR)]
            for v in range(videos):
                rows = []
                for way in range(2):
                    value = v_ref[2 * v + way, :, pl.ds(start, PAIR)]
                    rows += side_by_side(value[:, :HD], value[:, HD:])
                product = dot_last(weight, jnp.concatenate(rows, axis=0))
                out_refs[s][v, p] = product.astype(jnp.bfloat16)


def score_kernel(count, group, width, me_ref, q_ref, k_ref, *refs):
    others, (e_ref, stat_ref) = refs[: count - 1], refs[count - 1 :]
    first = (me_ref[0] & (group - 1)) * width
    items, rows, _ = q_ref.shape

    def one(i, carry):
        for p in range(width // PAIR):
            own = pl.ds(pl.multiple_of(first + p * PAIR, PAIR), PAIR)
            here = slice(p * PAIR, (p + 1) * PAIR)
            query = jnp.concatenate([q_ref[i, :, own]] + [r[i, :, here] for r in others], axis=0)
            keys = []
            for s in range(group):
                if s == 0:
                    key = k_ref[i, :, own]
                else:
                    key = others[s - 1][i, :, width + p * PAIR : width + (p + 1) * PAIR]
                keys += side_by_side(key[:, :HD], key[:, HD:])
            scores = dot_last(jnp.concatenate(keys, axis=0), query) * (HD ** (-0.5))
            for h in range(2):
                places = [slice((2 * s + h) * rows, (2 * s + h + 1) * rows) for s in range(group)]
                top = functools.reduce(jnp.maximum, [scores[place] for place in places])
                top = jnp.max(top, axis=0, keepdims=True)
                total = None
                for place in places:
                    exponent = jnp.exp(scores[place] - top)
                    e_ref[i, p, place, :] = exponent
                    total = exponent if total is None else total + exponent
                stat_ref[i, 0, 2 * p + h : 2 * p + h + 1, :] = top
                stat_ref[i, 1, 2 * p + h : 2 * p + h + 1, :] = jnp.sum(
                    total, axis=0, keepdims=True
                )
        return carry

    lax.fori_loop(0, items, one, 0)


def attend_kernel(count, group, scale_ref, skip_ref, e_ref, stat_ref, far_ref, *refs):
    vw_refs, out_ref, scratch = refs[:group], refs[group], refs[group + 1]
    videos, pairs = vw_refs[0].shape[:2]
    rows = e_ref.shape[2] // (2 * group)
    length = rows * count
    half = 2 * rows

    def one(v, carry):
        sums = []
        for way in range(2):
            i = 2 * v + way
            far_top = pltpu.roll(far_ref[i, 0], length // 2, 1)
            far_total = pltpu.roll(far_ref[i, 1], length // 2, 1)
            top = jnp.maximum(stat_ref[i, 0], far_top)
            near = jnp.exp(stat_ref[i, 0] - top)
            total = stat_ref[i, 1] * near + far_total * jnp.exp(far_top - top)
            factor = near / total
            acc = None
            for p in range(pairs):
                weights = []
                values = []
                for s in range(group):
                    for h in range(2):
                        place = slice((2 * s + h) * rows, (2 * s + h + 1) * rows)
                        scaled = e_ref[i, p, place, :] * factor[2 * p + h : 2 * p + h + 1]
                        weights.append(scaled.astype(jnp.bfloat16))
                    values.append(vw_refs[s][v, p][:, way * half : (way + 1) * half])
                term = jnp.dot(
                    jnp.concatenate(values, axis=1),
                    jnp.concatenate(weights, axis=0),
                    preferred_element_type=jnp.float32,
                )
                acc = term if acc is None else acc + term
            sums.append(acc)
        conditional, unconditional = sums
        guided = unconditional + scale_ref[0] * (conditional - unconditional)
        guided = jnp.where(skip_ref[v] == 1, conditional, guided)
        scratch[...] = jnp.concatenate([guided, guided], axis=0).T
        even = scratch[pl.ds(0, length // 2, stride=2), :]
        odd = scratch[pl.ds(1, length // 2, stride=2), :]
        column = lax.broadcasted_iota(jnp.int32, even.shape, 1)
        both = jnp.where(column < CH, even, odd)
        for s in range(count):
            out_ref[s, v] = both[s * rows // 2 : (s + 1) * rows // 2]
        return carry

    lax.fori_loop(0, videos, one, 0)


def call(kernel, outs, specs, name, scratch=(), flops=0, moved=0):
    return pl.pallas_call(
        kernel,
        out_shape=outs,
        in_specs=specs,
        out_specs=jax.tree.map(lambda _: VMEM, outs),
        scratch_shapes=scratch,
        name=name,
        compiler_params=pltpu.CompilerParams(vmem_limit_bytes=16 << 20),
        cost_estimate=pl.CostEstimate(flops=flops, bytes_accessed=moved, transcendentals=0),
    )


def on_device(count, latent, queries, keys, values, head_weight, step_index, skip_flags):
    section_index = lax.axis_index("section")
    me = lax.axis_index("sp")[None]
    _, videos, _, rows, feature_all = queries.shape
    items = videos * 2
    group = count // 2
    width = feature_all // group
    heads = width // HD
    length = rows * count
    query = queries[0].reshape(items, rows, feature_all)
    key = keys[0].reshape(items, rows, feature_all)
    value = values[0].reshape(items, rows, feature_all)

    def exchange(array, s):
        return lax.ppermute(array, "sp", [(i, i ^ s) for i in range(count)])

    def shape(*dims, dtype=jnp.bfloat16):
        return jax.ShapeDtypeStruct(dims, dtype)

    pack = call(
        functools.partial(pack_kernel, count, group, width),
        [shape(items, rows, (2 if s < group else 1) * width) for s in range(1, count)],
        [SMEM, VMEM, VMEM],
        "pack",
        moved=8 * items * rows * feature_all,
    )
    packed = pack(me, query, key)
    arrived = [exchange(packed[s - 1], s) for s in range(1, count)]

    project = call(
        functools.partial(project_kernel, group, width),
        [shape(videos, heads // 2, CH, 4 * rows)] * group,
        [SMEM, VMEM, VMEM],
        "project",
        flops=8 * items * rows * feature_all * CH,
        moved=3 * items * rows * feature_all,
    )
    projected = project(me, value, head_weight[0])
    projected = [projected[0]] + [exchange(projected[s], s) for s in range(1, group)]

    score = call(
        functools.partial(score_kernel, count, group, width),
        [
            shape(items, heads // 2, 2 * group * rows, length, dtype=jnp.float32),
            shape(items, 2, heads, length, dtype=jnp.float32),
        ],
        [SMEM] + [VMEM] * (count + 1),
        "score",
        flops=2 * items * heads * length * length * HD * 4,
        moved=8 * items * rows * feature_all,
    )
    exponents, near = score(me, query, key, *arrived)
    far = exchange(near, group)

    guidance = jnp.where(section_index == 0, jnp.float32(high_guidance), jnp.float32(low_guidance))
    skipping = jnp.where(section_index == 1, skip_flags, 0)
    attend = call(
        functools.partial(attend_kernel, count, group),
        shape(count, videos, rows // 2, 2 * CH, dtype=jnp.float32),
        [SMEM, SMEM] + [VMEM] * (group + 3),
        "attend",
        scratch=[pltpu.VMEM((length, 2 * CH), jnp.float32)],
        flops=2 * items * heads * length * length * HD * 4,
        moved=4 * items * rows * feature_all,
    )
    shares = attend(guidance[None], skipping, exponents, near, far, *projected)
    guided = shares[0]
    for s in range(1, count):
        guided = guided + exchange(shares[s], s)

    step_now = step_index[0]
    step_size = noise_level(step_now + 1) - noise_level(step_now)
    updated = latent[0] + step_size[:, None, None] * guided
    finish_mark = jnp.where(
        (section_index == 0) & (step_now + 1 == SWITCH), jnp.float32(1.0), jnp.float32(0.0)
    )
    arrived_mark = lax.ppermute(finish_mark, "section", [(0, 1)])
    arrived = lax.ppermute(updated, "section", [(0, 1)])
    taking = (section_index == 1) & (arrived_mark > 0.5)
    next_latent = jnp.where(taking[:, None, None], arrived, updated)
    return (guided[None], next_latent[None])


def solution(mesh):
    placed = (
        P("section", ("groups", "blk"), "sp", None),
        P("section", ("groups", "blk"), None, "sp", None),
        P("section", ("groups", "blk"), None, "sp", None),
        P("section", ("groups", "blk"), None, "sp", None),
        P("section", None, None),
        P("section", ("groups", "blk")),
        P(("groups", "blk")),
    )
    return jax.shard_map(
        functools.partial(on_device, mesh.shape["sp"]),
        mesh=mesh,
        in_specs=placed,
        out_specs=(
            P("section", ("groups", "blk"), "sp", None),
            P("section", ("groups", "blk"), "sp", None),
        ),
        check_vma=False,
    )
```

time: 109 us -> 109 us (level)
  starting transfers between devices: 22.9 us -> 14.1 us
  waiting for transfers between devices: 70 us -> 74.3 us
  local copies, waits for them, and re-layouts: 4.56 us -> 7.4 us
  Pallas kernels: 9.51 us -> 10.9 us
    ppermute x9 -> x8, starting transfers between devices: 20.4 us -> 11.5 us  [exchange(): return lax.ppermute(array, 'sp', [(i, i ^ s) for i in range(count)])]
    ppermute x9 -> x8, waiting for transfers between devices: 69.2 us -> 73.5 us  [exchange(): return lax.ppermute(array, 'sp', [(i, i ^ s) for i in range(count)])]
    unnamed x20 -> x22, local copies, waits for them, and re-layouts: 4.55 us -> 7.39 us
  transfers between devices with their start and end apart: 11 -> 10, of which waited for: 6 -> 5; matrix products, arithmetic and copies ran while one was open for 1% -> 1% of each run, Pallas kernels for 5% -> 6%
where the time goes in v2:
time: 109 us
  waiting for transfers between devices  74.3 us (68%)
  starting transfers between devices  14.1 us (13%)
  Pallas kernels  10.9 us (10%)
  local copies, waits for them, and re-layouts  7.4 us (7%)
  other arithmetic  1.32 us (1%)
    ppermute x8, waiting for transfers between devices, exchange(): return lax.ppermute(array, 'sp', [(i, i ^ s) for i in range(count)])  73.5 us
    ppermute x8, starting transfers between devices, exchange(): return lax.ppermute(array, 'sp', [(i, i ^ s) for i in range(count)])  11.5 us
    unnamed x22, local copies, waits for them, and re-layouts  7.39 us
    pallas_call x1, Pallas kernels, on_device(): exponents, near = score(me, query, key, *arrived)  4.6 us
    pallas_call x1, Pallas kernels, on_device(): shares = attend(guidance[None], skipping, exponents, near, far, *projected)  2.48 us
  transfers between devices with their start and end apart: 10, of which 5 were waited for; matrix products, arithmetic and copies ran while one was open for 1% of the time, Pallas kernels for 6%

profile of v2, /device:TPU:0, one launch (start us, length us, event | category | flops | bytes accessed | tf_op | source)
XLA Modules:
  0.0 108.7 jit_solution(9615670503516588493)
XLA Ops:
  0.6 0.0 copy-start
  0.6 1.4 %copy-done = bf16[1,3,2,32,4096]{4,3,2,1,0:T(8,128)(2,1)S(1)} copy-done((bf16[1,3,2,32,4096]{4,3,2,1,0:T(8,128)(2,1)S(1)}, bf16[1,3,2,32,4096]{4,3,2,1,0:T(8,128)(2,1)}, u32[]{:S(2)}) %copy-start) | copy-done | bytes 1572888
  2.0 1.4 %copy-done.2 = bf16[1,3,2,32,4096]{4,3,2,1,0:T(8,128)(2,1)S(1)} copy-done((bf16[1,3,2,32,4096]{4,3,2,1,0:T(8,128)(2,1)S(1)}, bf16[1,3,2,32,4096]{4,3,2,1,0:T(8,128)(2,1)}, u32[]{:S(2)}) %copy-start.2) | copy-done | bytes 1572888
  3.5 1.9 %pack.1 = (bf16[6,32,4096]{2,1,0:T(8,128)(2,1)}, bf16[6,32,2048]{2,1,0:T(8,128)(2,1)}, bf16[6,32,2048]{2,1,0:T(8,128)(2,1)}) custom-call(s32[1]{0:T(128)} %bitcast.1.me_ref, bf16[6,32,4096]{2,1,0:T(8,128)(2,1)S(1)} %bitcast.30, bf16[6,32,4096]{2,1,0:T(8,128)(2,1)S(1)} %bitcast.32), custom_call_target="tpu_custom_call" | custom-call | bytes 6291456 | tf_op jit(solution)/shard_map/pack/pallas_call | solution.py:195
  5.3 3.0 %collective-permute-start = (bf16[6,32,4096]{2,1,0:T(8,128)(2,1)}, bf16[6,32,4096]{2,1,0:T(8,128)(2,1)}, u32[]{:S(2)}, u32[]{:S(2)}) collective-permute-start(bf16[6,32,4096]{2,1,0:T(8,128)(2,1)} %get-tuple-element.9), channel_id=1, source_target_pairs={{0,2},{2,0},{4,6},{6,4},{1,3},{3,1},{5,7},{7,5},{8,10},{10,8},{12,... | collective-permute-start | bytes 4718600 | tf_op jit(solution)/shard_map/ppermute | solution.py:183
  8.3 2.6 %collective-permute-start.1 = (bf16[6,32,2048]{2,1,0:T(8,128)(2,1)}, bf16[6,32,2048]{2,1,0:T(8,128)(2,1)}, u32[]{:S(2)}, u32[]{:S(2)}) collective-permute-start(bf16[6,32,2048]{2,1,0:T(8,128)(2,1)} %get-tuple-element.10), channel_id=1, source_target_pairs={{0,4},{2,6},{4,0},{6,2},{1,5},{3,7},{5,1},{7,3},{8,12},{10,14},{12... | collective-permute-start | bytes 2359304 | tf_op jit(solution)/shard_map/ppermute | solution.py:183
  10.9 0.0 collective-permute-start.2
  10.9 1.0 copy-done.5
  12.0 2.0 %project.1 = (bf16[3,8,64,128]{3,2,1,0:T(8,128)(2,1)S(1)}, bf16[3,8,64,128]{3,2,1,0:T(8,128)(2,1)}) custom-call(s32[1]{0:T(128)} %bitcast.1.me_ref, bf16[6,32,4096]{2,1,0:T(8,128)(2,1)S(1)} %bitcast.34, bf16[64,4096]{1,0:T(8,128)(2,1)S(1)} %bitcast.35), custom_call_target="tpu_custom_call" | custom-call | flops 402653184 | bytes 2359296 | tf_op jit(solution)/shard_map/project/pallas_call | solution.py:206
  14.0 0.9 collective-permute-start.4
  14.8 45.5 %collective-permute-done.1.refs_1_ = bf16[6,32,2048]{2,1,0:T(8,128)(2,1)} collective-permute-done((bf16[6,32,2048]{2,1,0:T(8,128)(2,1)}, bf16[6,32,2048]{2,1,0:T(8,128)(2,1)}, u32[]{:S(2)}, u32[]{:S(2)}) %collective-permute-start.1) | collective-permute-done | bytes 786464 | tf_op jit(solution)/shard_map/ppermute | solution.py:183
  60.4 19.8 %collective-permute-done.2.refs_2_ = bf16[6,32,2048]{2,1,0:T(8,128)(2,1)} collective-permute-done((bf16[6,32,2048]{2,1,0:T(8,128)(2,1)}, bf16[6,32,2048]{2,1,0:T(8,128)(2,1)}, u32[]{:S(2)}, u32[]{:S(2)}) %collective-permute-start.2) | collective-permute-done | bytes 786464 | tf_op jit(solution)/shard_map/ppermute | solution.py:183
  80.2 0.0 collective-permute-done.refs_0_
  80.2 4.6 %score.1 = (f32[6,8,128,128]{3,2,1,0:T(8,128)S(1)}, f32[6,2,16,128]{3,2,1,0:T(8,128)}) custom-call(s32[1]{0:T(128)} %bitcast.1.me_ref, bf16[6,32,4096]{2,1,0:T(8,128)(2,1)S(1)} %bitcast.31, bf16[6,32,4096]{2,1,0:T(8,128)(2,1)S(1)} %bitcast.33, bf16[6,32,4096]{2,1,0:T(8,128)(2,1)} %collective-permute-done.refs_0_, ...), custom_call_target="tpu_custom_call" | custom-call | flops 1610612736 | bytes 6291456 | tf_op jit(solution)/shard_map/score/pallas_call | solution.py:220
  84.8 1.6 %copy-done.6 = f32[6,8,128,128]{3,2,1,0:T(8,128)} copy-done((f32[6,8,128,128]{3,2,1,0:T(8,128)}, f32[6,8,128,128]{3,2,1,0:T(8,128)S(1)}, u32[]{:S(2)}) %copy-start.6) | copy-done | bytes 3145752
  86.4 0.6 collective-permute-start.3
  87.0 0.0 collective-permute-done.4.refs_1_
  87.0 5.2 %collective-permute-done.3.far_ref = f32[6,2,16,128]{3,2,1,0:T(8,128)S(1)} collective-permute-done((f32[6,2,16,128]{3,2,1,0:T(8,128)}, f32[6,2,16,128]{3,2,1,0:T(8,128)S(1)}, u32[]{:S(2)}, u32[]{:S(2)}) %collective-permute-start.3) | collective-permute-done | bytes 98336 | tf_op jit(solution)/shard_map/ppermute | solution.py:183
  92.2 1.9 %copy-done.7 = f32[6,8,128,128]{3,2,1,0:T(8,128)S(1)} copy-done((f32[6,8,128,128]{3,2,1,0:T(8,128)S(1)}, f32[6,8,128,128]{3,2,1,0:T(8,128)}, u32[]{:S(2)}) %copy-start.7) | copy-done | bytes 3145752
  94.0 2.5 %attend.1 = f32[4,3,16,128]{3,2,1,0:T(8,128)S(1)} custom-call(f32[1]{0:T(128)} %bitcast.scale_ref, s32[3]{0:T(128)S(1)} %broadcast_select_fusion.skip_ref, f32[6,8,128,128]{3,2,1,0:T(8,128)S(1)} %copy-done.7, f32[6,2,16,128]{3,2,1,0:T(8,128)} %get-tuple-element.13.stat_ref, f32[6,2,16,128]{3,2,1,0:T(8,128)S(1)} %collective-permute-done.3.far_ref, ...), custom_call_target="tpu_custom_call" | custom-call | flops 1610612736 | bytes 3145728 | tf_op jit(solution)/shard_map/attend/pallas_call | solution.py:234
  96.6 0.1 collective-permute-start.5
  96.6 3.1 %collective-permute-start.6 = (f32[3,16,128]{2,1,0:T(8,128)S(1)}, f32[3,16,128]{2,1,0:T(8,128)S(1)}, u32[]{:S(2)}, u32[]{:S(2)}) collective-permute-start(f32[3,16,128]{2,1,0:T(8,128)S(1)} %get-tuple-element.20), channel_id=1, source_target_pairs={{0,4},{2,6},{4,0},{6,2},{1,5},{3,7},{5,1},{7,3},{8,12},{10,14},{12... | collective-permute-start | bytes 73736 | tf_op jit(solution)/shard_map/ppermute | solution.py:183
  99.7 1.3 %collective-permute-start.7 = (f32[3,16,128]{2,1,0:T(8,128)S(1)}, f32[3,16,128]{2,1,0:T(8,128)S(1)}, u32[]{:S(2)}, u32[]{:S(2)}) collective-permute-start(f32[3,16,128]{2,1,0:T(8,128)S(1)} %get-tuple-element.19), channel_id=1, source_target_pairs={{0,6},{2,4},{4,2},{6,0},{1,7},{3,5},{5,3},{7,1},{8,14},{10,12},{12... | collective-permute-start | bytes 73736 | tf_op jit(solution)/shard_map/ppermute | solution.py:183
  101.0 1.3 %collective-permute-start.8 = (f32[3]{0:T(128)S(1)}, f32[3]{0:T(128)S(1)}, u32[]{:S(2)}, u32[]{:S(2)}) collective-permute-start(f32[3]{0:T(128)S(1)} %get-tuple-element.21), channel_id=1, source_target_pairs={{0,8},{1,9},{2,10},{3,11},{4,12},{5,13},{6,14},{7,15},{16,24},{17,... | collective-permute-start | bytes 44 | tf_op jit(solution)/shard_map/ppermute | solution.py:245
  102.3 0.0 collective-permute-done.5
  102.3 0.0 collective-permute-done.6
  102.3 3.0 %collective-permute-done.7 = f32[3,16,128]{2,1,0:T(8,128)S(1)} collective-permute-done((f32[3,16,128]{2,1,0:T(8,128)S(1)}, f32[3,16,128]{2,1,0:T(8,128)S(1)}, u32[]{:S(2)}, u32[]{:S(2)}) %collective-permute-start.7) | collective-permute-done | bytes 24608 | tf_op jit(solution)/shard_map/ppermute | solution.py:183
  105.3 0.6 bitcast_add_fusion
  105.9 1.3 %collective-permute-start.9 = (f32[3,16,128]{2,1,0:T(8,128)S(1)}, f32[3,16,128]{2,1,0:T(8,128)S(1)}, u32[]{:S(2)}, u32[]{:S(2)}) collective-permute-start(f32[3,16,128]{2,1,0:T(8,128)S(1)} %get-tuple-element.16), channel_id=1, source_target_pairs={{0,8},{1,9},{2,10},{3,11},{4,12},{5,13},{6,14},{7,15},{16,24},{17,... | collective-permute-start | bytes 73736 | tf_op jit(solution)/shard_map/ppermute | solution.py:246
  107.2 0.0 collective-permute-done.8
  107.2 0.8 collective-permute-done.9
  108.1 0.7 select_bitcast_fusion
  (20 shorter events, 0.1 us)
Async XLA Ops:
  0.6 1.4 %copy-start = (bf16[1,3,2,32,4096]{4,3,2,1,0:T(8,128)(2,1)S(1)}, bf16[1,3,2,32,4096]{4,3,2,1,0:T(8,128)(2,1)}, u32[]{:S(2)}) copy-start(bf16[1,3,2,32,4096]{4,3,2,1,0:T(8,128)(2,1)} %param.8) | copy-start | bytes 4718596
  2.0 1.4 %copy-start.2 = (bf16[1,3,2,32,4096]{4,3,2,1,0:T(8,128)(2,1)S(1)}, bf16[1,3,2,32,4096]{4,3,2,1,0:T(8,128)(2,1)}, u32[]{:S(2)}) copy-start(bf16[1,3,2,32,4096]{4,3,2,1,0:T(8,128)(2,1)} %param.9) | copy-start | bytes 4718596
  3.5 7.5 %copy-start.4 = (bf16[1,3,2,32,4096]{4,3,2,1,0:T(8,128)(2,1)S(1)}, bf16[1,3,2,32,4096]{4,3,2,1,0:T(8,128)(2,1)}, u32[]{:S(2)}) copy-start(bf16[1,3,2,32,4096]{4,3,2,1,0:T(8,128)(2,1)} %param.10) | copy-start | bytes 4718596
  3.5 76.7 %copy-start.3 = (bf16[1,3,2,32,4096]{4,3,2,1,0:T(8,128)(2,1)S(1)}, bf16[1,3,2,32,4096]{4,3,2,1,0:T(8,128)(2,1)}, u32[]{:S(2)}) copy-start(bf16[1,3,2,32,4096]{4,3,2,1,0:T(8,128)(2,1)} %param.9) | copy-start | bytes 4718596
  5.3 74.9 %copy-start.1 = (bf16[1,3,2,32,4096]{4,3,2,1,0:T(8,128)(2,1)S(1)}, bf16[1,3,2,32,4096]{4,3,2,1,0:T(8,128)(2,1)}, u32[]{:S(2)}) copy-start(bf16[1,3,2,32,4096]{4,3,2,1,0:T(8,128)(2,1)} %param.8) | copy-start | bytes 4718596
  5.3 74.9 %collective-permute-start = (bf16[6,32,4096]{2,1,0:T(8,128)(2,1)}, bf16[6,32,4096]{2,1,0:T(8,128)(2,1)}, u32[]{:S(2)}, u32[]{:S(2)}) collective-permute-start(bf16[6,32,4096]{2,1,0:T(8,128)(2,1)} %get-tuple-element.9), channel_id=1, source_target_pairs={{0,2},{2,0},{4,6},{6,4},{1,3},{3,1},{5,7},{7,5},{8,10},{10,8},{12,... | collective-permute-start | bytes 4718600 | tf_op jit(solution)/shard_map/ppermute | solution.py:183
  8.3 52.0 %collective-permute-start.1 = (bf16[6,32,2048]{2,1,0:T(8,128)(2,1)}, bf16[6,32,2048]{2,1,0:T(8,128)(2,1)}, u32[]{:S(2)}, u32[]{:S(2)}) collective-permute-start(bf16[6,32,2048]{2,1,0:T(8,128)(2,1)} %get-tuple-element.10), channel_id=1, source_target_pairs={{0,4},{2,6},{4,0},{6,2},{1,5},{3,7},{5,1},{7,3},{8,12},{10,14},{12... | collective-permute-start | bytes 2359304 | tf_op jit(solution)/shard_map/ppermute | solution.py:183
  10.9 69.3 %collective-permute-start.2 = (bf16[6,32,2048]{2,1,0:T(8,128)(2,1)}, bf16[6,32,2048]{2,1,0:T(8,128)(2,1)}, u32[]{:S(2)}, u32[]{:S(2)}) collective-permute-start(bf16[6,32,2048]{2,1,0:T(8,128)(2,1)} %get-tuple-element.11), channel_id=1, source_target_pairs={{0,6},{2,4},{4,2},{6,0},{1,7},{3,5},{5,3},{7,1},{8,14},{10,12},{12... | collective-permute-start | bytes 2359304 | tf_op jit(solution)/shard_map/ppermute | solution.py:183
  10.9 1.0 copy-start.5
  14.0 73.0 %collective-permute-start.4 = (bf16[3,8,64,128]{3,2,1,0:T(8,128)(2,1)}, bf16[3,8,64,128]{3,2,1,0:T(8,128)(2,1)}, u32[]{:S(2)}, u32[]{:S(2)}) collective-permute-start(bf16[3,8,64,128]{3,2,1,0:T(8,128)(2,1)} %get-tuple-element.15), channel_id=1, source_target_pairs={{0,2},{2,0},{4,6},{6,4},{1,3},{3,1},{5,7},{7,5},{8,10},{10,8},{12,... | collective-permute-start | bytes 1179656 | tf_op jit(solution)/shard_map/ppermute | solution.py:183
  14.8 72.1 %copy-start.10 = (s32[3]{0:T(128)S(1)}, s32[3]{0:T(128)}, u32[]{:S(2)}) copy-start(s32[3]{0:T(128)} %param.13) | copy-start | bytes 40
  84.8 1.6 %copy-start.6 = (f32[6,8,128,128]{3,2,1,0:T(8,128)}, f32[6,8,128,128]{3,2,1,0:T(8,128)S(1)}, u32[]{:S(2)}) copy-start(f32[6,8,128,128]{3,2,1,0:T(8,128)S(1)} %get-tuple-element.12.e_ref) | copy-start | bytes 9437188
  86.4 5.7 %collective-permute-start.3 = (f32[6,2,16,128]{3,2,1,0:T(8,128)}, f32[6,2,16,128]{3,2,1,0:T(8,128)S(1)}, u32[]{:S(2)}, u32[]{:S(2)}) collective-permute-start(f32[6,2,16,128]{3,2,1,0:T(8,128)} %get-tuple-element.13.stat_ref), channel_id=1, source_target_pairs={{0,4},{2,6},{4,0},{6,2},{1,5},{3,7},{5,1},{7,3},{8,12},{10,14},{12... | collective-permute-start | bytes 294920 | tf_op jit(solution)/shard_map/ppermute | solution.py:183
  92.2 1.9 %copy-start.7 = (f32[6,8,128,128]{3,2,1,0:T(8,128)S(1)}, f32[6,8,128,128]{3,2,1,0:T(8,128)}, u32[]{:S(2)}) copy-start(f32[6,8,128,128]{3,2,1,0:T(8,128)} %copy-done.6) | copy-start | bytes 9437188
  94.0 7.0 %copy-start.9 = (s32[1,3]{1,0:T(1,128)S(1)}, s32[1,3]{1,0:T(1,128)}, u32[]{:S(2)}) copy-start(s32[1,3]{1,0:T(1,128)} %param.12) | copy-start | bytes 40
  94.0 11.3 %copy-start.8 = (f32[1,3,16,128]{3,2,1,0:T(8,128)S(1)}, f32[1,3,16,128]{3,2,1,0:T(8,128)}, u32[]{:S(2)}) copy-start(f32[1,3,16,128]{3,2,1,0:T(8,128)} %param.7) | copy-start | bytes 73732
  96.6 5.8 %collective-permute-start.5 = (f32[3,16,128]{2,1,0:T(8,128)S(1)}, f32[3,16,128]{2,1,0:T(8,128)S(1)}, u32[]{:S(2)}, u32[]{:S(2)}) collective-permute-start(f32[3,16,128]{2,1,0:T(8,128)S(1)} %get-tuple-element.18), channel_id=1, source_target_pairs={{0,2},{2,0},{4,6},{6,4},{1,3},{3,1},{5,7},{7,5},{8,10},{10,8},{12,... | collective-permute-start | bytes 73736 | tf_op jit(solution)/shard_map/ppermute | solution.py:183
  96.6 5.7 %collective-permute-start.6 = (f32[3,16,128]{2,1,0:T(8,128)S(1)}, f32[3,16,128]{2,1,0:T(8,128)S(1)}, u32[]{:S(2)}, u32[]{:S(2)}) collective-permute-start(f32[3,16,128]{2,1,0:T(8,128)S(1)} %get-tuple-element.20), channel_id=1, source_target_pairs={{0,4},{2,6},{4,0},{6,2},{1,5},{3,7},{5,1},{7,3},{8,12},{10,14},{12... | collective-permute-start | bytes 73736 | tf_op jit(solution)/shard_map/ppermute | solution.py:183
  99.7 5.6 %collective-permute-start.7 = (f32[3,16,128]{2,1,0:T(8,128)S(1)}, f32[3,16,128]{2,1,0:T(8,128)S(1)}, u32[]{:S(2)}, u32[]{:S(2)}) collective-permute-start(f32[3,16,128]{2,1,0:T(8,128)S(1)} %get-tuple-element.19), channel_id=1, source_target_pairs={{0,6},{2,4},{4,2},{6,0},{1,7},{3,5},{5,3},{7,1},{8,14},{10,12},{12... | collective-permute-start | bytes 73736 | tf_op jit(solution)/shard_map/ppermute | solution.py:183
  101.0 6.2 %collective-permute-start.8 = (f32[3]{0:T(128)S(1)}, f32[3]{0:T(128)S(1)}, u32[]{:S(2)}, u32[]{:S(2)}) collective-permute-start(f32[3]{0:T(128)S(1)} %get-tuple-element.21), channel_id=1, source_target_pairs={{0,8},{1,9},{2,10},{3,11},{4,12},{5,13},{6,14},{7,15},{16,24},{17,... | collective-permute-start | bytes 44 | tf_op jit(solution)/shard_map/ppermute | solution.py:245
  105.9 2.1 %collective-permute-start.9 = (f32[3,16,128]{2,1,0:T(8,128)S(1)}, f32[3,16,128]{2,1,0:T(8,128)S(1)}, u32[]{:S(2)}, u32[]{:S(2)}) collective-permute-start(f32[3,16,128]{2,1,0:T(8,128)S(1)} %get-tuple-element.16), channel_id=1, source_target_pairs={{0,8},{1,9},{2,10},{3,11},{4,12},{5,13},{6,14},{7,15},{16,24},{17,... | collective-permute-start | bytes 73736 | tf_op jit(solution)/shard_map/ppermute | solution.py:246

commit v3 on v2

v3 whole, which is shorter than its diff:
```python
import functools

import jax
import jax.numpy as jnp
from jax import lax
from jax.experimental import pallas as pl
from jax.experimental.pallas import tpu as pltpu
from jax.sharding import PartitionSpec as P

HD = 128
CH = 64
STEPS = 40
SWITCH = 25


noise_shift = 12.0
high_guidance = 4.0
low_guidance = 3.0

VMEM = pl.BlockSpec(memory_space=pltpu.VMEM)
SMEM = pl.BlockSpec(memory_space=pltpu.SMEM)
HBM = pl.BlockSpec(memory_space=pltpu.HBM)
PAIR = 2 * HD


def noise_level(step_now):
    fraction = 1.0 - step_now.astype(jnp.float32) / STEPS
    return noise_shift * fraction / (1.0 + (noise_shift - 1.0) * fraction)


def dot_last(left, right):
    return lax.dot_general(
        left, right, (((1,), (1,)), ((), ())), preferred_element_type=jnp.float32
    )


def side_by_side(first, second):
    zero = jnp.zeros_like(first)
    return [
        jnp.concatenate([first, zero], axis=1),
        jnp.concatenate([zero, second], axis=1),
    ]


def pack_kernel(first, group, width, shifts, me_ref, q_ref, *refs):
    out_refs, sems = refs[:-1], refs[-1]
    copies = []
    for n, (s, out_ref) in enumerate(zip(shifts, out_refs)):
        start = pl.multiple_of(((me_ref[0] ^ s) & (group - 1)) * width, width)
        for i in range(out_ref.shape[0]):
            copies.append(
                pltpu.make_async_copy(
                    q_ref.at[first + i, :, pl.ds(start, width)], out_ref.at[i], sems.at[n, i]
                )
            )
    for copy in copies:
        copy.start()
    for copy in copies:
        copy.wait()


def pack_near_kernel(first, group, width, me_ref, q_ref, k_ref, *refs):
    out_refs, sems = refs[:-1], refs[-1]
    copies = []
    for s in range(1, group):
        start = pl.multiple_of(((me_ref[0] ^ s) & (group - 1)) * width, width)
        for n, ref in enumerate([q_ref, k_ref]):
            for i in range(out_refs[0].shape[0]):
                copies.append(
                    pltpu.make_async_copy(
                        ref.at[first + i, :, pl.ds(start, width)],
                        out_refs[s - 1].at[i, :, pl.ds(n * width, width)],
                        sems.at[s - 1, n, i],
                    )
                )
    for copy in copies:
        copy.start()
    for copy in copies:
        copy.wait()


def project_kernel(first, group, width, me_ref, v_ref, w_ref, *out_refs):
    me = me_ref[0]
    videos = out_refs[0].shape[0]
    for s in range(group):
        lane = ((me ^ s) & (group - 1)) * width
        for p in range(width // PAIR):
            start = pl.multiple_of(lane + p * PAIR, PAIR)
            weight = w_ref[:, pl.ds(start, PAIR)]
            for v in range(videos):
                rows = []
                for way in range(2):
                    value = v_ref[2 * (first + v) + way, :, pl.ds(start, PAIR)]
                    rows += side_by_side(value[:, :HD], value[:, HD:])
                product = dot_last(weight, jnp.concatenate(rows, axis=0))
                out_refs[s][v, p] = product.astype(jnp.bfloat16)


def score_kernel(first, count, group, width, me_ref, q_ref, k_ref, *refs):
    others, outs = refs[: count - 1], refs[count - 1 :]
    whole = group == count
    lane = (me_ref[0] & (group - 1)) * width
    rows = q_ref.shape[1]
    items = outs[0].shape[0]

    def one(i, carry):
        for p in range(width // PAIR):
            own = pl.ds(pl.multiple_of(lane + p * PAIR, PAIR), PAIR)
            here = slice(p * PAIR, (p + 1) * PAIR)
            query = jnp.concatenate(
                [q_ref[2 * first + i, :, own]] + [r[i, :, here] for r in others], axis=0
            )
            keys = []
            for s in range(group):
                if s == 0:
                    key = k_ref[2 * first + i, :, own]
                else:
                    key = others[s - 1][i, :, width + p * PAIR : width + (p + 1) * PAIR]
                keys += side_by_side(key[:, :HD], key[:, HD:])
            scores = dot_last(jnp.concatenate(keys, axis=0), query) * (HD ** (-0.5))
            for h in range(2):
                places = [slice((2 * s + h) * rows, (2 * s + h + 1) * rows) for s in range(group)]
                top = functools.reduce(jnp.maximum, [scores[place] for place in places])
                top = jnp.max(top, axis=0, keepdims=True)
                exponents = [jnp.exp(scores[place] - top) for place in places]
                total = jnp.sum(
                    functools.reduce(jnp.add, exponents), axis=0, keepdims=True
                )
                if whole:
                    share = 1.0 / total
                    exponents = [(e * share).astype(jnp.bfloat16) for e in exponents]
                else:
                    outs[1][i, 0, 2 * p + h : 2 * p + h + 1, :] = top
                    outs[1][i, 1, 2 * p + h : 2 * p + h + 1, :] = total
                for place, e in zip(places, exponents):
                    outs[0][i, p, place, :] = e
        return carry

    lax.fori_loop(0, items, one, 0)


def attend_kernel(first, count, group, keep, scale_ref, skip_ref, *refs):
    scratch, refs = refs[-1], refs[:-1]
    whole = group == count
    e_ref, refs = refs[0], refs[1:]
    if not whole:
        (stat_ref, far_ref), refs = refs[:2], refs[2:]
    vw_refs, refs = refs[:group], refs[group:]
    before_refs, out_refs = (refs[:count] if keep else ()), refs[-count:]
    items, pairs = e_ref.shape[:2]
    rows = e_ref.shape[2] // (2 * group)
    length = rows * count
    half = 2 * rows
    offset = first if before_refs else 0

    def one(v, carry):
        sums = []
        for way in range(2):
            i = 2 * v + way
            if not whole:
                far_top = pltpu.roll(far_ref[i, 0], length // 2, 1)
                far_total = pltpu.roll(far_ref[i, 1], length // 2, 1)
                top = jnp.maximum(stat_ref[i, 0], far_top)
                near = jnp.exp(stat_ref[i, 0] - top)
                factor = near / (stat_ref[i, 1] * near + far_total * jnp.exp(far_top - top))
            acc = None
            for p in range(pairs):
                weights = []
                values = []
                for s in range(group):
                    for h in range(2):
                        e = e_ref[i, p, (2 * s + h) * rows : (2 * s + h + 1) * rows, :]
                        if not whole:
                            e = (e * factor[2 * p + h : 2 * p + h + 1]).astype(jnp.bfloat16)
                        weights.append(e)
                    values.append(vw_refs[s][v, p][:, way * half : (way + 1) * half])
                term = jnp.dot(
                    jnp.concatenate(values, axis=1),
                    jnp.concatenate(weights, axis=0),
                    preferred_element_type=jnp.float32,
                )
                acc = term if acc is None else acc + term
            sums.append(acc)
        conditional, unconditional = sums
        guided = unconditional + scale_ref[0] * (conditional - unconditional)
        guided = jnp.where(skip_ref[first + v] == 1, conditional, guided)
        scratch[...] = jnp.concatenate([guided, guided], axis=0).T
        even = scratch[pl.ds(0, length // 2, stride=2), :]
        odd = scratch[pl.ds(1, length // 2, stride=2), :]
        column = lax.broadcasted_iota(jnp.int32, even.shape, 1)
        both = jnp.where(column < CH, even, odd)
        for s in range(count):
            out_refs[s][offset + v] = both[s * rows // 2 : (s + 1) * rows // 2]
        return carry

    lax.fori_loop(0, items // 2, one, 0)
    for before_ref, out_ref in zip(before_refs, out_refs):
        out_ref[0:first] = before_ref[...]


def call(kernel, outs, specs, name, scratch=(), flops=0, moved=0, space=VMEM, limit=16 << 20):
    return pl.pallas_call(
        kernel,
        out_shape=outs,
        in_specs=specs,
        out_specs=space if isinstance(space, list) else jax.tree.map(lambda _: space, outs),
        scratch_shapes=scratch,
        name=name,
        compiler_params=pltpu.CompilerParams(vmem_limit_bytes=limit),
        cost_estimate=pl.CostEstimate(flops=flops, bytes_accessed=moved, transcendentals=0),
    )


def after(array, *others):
    return lax.optimization_barrier((array, *others))[0]


def shape(*dims, dtype=jnp.bfloat16):
    return jax.ShapeDtypeStruct(dims, dtype)


def on_device(count, latent, queries, keys, values, head_weight, step_index, skip_flags):
    section_index = lax.axis_index("section")
    me = lax.axis_index("sp")[None]
    _, videos, _, rows, feature_all = queries.shape
    items = videos * 2
    length = rows * count
    query = queries[0].reshape(items, rows, feature_all)
    key = keys[0].reshape(items, rows, feature_all)
    value = values[0].reshape(items, rows, feature_all)
    late = max(1, videos // 3)
    early = videos - late

    def exchange(array, s):
        return lax.ppermute(array, "sp", [(i, i ^ s) for i in range(count)])

    def pack(me, first, many, group, shifts):
        width = feature_all // group
        return call(
            functools.partial(pack_kernel, 2 * first, group, width, shifts),
            [shape(2 * many, rows, width)] * len(shifts),
            [SMEM, HBM],
            "pack",
            scratch=[pltpu.SemaphoreType.DMA((len(shifts), 2 * many))],
            moved=8 * many * rows * width * len(shifts),
            limit=None,
        )(me, query)

    def pack_near(me, first, many, group):
        width = feature_all // group
        return call(
            functools.partial(pack_near_kernel, 2 * first, group, width),
            [shape(2 * many, rows, 2 * width)] * (group - 1),
            [SMEM, HBM, HBM],
            "pack_near",
            scratch=[pltpu.SemaphoreType.DMA((group - 1, 2, 2 * many))],
            moved=16 * many * rows * width * (group - 1),
            limit=None,
        )(me, query, key)

    def project(me, first, many, group):
        width = feature_all // group
        return call(
            functools.partial(project_kernel, first, group, width),
            [shape(many, width // PAIR, CH, 4 * rows)] * group,
            [SMEM, VMEM, VMEM],
            "project",
            flops=16 * many * rows * feature_all * CH,
            moved=6 * many * rows * feature_all,
        )(me, value, head_weight[0])

    def score(me, first, many, group, arrived):
        width = feature_all // group
        heads = width // HD
        dims = (2 * many, heads // 2, 2 * group * rows, length)
        if group == count:
            outs = [shape(*dims)]
        else:
            outs = [
                shape(*dims, dtype=jnp.float32),
                shape(2 * many, 2, heads, length, dtype=jnp.float32),
            ]
        return call(
            functools.partial(score_kernel, first, count, group, width),
            outs,
            [SMEM] + [VMEM] * (count + 1),
            "score",
            flops=16 * many * heads * length * length * HD,
            moved=16 * many * rows * feature_all,
        )(me, query, key, *[arrived[s] for s in range(1, count)])

    guidance = jnp.where(section_index == 0, jnp.float32(high_guidance), jnp.float32(low_guidance))
    skipping = jnp.where(section_index == 1, skip_flags, 0)

    def attend(first, group, weights, projected, before=()):
        many = projected[0].shape[0]
        total = first + many
        return call(
            functools.partial(attend_kernel, first, count, group, bool(before)),
            [shape(total, rows // 2, 2 * CH, dtype=jnp.float32)] * count,
            [SMEM, SMEM] + [VMEM] * (len(weights) + group + len(before)),
            "attend",
            scratch=[pltpu.VMEM((length, 2 * CH), jnp.float32)],
            flops=16 * many * feature_all * length * HD,
            moved=8 * many * rows * feature_all,
        )(guidance[None], skipping, *weights, *projected, *before)

    half = count // 2
    step_now = step_index[0]
    finish_mark = jnp.where(
        (section_index == 0) & (step_now + 1 == SWITCH), jnp.float32(1.0), jnp.float32(0.0)
    )

    far_shifts = list(range(count - 1, half - 1, -1))

    def send_far(first, many):
        packed = pack(me, first, many, half, far_shifts)
        return {s: exchange(array, s) for s, array in zip(far_shifts, packed)}

    def send_near(first, many, gate=()):
        packed = pack_near(me, first, many, half)
        return {s: exchange(after(array, *gate), s) for s, array in enumerate(packed, 1)}

    def send_values(first, many, gate=()):
        sent = project(me, first, many, half)
        return [sent[0]] + [exchange(after(sent[s], *gate), s) for s in range(1, half)]

    arrived = send_far(0, early)
    arrived.update(send_near(0, early))
    late_arrived = send_far(early, late)
    late_arrived.update(send_near(early, late, [arrived[half]]))
    values_here = send_values(0, early, [arrived[count - 1]])
    late_values = send_values(early, late, [arrived[1]])

    arrived_mark = lax.ppermute(finish_mark, "section", [(0, 1)])
    exponents, near = score(after(me, arrived_mark), 0, early, half, arrived)
    far = exchange(near, half)
    shares = attend(0, half, [exponents, near, far], values_here)

    exponents, near = score(me, early, late, half, late_arrived)
    far = exchange(near, half)
    shares = attend(early, half, [exponents, near, far], late_values, shares)

    guided = shares[0]
    for s in range(1, count):
        guided = guided + exchange(shares[s], s)
    step_size = noise_level(step_now + 1) - noise_level(step_now)
    updated = latent[0] + step_size[:, None, None] * guided
    taken = lax.ppermute(updated, "section", [(0, 1)])
    taking = (section_index == 1) & (arrived_mark > 0.5)
    next_latent = jnp.where(taking[:, None, None], taken, updated)
    return (guided[None], next_latent[None])


def solution(mesh):
    placed = (
        P("section", ("groups", "blk"), "sp", None),
        P("section", ("groups", "blk"), None, "sp", None),
        P("section", ("groups", "blk"), None, "sp", None),
        P("section", ("groups", "blk"), None, "sp", None),
        P("section", None, None),
        P("section", ("groups", "blk")),
        P(("groups", "blk")),
    )
    return jax.shard_map(
        functools.partial(on_device, mesh.shape["sp"]),
        mesh=mesh,
        in_specs=placed,
        out_specs=(
            P("section", ("groups", "blk"), "sp", None),
            P("section", ("groups", "blk"), "sp", None),
        ),
        check_vma=False,
    )
```

time: 109 us -> 101 us (0.927)
  waiting for transfers between devices: 74.3 us -> 46.2 us
  starting transfers between devices: 14.1 us -> 27 us
  Pallas kernels: 10.9 us -> 18.1 us
    ppermute x8 -> x13, waiting for transfers between devices: 73.5 us -> 45.3 us  [exchange(): return lax.ppermute(array, 'sp', [(i, i ^ s) for i in range(count)])]
    ppermute x8 -> x13, starting transfers between devices: 11.5 us -> 24.2 us  [exchange(): return lax.ppermute(array, 'sp', [(i, i ^ s) for i in range(count)])]
    pallas_call x4 -> x10, Pallas kernels: 10.9 us -> 18.1 us  [the longest x2 4.59 us: score(): call(functools.partial(score_kernel, first, count, group, width), outs, [...]
    unnamed x22 -> x30, local copies, waits for them, and re-layouts: 7.39 us -> 7.08 us
  transfers between devices with their start and end apart: 10 -> 15, of which waited for: 5 -> 8; matrix products, arithmetic and copies ran while one was open for 1% -> 0% of each run, Pallas kernels for 6% -> 15%
where the time goes in v3:
time: 101 us; the launch traced here: 100 us
  waiting for transfers between devices  46.2 us (46%)
  starting transfers between devices  27 us (27%)
  Pallas kernels  18.1 us (18%)
  local copies, waits for them, and re-layouts  7.08 us (7%)
  other arithmetic  1.32 us (1%)
    ppermute x13, waiting for transfers between devices, exchange(): return lax.ppermute(array, 'sp', [(i, i ^ s) for i in range(count)])  45.3 us
    ppermute x13, starting transfers between devices, exchange(): return lax.ppermute(array, 'sp', [(i, i ^ s) for i in range(count)])  24.2 us
    unnamed x30, local copies, waits for them, and re-layouts  7.08 us
    pallas_call x2, Pallas kernels, score(): call(functools.partial(score_kernel, first, count, group, width), outs, [...  4.59 us
    pallas_call x2, Pallas kernels, pack_near(): call(functools.partial(pack_near_kernel, 2 * first, group, width), [shape...  4.27 us
    pallas_call x2, Pallas kernels, pack(): call(functools.partial(pack_kernel, 2 * first, group, width, shifts), [sh...  4.27 us
    pallas_call x2, Pallas kernels, attend(): call(functools.partial(attend_kernel, first, count, group, bool(before)),...  2.91 us
    pallas_call x2, Pallas kernels, project(): call(functools.partial(project_kernel, first, group, width), [shape(many,...  2.02 us
  transfers between devices with their start and end apart: 15, of which 8 were waited for; matrix products, arithmetic and copies ran while one was open for 0% of the time, Pallas kernels for 15%

profile of v3, /device:TPU:0, one launch (start us, length us, event | category | flops | bytes accessed | tf_op | source)
XLA Modules:
  0.0 100.5 jit_solution(11109619368494135816)
XLA Ops:
  0.6 2.3 %pack_near.3 = bf16[4,32,4096]{2,1,0:T(8,128)(2,1)} custom-call(s32[1]{0:T(128)} %bitcast.1.me_ref, bf16[6,32,4096]{2,1,0:T(8,128)(2,1)} %bitcast.15, bf16[6,32,4096]{2,1,0:T(8,128)(2,1)} %bitcast.21), custom_call_target="tpu_custom_call" | custom-call | bytes 2097152 | tf_op jit(solution)/shard_map/pack_near/pallas_call | solution.py:251
  3.0 3.1 %collective-permute-start.5 = (bf16[4,32,4096]{2,1,0:T(8,128)(2,1)}, bf16[4,32,4096]{2,1,0:T(8,128)(2,1)}, u32[]{:S(2)}, u32[]{:S(2)}) collective-permute-start(bf16[4,32,4096]{2,1,0:T(8,128)(2,1)} %pack_near.3), channel_id=1, source_target_pairs={{0,2},{2,0},{4,6},{6,4},{1,3},{3,1},{5,7},{7,5},{8,10},{10,8},{12,... | collective-permute-start | bytes 3145736 | tf_op jit(solution)/shard_map/ppermute | solution.py:235
  6.1 2.3 %pack.2 = (bf16[4,32,2048]{2,1,0:T(8,128)(2,1)}, bf16[4,32,2048]{2,1,0:T(8,128)(2,1)}) custom-call(s32[1]{0:T(128)} %bitcast.1.me_ref, bf16[6,32,4096]{2,1,0:T(8,128)(2,1)} %bitcast.16), custom_call_target="tpu_custom_call" | custom-call | bytes 2097152 | tf_op jit(solution)/shard_map/pack/pallas_call | solution.py:239
  8.4 2.7 %collective-permute-start = (bf16[4,32,2048]{2,1,0:T(8,128)(2,1)}, bf16[4,32,2048]{2,1,0:T(8,128)(2,1)S(1)}, u32[]{:S(2)}, u32[]{:S(2)}) collective-permute-start(bf16[4,32,2048]{2,1,0:T(8,128)(2,1)} %get-tuple-element.26), channel_id=1, source_target_pairs={{0,4},{2,6},{4,0},{6,2},{1,5},{3,7},{5,1},{7,3},{8,12},{10,14},{12... | collective-permute-start | bytes 1572872 | tf_op jit(solution)/shard_map/ppermute | solution.py:235
  11.1 1.9 %pack_near.2 = bf16[2,32,4096]{2,1,0:T(8,128)(2,1)} custom-call(s32[1]{0:T(128)} %bitcast.1.me_ref, bf16[6,32,4096]{2,1,0:T(8,128)(2,1)} %bitcast.17, bf16[6,32,4096]{2,1,0:T(8,128)(2,1)} %bitcast.22), custom_call_target="tpu_custom_call" | custom-call | bytes 1048576 | tf_op jit(solution)/shard_map/pack_near/pallas_call | solution.py:251
  13.0 28.2 %collective-permute-done.refs_1_ = bf16[4,32,2048]{2,1,0:T(8,128)(2,1)S(1)} collective-permute-done((bf16[4,32,2048]{2,1,0:T(8,128)(2,1)}, bf16[4,32,2048]{2,1,0:T(8,128)(2,1)S(1)}, u32[]{:S(2)}, u32[]{:S(2)}) %collective-permute-start) | collective-permute-done | bytes 524320 | tf_op jit(solution)/shard_map/ppermute | solution.py:235
  41.2 0.8 copy-done.6
  42.0 3.4 %collective-permute-start.1 = (bf16[2,32,4096]{2,1,0:T(8,128)(2,1)}, bf16[2,32,4096]{2,1,0:T(8,128)(2,1)}, u32[]{:S(2)}, u32[]{:S(2)}) collective-permute-start(bf16[2,32,4096]{2,1,0:T(8,128)(2,1)} %pack_near.2), channel_id=1, source_target_pairs={{0,2},{2,0},{4,6},{6,4},{1,3},{3,1},{5,7},{7,5},{8,10},{10,8},{12,... | collective-permute-start | bytes 1572872 | tf_op jit(solution)/shard_map/ppermute | solution.py:235
  45.5 1.6 %collective-permute-start.7 = (f32[3]{0:T(128)S(1)}, f32[3]{0:T(128)S(1)}, u32[]{:S(2)}, u32[]{:S(2)}) collective-permute-start(f32[3]{0:T(128)S(1)} %get-tuple-element.52), channel_id=1, source_target_pairs={{0,8},{1,9},{2,10},{3,11},{4,12},{5,13},{6,14},{7,15},{16,24},{17,... | collective-permute-start | bytes 44 | tf_op jit(solution)/shard_map/ppermute | solution.py:335
  47.1 1.9 %pack.3 = (bf16[2,32,2048]{2,1,0:T(8,128)(2,1)}, bf16[2,32,2048]{2,1,0:T(8,128)(2,1)}) custom-call(s32[1]{0:T(128)} %bitcast.1.me_ref, bf16[6,32,4096]{2,1,0:T(8,128)(2,1)} %bitcast.18), custom_call_target="tpu_custom_call" | custom-call | bytes 1048576 | tf_op jit(solution)/shard_map/pack/pallas_call | solution.py:239
  49.1 1.4 %copy-done.2 = bf16[1,3,2,32,4096]{4,3,2,1,0:T(8,128)(2,1)S(1)} copy-done((bf16[1,3,2,32,4096]{4,3,2,1,0:T(8,128)(2,1)S(1)}, bf16[1,3,2,32,4096]{4,3,2,1,0:T(8,128)(2,1)}, u32[]{:S(2)}) %copy-start.2) | copy-done | bytes 1572888
  50.5 1.0 %copy-done.4 = bf16[1,64,4096]{2,1,0:T(8,128)(2,1)S(1)} copy-done((bf16[1,64,4096]{2,1,0:T(8,128)(2,1)S(1)}, bf16[1,64,4096]{2,1,0:T(8,128)(2,1)}, u32[]{:S(2)}) %copy-start.4) | copy-done | bytes 524312
  51.5 1.5 %project.3 = (bf16[2,8,64,128]{3,2,1,0:T(8,128)(2,1)S(1)}, bf16[2,8,64,128]{3,2,1,0:T(8,128)(2,1)}) custom-call(s32[1]{0:T(128)} %bitcast.1.me_ref, bf16[6,32,4096]{2,1,0:T(8,128)(2,1)S(1)} %bitcast.25, bf16[64,4096]{1,0:T(8,128)(2,1)S(1)} %bitcast.27), custom_call_target="tpu_custom_call" | custom-call | flops 268435456 | bytes 1572864 | tf_op jit(solution)/shard_map/project/pallas_call | solution.py:263
  53.1 2.3 %collective-permute-start.3 = (bf16[2,32,2048]{2,1,0:T(8,128)(2,1)}, bf16[2,32,2048]{2,1,0:T(8,128)(2,1)}, u32[]{:S(2)}, u32[]{:S(2)}) collective-permute-start(bf16[2,32,2048]{2,1,0:T(8,128)(2,1)} %get-tuple-element.29), channel_id=1, source_target_pairs={{0,6},{2,4},{4,2},{6,0},{1,7},{3,5},{5,3},{7,1},{8,14},{10,12},{12... | collective-permute-start | bytes 786440 | tf_op jit(solution)/shard_map/ppermute | solution.py:235
  55.4 3.4 %collective-permute-start.10 = (bf16[2,8,64,128]{3,2,1,0:T(8,128)(2,1)}, bf16[2,8,64,128]{3,2,1,0:T(8,128)(2,1)}, u32[]{:S(2)}, u32[]{:S(2)}) collective-permute-start(bf16[2,8,64,128]{3,2,1,0:T(8,128)(2,1)} %get-tuple-element.41), channel_id=1, source_target_pairs={{0,2},{2,0},{4,6},{6,4},{1,3},{3,1},{5,7},{7,5},{8,10},{10,8},{12,... | collective-permute-start | bytes 786440 | tf_op jit(solution)/shard_map/ppermute | solution.py:235
  58.8 2.8 %score.3 = (f32[4,8,128,128]{3,2,1,0:T(8,128)S(1)}, f32[4,2,16,128]{3,2,1,0:T(8,128)S(1)}) custom-call(s32[1]{0:T(128)} %bitcast.1.me_ref, bf16[6,32,4096]{2,1,0:T(8,128)(2,1)S(1)} %bitcast.19, bf16[6,32,4096]{2,1,0:T(8,128)(2,1)S(1)} %bitcast.23, bf16[4,32,4096]{2,1,0:T(8,128)(2,1)} %collective-permute-done.5.refs_0_, bf16[4,32,2048]{2,1,0:T(8,128)(2,1)S(1)} %copy-done.7, ...), custom_call_target="tpu_custom_call" | custom-call | flops 1073741824 | bytes 4194304 | tf_op jit(solution)/shard_map/score/pallas_call | solution.py:283
  61.6 1.4 %copy-done.8 = f32[4,8,128,128]{3,2,1,0:T(8,128)} copy-done((f32[4,8,128,128]{3,2,1,0:T(8,128)}, f32[4,8,128,128]{3,2,1,0:T(8,128)S(1)}, u32[]{:S(2)}) %copy-start.8) | copy-done | bytes 2097176
  63.0 1.0 %collective-permute-start.9 = (f32[4,2,16,128]{3,2,1,0:T(8,128)S(1)}, f32[4,2,16,128]{3,2,1,0:T(8,128)S(1)}, u32[]{:S(2)}, u32[]{:S(2)}) collective-permute-start(f32[4,2,16,128]{3,2,1,0:T(8,128)S(1)} %get-tuple-element.38.refs_1_), channel_id=1, source_target_pairs={{0,4},{2,6},{4,0},{6,2},{1,5},{3,7},{5,1},{7,3},{8,12},{10,14},{12... | collective-permute-start | bytes 196616 | tf_op jit(solution)/shard_map/ppermute | solution.py:235
  64.0 1.4 %copy-done.3 = bf16[1,3,2,32,4096]{4,3,2,1,0:T(8,128)(2,1)S(1)} copy-done((bf16[1,3,2,32,4096]{4,3,2,1,0:T(8,128)(2,1)S(1)}, bf16[1,3,2,32,4096]{4,3,2,1,0:T(8,128)(2,1)}, u32[]{:S(2)}) %copy-start.3) | copy-done | bytes 1572888
  65.4 1.0 %copy-done.5 = bf16[1,64,4096]{2,1,0:T(8,128)(2,1)S(1)} copy-done((bf16[1,64,4096]{2,1,0:T(8,128)(2,1)S(1)}, bf16[1,64,4096]{2,1,0:T(8,128)(2,1)}, u32[]{:S(2)}) %copy-start.5) | copy-done | bytes 524312
  67.0 2.4 %collective-permute-done.2.refs_1_ = bf16[2,32,2048]{2,1,0:T(8,128)(2,1)S(1)} collective-permute-done((bf16[2,32,2048]{2,1,0:T(8,128)(2,1)}, bf16[2,32,2048]{2,1,0:T(8,128)(2,1)S(1)}, u32[]{:S(2)}, u32[]{:S(2)}) %collective-permute-start.2) | collective-permute-done | bytes 262176 | tf_op jit(solution)/shard_map/ppermute | solution.py:235
  69.4 8.6 %collective-permute-done.3.refs_2_ = bf16[2,32,2048]{2,1,0:T(8,128)(2,1)} collective-permute-done((bf16[2,32,2048]{2,1,0:T(8,128)(2,1)}, bf16[2,32,2048]{2,1,0:T(8,128)(2,1)}, u32[]{:S(2)}, u32[]{:S(2)}) %collective-permute-start.3) | collective-permute-done | bytes 262176 | tf_op jit(solution)/shard_map/ppermute | solution.py:235
  78.0 1.8 %score.2 = (f32[2,8,128,128]{3,2,1,0:T(8,128)S(1)}, f32[2,2,16,128]{3,2,1,0:T(8,128)S(1)}) custom-call(s32[1]{0:T(128)} %bitcast.1.me_ref, bf16[6,32,4096]{2,1,0:T(8,128)(2,1)S(1)} %bitcast.20, bf16[6,32,4096]{2,1,0:T(8,128)(2,1)S(1)} %bitcast.24, bf16[2,32,4096]{2,1,0:T(8,128)(2,1)} %collective-permute-done.1.refs_0_, ...), custom_call_target="tpu_custom_call" | custom-call | flops 536870912 | bytes 2097152 | tf_op jit(solution)/shard_map/score/pallas_call | solution.py:283
  79.8 3.7 %collective-permute-start.4 = (f32[2,2,16,128]{3,2,1,0:T(8,128)S(1)}, f32[2,2,16,128]{3,2,1,0:T(8,128)S(1)}, u32[]{:S(2)}, u32[]{:S(2)}) collective-permute-start(f32[2,2,16,128]{3,2,1,0:T(8,128)S(1)} %get-tuple-element.31.refs_1_), channel_id=1, source_target_pairs={{0,4},{2,6},{4,0},{6,2},{1,5},{3,7},{5,1},{7,3},{8,12},{10,14},{12... | collective-permute-start | bytes 98312 | tf_op jit(solution)/shard_map/ppermute | solution.py:235
  84.2 1.9 %attend.2 = (f32[2,16,128]{2,1,0:T(8,128)S(1)}, f32[2,16,128]{2,1,0:T(8,128)S(1)}, f32[2,16,128]{2,1,0:T(8,128)S(1)}, f32[2,16,128]{2,1,0:T(8,128)S(1)}) custom-call(f32[1]{0:T(128)} %bitcast.scale_ref, s32[3]{0:T(128)S(1)} %broadcast_select_fusion.skip_ref, f32[4,8,128,128]{3,2,1,0:T(8,128)S(1)} %copy-done.9, ...), custom_call_target="tpu_custom_call" | custom-call | flops 2147483648 | bytes 2097152 | tf_op jit(solution)/shard_map/attend/pallas_call | solution.py:298
  86.2 2.3 %collective-permute-done.6.refs_4_ = bf16[1,8,64,128]{3,2,1,0:T(8,128)(2,1)S(1)} collective-permute-done((bf16[1,8,64,128]{3,2,1,0:T(8,128)(2,1)S(1)}, bf16[1,8,64,128]{3,2,1,0:T(8,128)(2,1)S(1)}, u32[]{:S(2)}, u32[]{:S(2)}) %collective-permute-start.6) | collective-permute-done | bytes 131104 | tf_op jit(solution)/shard_map/ppermute | solution.py:235
  88.5 1.0 attend.3
  89.9 1.5 %collective-permute-start.12 = (f32[3,16,128]{2,1,0:T(8,128)S(1)}, f32[3,16,128]{2,1,0:T(8,128)S(1)}, u32[]{:S(2)}, u32[]{:S(2)}) collective-permute-start(f32[3,16,128]{2,1,0:T(8,128)S(1)} %get-tuple-element.48), channel_id=1, source_target_pairs={{0,4},{2,6},{4,0},{6,2},{1,5},{3,7},{5,1},{7,3},{8,12},{10,14},{12... | collective-permute-start | bytes 73736 | tf_op jit(solution)/shard_map/ppermute | solution.py:235
  91.4 2.5 %collective-permute-start.13 = (f32[3,16,128]{2,1,0:T(8,128)S(1)}, f32[3,16,128]{2,1,0:T(8,128)S(1)}, u32[]{:S(2)}, u32[]{:S(2)}) collective-permute-start(f32[3,16,128]{2,1,0:T(8,128)S(1)} %get-tuple-element.49), channel_id=1, source_target_pairs={{0,6},{2,4},{4,2},{6,0},{1,7},{3,5},{5,3},{7,1},{8,14},{10,12},{12... | collective-permute-start | bytes 73736 | tf_op jit(solution)/shard_map/ppermute | solution.py:235
  94.6 2.4 %collective-permute-done.13 = f32[3,16,128]{2,1,0:T(8,128)S(1)} collective-permute-done((f32[3,16,128]{2,1,0:T(8,128)S(1)}, f32[3,16,128]{2,1,0:T(8,128)S(1)}, u32[]{:S(2)}, u32[]{:S(2)}) %collective-permute-start.13) | collective-permute-done | bytes 24608 | tf_op jit(solution)/shard_map/ppermute | solution.py:235
  97.7 1.3 %collective-permute-start.14 = (f32[3,16,128]{2,1,0:T(8,128)S(1)}, f32[3,16,128]{2,1,0:T(8,128)S(1)}, u32[]{:S(2)}, u32[]{:S(2)}) collective-permute-start(f32[3,16,128]{2,1,0:T(8,128)S(1)} %get-tuple-element.50), channel_id=1, source_target_pairs={{0,8},{1,9},{2,10},{3,11},{4,12},{5,13},{6,14},{7,15},{16,24},{17,... | collective-permute-start | bytes 73736 | tf_op jit(solution)/shard_map/ppermute | solution.py:349
  99.0 0.8 collective-permute-done.14
  (43 shorter events, 3.8 us)
Async XLA Ops:
  3.0 55.9 %collective-permute-start.5 = (bf16[4,32,4096]{2,1,0:T(8,128)(2,1)}, bf16[4,32,4096]{2,1,0:T(8,128)(2,1)}, u32[]{:S(2)}, u32[]{:S(2)}) collective-permute-start(bf16[4,32,4096]{2,1,0:T(8,128)(2,1)} %pack_near.3), channel_id=1, source_target_pairs={{0,2},{2,0},{4,6},{6,4},{1,3},{3,1},{5,7},{7,5},{8,10},{10,8},{12,... | collective-permute-start | bytes 3145736 | tf_op jit(solution)/shard_map/ppermute | solution.py:235
  8.4 32.8 %collective-permute-start = (bf16[4,32,2048]{2,1,0:T(8,128)(2,1)}, bf16[4,32,2048]{2,1,0:T(8,128)(2,1)S(1)}, u32[]{:S(2)}, u32[]{:S(2)}) collective-permute-start(bf16[4,32,2048]{2,1,0:T(8,128)(2,1)} %get-tuple-element.26), channel_id=1, source_target_pairs={{0,4},{2,6},{4,0},{6,2},{1,5},{3,7},{5,1},{7,3},{8,12},{10,14},{12... | collective-permute-start | bytes 1572872 | tf_op jit(solution)/shard_map/ppermute | solution.py:235
  11.1 44.4 %collective-permute-start.8 = (bf16[4,32,2048]{2,1,0:T(8,128)(2,1)}, bf16[4,32,2048]{2,1,0:T(8,128)(2,1)}, u32[]{:S(2)}, u32[]{:S(2)}) collective-permute-start(bf16[4,32,2048]{2,1,0:T(8,128)(2,1)} %get-tuple-element.36), channel_id=1, source_target_pairs={{0,6},{2,4},{4,2},{6,0},{1,7},{3,5},{5,3},{7,1},{8,14},{10,12},{12... | collective-permute-start | bytes 1572872 | tf_op jit(solution)/shard_map/ppermute | solution.py:235
  11.1 34.4 %copy-start.13 = (s32[1,3]{1,0:T(1,128)S(1)}, s32[1,3]{1,0:T(1,128)}, u32[]{:S(2)}) copy-start(s32[1,3]{1,0:T(1,128)} %param.12) | copy-start | bytes 40
  41.2 0.8 copy-start.6
  42.0 36.0 %collective-permute-start.1 = (bf16[2,32,4096]{2,1,0:T(8,128)(2,1)}, bf16[2,32,4096]{2,1,0:T(8,128)(2,1)}, u32[]{:S(2)}, u32[]{:S(2)}) collective-permute-start(bf16[2,32,4096]{2,1,0:T(8,128)(2,1)} %pack_near.2), channel_id=1, source_target_pairs={{0,2},{2,0},{4,6},{6,4},{1,3},{3,1},{5,7},{7,5},{8,10},{10,8},{12,... | collective-permute-start | bytes 1572872 | tf_op jit(solution)/shard_map/ppermute | solution.py:235
  45.5 13.3 %copy-start = (bf16[1,3,2,32,4096]{4,3,2,1,0:T(8,128)(2,1)S(1)}, bf16[1,3,2,32,4096]{4,3,2,1,0:T(8,128)(2,1)}, u32[]{:S(2)}) copy-start(bf16[1,3,2,32,4096]{4,3,2,1,0:T(8,128)(2,1)} %param.8) | copy-start | bytes 4718596
  45.5 13.3 %copy-start.1 = (bf16[1,3,2,32,4096]{4,3,2,1,0:T(8,128)(2,1)S(1)}, bf16[1,3,2,32,4096]{4,3,2,1,0:T(8,128)(2,1)}, u32[]{:S(2)}) copy-start(bf16[1,3,2,32,4096]{4,3,2,1,0:T(8,128)(2,1)} %param.9) | copy-start | bytes 4718596
  45.5 7.6 %collective-permute-start.7 = (f32[3]{0:T(128)S(1)}, f32[3]{0:T(128)S(1)}, u32[]{:S(2)}, u32[]{:S(2)}) collective-permute-start(f32[3]{0:T(128)S(1)} %get-tuple-element.52), channel_id=1, source_target_pairs={{0,8},{1,9},{2,10},{3,11},{4,12},{5,13},{6,14},{7,15},{16,24},{17,... | collective-permute-start | bytes 44 | tf_op jit(solution)/shard_map/ppermute | solution.py:335
  49.0 20.4 %collective-permute-start.2 = (bf16[2,32,2048]{2,1,0:T(8,128)(2,1)}, bf16[2,32,2048]{2,1,0:T(8,128)(2,1)S(1)}, u32[]{:S(2)}, u32[]{:S(2)}) collective-permute-start(bf16[2,32,2048]{2,1,0:T(8,128)(2,1)} %get-tuple-element.28), channel_id=1, source_target_pairs={{0,4},{2,6},{4,0},{6,2},{1,5},{3,7},{5,1},{7,3},{8,12},{10,14},{12... | collective-permute-start | bytes 786440 | tf_op jit(solution)/shard_map/ppermute | solution.py:235
  49.1 1.4 %copy-start.2 = (bf16[1,3,2,32,4096]{4,3,2,1,0:T(8,128)(2,1)S(1)}, bf16[1,3,2,32,4096]{4,3,2,1,0:T(8,128)(2,1)}, u32[]{:S(2)}) copy-start(bf16[1,3,2,32,4096]{4,3,2,1,0:T(8,128)(2,1)} %param.10) | copy-start | bytes 4718596
  50.5 1.0 %copy-start.4 = (bf16[1,64,4096]{2,1,0:T(8,128)(2,1)S(1)}, bf16[1,64,4096]{2,1,0:T(8,128)(2,1)}, u32[]{:S(2)}) copy-start(bf16[1,64,4096]{2,1,0:T(8,128)(2,1)} %param.11) | copy-start | bytes 1572868
  51.5 7.3 %copy-start.7 = (bf16[4,32,2048]{2,1,0:T(8,128)(2,1)S(1)}, bf16[4,32,2048]{2,1,0:T(8,128)(2,1)}, u32[]{:S(2)}) copy-start(bf16[4,32,2048]{2,1,0:T(8,128)(2,1)} %copy-done.6) | copy-start | bytes 1572868
  53.1 8.6 %copy-start.10 = (bf16[2,8,64,128]{3,2,1,0:T(8,128)(2,1)}, bf16[2,8,64,128]{3,2,1,0:T(8,128)(2,1)S(1)}, u32[]{:S(2)}) copy-start(bf16[2,8,64,128]{3,2,1,0:T(8,128)(2,1)S(1)} %get-tuple-element.39.refs_3_) | copy-start | bytes 786436
  53.1 24.9 %collective-permute-start.3 = (bf16[2,32,2048]{2,1,0:T(8,128)(2,1)}, bf16[2,32,2048]{2,1,0:T(8,128)(2,1)}, u32[]{:S(2)}, u32[]{:S(2)}) collective-permute-start(bf16[2,32,2048]{2,1,0:T(8,128)(2,1)} %get-tuple-element.29), channel_id=1, source_target_pairs={{0,6},{2,4},{4,2},{6,0},{1,7},{3,5},{5,3},{7,1},{8,14},{10,12},{12... | collective-permute-start | bytes 786440 | tf_op jit(solution)/shard_map/ppermute | solution.py:235
  55.4 8.6 %copy-start.14 = (s32[3]{0:T(128)S(1)}, s32[3]{0:T(128)}, u32[]{:S(2)}) copy-start(s32[3]{0:T(128)} %param.13) | copy-start | bytes 40
  55.4 28.8 %collective-permute-start.10 = (bf16[2,8,64,128]{3,2,1,0:T(8,128)(2,1)}, bf16[2,8,64,128]{3,2,1,0:T(8,128)(2,1)}, u32[]{:S(2)}, u32[]{:S(2)}) collective-permute-start(bf16[2,8,64,128]{3,2,1,0:T(8,128)(2,1)} %get-tuple-element.41), channel_id=1, source_target_pairs={{0,2},{2,0},{4,6},{6,4},{1,3},{3,1},{5,7},{7,5},{8,10},{10,8},{12,... | collective-permute-start | bytes 786440 | tf_op jit(solution)/shard_map/ppermute | solution.py:235
  61.6 1.4 %copy-start.8 = (f32[4,8,128,128]{3,2,1,0:T(8,128)}, f32[4,8,128,128]{3,2,1,0:T(8,128)S(1)}, u32[]{:S(2)}) copy-start(f32[4,8,128,128]{3,2,1,0:T(8,128)S(1)} %get-tuple-element.37.refs_0_) | copy-start | bytes 6291460
  63.0 21.2 %collective-permute-start.9 = (f32[4,2,16,128]{3,2,1,0:T(8,128)S(1)}, f32[4,2,16,128]{3,2,1,0:T(8,128)S(1)}, u32[]{:S(2)}, u32[]{:S(2)}) collective-permute-start(f32[4,2,16,128]{3,2,1,0:T(8,128)S(1)} %get-tuple-element.38.refs_1_), channel_id=1, source_target_pairs={{0,4},{2,6},{4,0},{6,2},{1,5},{3,7},{5,1},{7,3},{8,12},{10,14},{12... | collective-permute-start | bytes 196616 | tf_op jit(solution)/shard_map/ppermute | solution.py:235
  64.0 1.4 %copy-start.3 = (bf16[1,3,2,32,4096]{4,3,2,1,0:T(8,128)(2,1)S(1)}, bf16[1,3,2,32,4096]{4,3,2,1,0:T(8,128)(2,1)}, u32[]{:S(2)}) copy-start(bf16[1,3,2,32,4096]{4,3,2,1,0:T(8,128)(2,1)} %param.10) | copy-start | bytes 4718596
  65.4 1.0 %copy-start.5 = (bf16[1,64,4096]{2,1,0:T(8,128)(2,1)S(1)}, bf16[1,64,4096]{2,1,0:T(8,128)(2,1)}, u32[]{:S(2)}) copy-start(bf16[1,64,4096]{2,1,0:T(8,128)(2,1)} %param.11) | copy-start | bytes 1572868
  67.0 17.3 %copy-start.9 = (f32[4,8,128,128]{3,2,1,0:T(8,128)S(1)}, f32[4,8,128,128]{3,2,1,0:T(8,128)}, u32[]{:S(2)}) copy-start(f32[4,8,128,128]{3,2,1,0:T(8,128)} %copy-done.8) | copy-start | bytes 6291460
  67.0 17.3 %copy-start.11 = (bf16[2,8,64,128]{3,2,1,0:T(8,128)(2,1)S(1)}, bf16[2,8,64,128]{3,2,1,0:T(8,128)(2,1)}, u32[]{:S(2)}) copy-start(bf16[2,8,64,128]{3,2,1,0:T(8,128)(2,1)} %copy-done.10) | copy-start | bytes 786436
  79.8 6.3 %collective-permute-start.4 = (f32[2,2,16,128]{3,2,1,0:T(8,128)S(1)}, f32[2,2,16,128]{3,2,1,0:T(8,128)S(1)}, u32[]{:S(2)}, u32[]{:S(2)}) collective-permute-start(f32[2,2,16,128]{3,2,1,0:T(8,128)S(1)} %get-tuple-element.31.refs_1_), channel_id=1, source_target_pairs={{0,4},{2,6},{4,0},{6,2},{1,5},{3,7},{5,1},{7,3},{8,12},{10,14},{12... | collective-permute-start | bytes 98312 | tf_op jit(solution)/shard_map/ppermute | solution.py:235
  83.5 5.0 %collective-permute-start.6 = (bf16[1,8,64,128]{3,2,1,0:T(8,128)(2,1)S(1)}, bf16[1,8,64,128]{3,2,1,0:T(8,128)(2,1)S(1)}, u32[]{:S(2)}, u32[]{:S(2)}) collective-permute-start(bf16[1,8,64,128]{3,2,1,0:T(8,128)(2,1)S(1)} %get-tuple-element.34), channel_id=1, source_target_pairs={{0,2},{2,0},{4,6},{6,4},{1,3},{3,1},{5,7},{7,5},{8,10},{10,8},{12,... | collective-permute-start | bytes 393224 | tf_op jit(solution)/shard_map/ppermute | solution.py:235
  88.5 8.6 %copy-start.12 = (f32[1,3,16,128]{3,2,1,0:T(8,128)S(1)}, f32[1,3,16,128]{3,2,1,0:T(8,128)}, u32[]{:S(2)}) copy-start(f32[1,3,16,128]{3,2,1,0:T(8,128)} %param.7) | copy-start | bytes 73732
  89.5 4.5 %collective-permute-start.11 = (f32[3,16,128]{2,1,0:T(8,128)S(1)}, f32[3,16,128]{2,1,0:T(8,128)S(1)}, u32[]{:S(2)}, u32[]{:S(2)}) collective-permute-start(f32[3,16,128]{2,1,0:T(8,128)S(1)} %get-tuple-element.47), channel_id=1, source_target_pairs={{0,2},{2,0},{4,6},{6,4},{1,3},{3,1},{5,7},{7,5},{8,10},{10,8},{12,... | collective-permute-start | bytes 73736 | tf_op jit(solution)/shard_map/ppermute | solution.py:235
  89.9 4.7 %collective-permute-start.12 = (f32[3,16,128]{2,1,0:T(8,128)S(1)}, f32[3,16,128]{2,1,0:T(8,128)S(1)}, u32[]{:S(2)}, u32[]{:S(2)}) collective-permute-start(f32[3,16,128]{2,1,0:T(8,128)S(1)} %get-tuple-element.48), channel_id=1, source_target_pairs={{0,4},{2,6},{4,0},{6,2},{1,5},{3,7},{5,1},{7,3},{8,12},{10,14},{12... | collective-permute-start | bytes 73736 | tf_op jit(solution)/shard_map/ppermute | solution.py:235
  91.4 5.6 %collective-permute-start.13 = (f32[3,16,128]{2,1,0:T(8,128)S(1)}, f32[3,16,128]{2,1,0:T(8,128)S(1)}, u32[]{:S(2)}, u32[]{:S(2)}) collective-permute-start(f32[3,16,128]{2,1,0:T(8,128)S(1)} %get-tuple-element.49), channel_id=1, source_target_pairs={{0,6},{2,4},{4,2},{6,0},{1,7},{3,5},{5,3},{7,1},{8,14},{10,12},{12... | collective-permute-start | bytes 73736 | tf_op jit(solution)/shard_map/ppermute | solution.py:235
  97.7 2.1 %collective-permute-start.14 = (f32[3,16,128]{2,1,0:T(8,128)S(1)}, f32[3,16,128]{2,1,0:T(8,128)S(1)}, u32[]{:S(2)}, u32[]{:S(2)}) collective-permute-start(f32[3,16,128]{2,1,0:T(8,128)S(1)} %get-tuple-element.50), channel_id=1, source_target_pairs={{0,8},{1,9},{2,10},{3,11},{4,12},{5,13},{6,14},{7,15},{16,24},{17,... | collective-permute-start | bytes 73736 | tf_op jit(solution)/shard_map/ppermute | solution.py:349

commit v4 on v3

v4 whole, which is shorter than its diff:
```python
import functools

import jax
import jax.numpy as jnp
from jax import lax
from jax.experimental import pallas as pl
from jax.experimental.pallas import tpu as pltpu
from jax.sharding import PartitionSpec as P

HD = 128
CH = 64
STEPS = 40
SWITCH = 25


noise_shift = 12.0
high_guidance = 4.0
low_guidance = 3.0

VMEM = pl.BlockSpec(memory_space=pltpu.VMEM)
SMEM = pl.BlockSpec(memory_space=pltpu.SMEM)
HBM = pl.BlockSpec(memory_space=pltpu.HBM)
PAIR = 2 * HD


def noise_level(step_now):
    fraction = 1.0 - step_now.astype(jnp.float32) / STEPS
    return noise_shift * fraction / (1.0 + (noise_shift - 1.0) * fraction)


def dot_last(left, right):
    return lax.dot_general(
        left, right, (((1,), (1,)), ((), ())), preferred_element_type=jnp.float32
    )


def side_by_side(first, second):
    zero = jnp.zeros_like(first)
    return [
        jnp.concatenate([first, zero], axis=1),
        jnp.concatenate([zero, second], axis=1),
    ]


def through(moves, staged, sems_in, sems_out):
    inward = [
        pltpu.make_async_copy(source, staged.at[n], sems_in.at[n])
        for n, (source, _) in enumerate(moves)
    ]
    outward = [
        pltpu.make_async_copy(staged.at[n], target, sems_out.at[n])
        for n, (_, target) in enumerate(moves)
    ]
    for copy in inward:
        copy.start()
    for before, copy in zip(inward, outward):
        before.wait()
        copy.start()
    for copy in outward:
        copy.wait()


def pack_kernel(first, group, width, me_ref, q_ref, k_ref, *refs):
    out_refs, scratch = refs[:-3], refs[-3:]
    moves = []
    for s, out_ref in enumerate(out_refs, 1):
        start = pl.multiple_of(((me_ref[0] ^ s) & (group - 1)) * width, width)
        for n, ref in enumerate([q_ref, k_ref] if s < group else [q_ref]):
            for i in range(out_ref.shape[0]):
                moves.append(
                    (
                        ref.at[first + i, :, pl.ds(start, width)],
                        out_ref.at[i, :, pl.ds(n * width, width)],
                    )
                )
    through(moves, *scratch)


def project_kernel(first, group, width, me_ref, v_ref, w_ref, *out_refs):
    me = me_ref[0]
    videos = out_refs[0].shape[0]
    for s in range(group):
        lane = ((me ^ s) & (group - 1)) * width
        for p in range(width // PAIR):
            start = pl.multiple_of(lane + p * PAIR, PAIR)
            weight = w_ref[:, pl.ds(start, PAIR)]
            for v in range(videos):
                rows = []
                for way in range(2):
                    value = v_ref[2 * (first + v) + way, :, pl.ds(start, PAIR)]
                    rows += side_by_side(value[:, :HD], value[:, HD:])
                product = dot_last(weight, jnp.concatenate(rows, axis=0)).astype(jnp.bfloat16)
                half = product.shape[1] // 2
                for way in range(2):
                    out_refs[s][v, way, p // 2, :, (p % 2) * half : (p % 2 + 1) * half] = product[
                        :, way * half : (way + 1) * half
                    ]


def score_kernel(first, count, group, width, me_ref, q_ref, k_ref, *refs):
    others, outs = refs[: count - 1], refs[count - 1 :]
    whole = group == count
    lane = (me_ref[0] & (group - 1)) * width
    rows = q_ref.shape[1]
    items = outs[0].shape[0]

    def one(i, carry):
        for p in range(width // PAIR):
            own = pl.ds(pl.multiple_of(lane + p * PAIR, PAIR), PAIR)
            here = slice(p * PAIR, (p + 1) * PAIR)
            query = jnp.concatenate(
                [q_ref[2 * first + i, :, own]] + [r[i, :, here] for r in others], axis=0
            )
            keys = []
            for s in range(group):
                if s == 0:
                    key = k_ref[2 * first + i, :, own]
                else:
                    key = others[s - 1][i, :, width + p * PAIR : width + (p + 1) * PAIR]
                keys += side_by_side(key[:, :HD], key[:, HD:])
            scores = dot_last(jnp.concatenate(keys, axis=0), query) * (HD ** (-0.5))
            for h in range(2):
                places = [slice((2 * s + h) * rows, (2 * s + h + 1) * rows) for s in range(group)]
                top = functools.reduce(jnp.maximum, [scores[place] for place in places])
                top = jnp.max(top, axis=0, keepdims=True)
                exponents = [jnp.exp(scores[place] - top) for place in places]
                total = jnp.sum(
                    functools.reduce(jnp.add, exponents), axis=0, keepdims=True
                )
                if whole:
                    share = 1.0 / total
                    exponents = [(e * share).astype(jnp.bfloat16) for e in exponents]
                else:
                    outs[1][i, 2 * p + h : 2 * p + h + 1, :] = top
                    outs[2][i, 2 * p + h : 2 * p + h + 1, :] = top + jnp.log(total)
                row = (2 * (p % 2) + h) * rows
                for s, e in enumerate(exponents):
                    outs[0][i, p // 2, s, row : row + rows, :] = e
        return carry

    lax.fori_loop(0, items, one, 0)


def factors(i, top_ref, near_ref, far_ref):
    far = pltpu.roll(far_ref[i], far_ref.shape[2] // 2, 1)
    near = near_ref[i]
    most = jnp.maximum(near, far)
    return jnp.exp(top_ref[i] - most - jnp.log(jnp.exp(near - most) + jnp.exp(far - most)))


def weigh(i, group, e_ref, top_ref, near_ref, far_ref):
    factor = factors(i, top_ref, near_ref, far_ref)
    rows = e_ref.shape[3] // 4
    parts = []
    for q in range(e_ref.shape[1]):
        for s in range(group):
            for h in range(4):
                e = e_ref[i, q, s, h * rows : (h + 1) * rows, :]
                parts.append((e * factor[4 * q + h : 4 * q + h + 1]).astype(jnp.bfloat16))
    return jnp.concatenate(parts, axis=0)


def weigh_kernel(group, e_ref, top_ref, near_ref, far_ref, out_ref):
    def one(i, carry):
        out_ref[i] = weigh(i, group, e_ref, top_ref, near_ref, far_ref)
        return carry

    lax.fori_loop(0, e_ref.shape[0], one, 0)


def attend_kernel(first, count, group, parts, scale_ref, skip_ref, *refs):
    weight_refs, refs = refs[:parts], refs[parts:]
    vw_refs, refs = refs[:group], refs[group:]
    before_refs, out_refs, scratch = refs[: -count - 1], refs[-count - 1 : -1], refs[-1]
    items = weight_refs[0].shape[0]
    quads, _, columns = vw_refs[0].shape[2:]
    rows = columns // 4
    length = rows * count
    offset = first if before_refs else 0

    def one(v, carry):
        sums = []
        for way in range(2):
            i = 2 * v + way
            if parts > 1:
                weights = weigh(i, group, *weight_refs)
            else:
                weights = weight_refs[0][i]
            values = [r[v, way, q] for q in range(quads) for r in vw_refs]
            sums.append(
                jnp.dot(
                    jnp.concatenate(values, axis=1), weights, preferred_element_type=jnp.float32
                )
            )
        conditional, unconditional = sums
        guided = unconditional + scale_ref[0] * (conditional - unconditional)
        guided = jnp.where(skip_ref[first + v] == 1, conditional, guided)
        scratch[...] = jnp.concatenate([guided, guided], axis=0).T
        even = scratch[pl.ds(0, length // 2, stride=2), :]
        odd = scratch[pl.ds(1, length // 2, stride=2), :]
        column = lax.broadcasted_iota(jnp.int32, even.shape, 1)
        both = jnp.where(column < CH, even, odd)
        for s in range(count):
            out_refs[s][offset + v] = both[s * rows // 2 : (s + 1) * rows // 2]
        return carry

    lax.fori_loop(0, items // 2, one, 0)
    for before_ref, out_ref in zip(before_refs, out_refs):
        out_ref[0:first] = before_ref[...]


def call(kernel, outs, specs, name, scratch=(), flops=0, moved=0, space=VMEM, limit=16 << 20):
    return pl.pallas_call(
        kernel,
        out_shape=outs,
        in_specs=specs,
        out_specs=space if isinstance(space, list) else jax.tree.map(lambda _: space, outs),
        scratch_shapes=scratch,
        name=name,
        compiler_params=pltpu.CompilerParams(vmem_limit_bytes=limit),
        cost_estimate=pl.CostEstimate(flops=flops, bytes_accessed=moved, transcendentals=0),
    )


def after(array, *others):
    return lax.optimization_barrier((array, *others))[0]


def shape(*dims, dtype=jnp.bfloat16):
    return jax.ShapeDtypeStruct(dims, dtype)


def on_device(count, latent, queries, keys, values, head_weight, step_index, skip_flags):
    section_index = lax.axis_index("section")
    me = lax.axis_index("sp")[None]
    _, videos, _, rows, feature_all = queries.shape
    items = videos * 2
    length = rows * count
    query = queries[0].reshape(items, rows, feature_all)
    key = keys[0].reshape(items, rows, feature_all)
    value = values[0].reshape(items, rows, feature_all)
    late = max(1, videos // 3)
    early = videos - late

    def exchange(array, s):
        return lax.ppermute(array, "sp", [(i, i ^ s) for i in range(count)])

    def staging(number, width):
        return [
            pltpu.VMEM((number, rows, width), jnp.bfloat16),
            pltpu.SemaphoreType.DMA((number,)),
            pltpu.SemaphoreType.DMA((number,)),
        ]

    def pack(me, first, many, group):
        width = feature_all // group
        wide = [(2 if s < group else 1) * width for s in range(1, count)]
        return call(
            functools.partial(pack_kernel, 2 * first, group, width),
            [shape(2 * many, rows, w) for w in wide],
            [SMEM, HBM, HBM],
            "pack",
            scratch=staging(2 * many * (count + group - 2), width),
            moved=8 * many * rows * sum(wide),
            space=HBM,
            limit=None,
        )(me, query, key)

    def project(me, first, many, group):
        width = feature_all // group
        return call(
            functools.partial(project_kernel, first, group, width),
            [shape(many, 2, width // (2 * PAIR), CH, 4 * rows)] * group,
            [SMEM, VMEM, VMEM],
            "project",
            flops=16 * many * rows * feature_all * CH,
            moved=6 * many * rows * feature_all,
        )(me, value, head_weight[0])

    def score(me, first, many, group, arrived):
        width = feature_all // group
        heads = width // HD
        dims = (2 * many, heads // 4, group, 4 * rows, length)
        if group == count:
            outs = [shape(*dims)]
        else:
            outs = [
                shape(*dims, dtype=jnp.float32),
                shape(2 * many, heads, length, dtype=jnp.float32),
                shape(2 * many, heads, length, dtype=jnp.float32),
            ]
        return call(
            functools.partial(score_kernel, first, count, group, width),
            outs,
            [SMEM] + [VMEM] * (count + 1),
            "score",
            flops=16 * many * heads * length * length * HD,
            moved=16 * many * rows * feature_all,
        )(me, query, key, *[arrived[s] for s in range(1, count)])

    guidance = jnp.where(section_index == 0, jnp.float32(high_guidance), jnp.float32(low_guidance))
    skipping = jnp.where(section_index == 1, skip_flags, 0)

    def attend(first, many, group, weights, projected, before=()):
        total = first + many
        return call(
            functools.partial(attend_kernel, first, count, group, len(weights)),
            [shape(total, rows // 2, 2 * CH, dtype=jnp.float32)] * count,
            [SMEM, SMEM] + [VMEM] * (len(weights) + group + len(before)),
            "attend",
            scratch=[pltpu.VMEM((length, 2 * CH), jnp.float32)],
            flops=16 * many * feature_all * length * HD,
            moved=8 * many * rows * feature_all,
        )(guidance[None], skipping, *weights, *projected, *before)

    def weigh_all(exponents, top, near, far):
        return call(
            functools.partial(weigh_kernel, half),
            shape(exponents.shape[0], exponents.size // exponents.shape[0] // length, length),
            [VMEM] * 4,
            "weigh",
            flops=exponents.size,
            moved=6 * exponents.size,
        )(exponents, top, near, far)

    half = count // 2
    step_now = step_index[0]
    step_size = noise_level(step_now + 1) - noise_level(step_now)
    finish_mark = jnp.where(
        (section_index == 0) & (step_now + 1 == SWITCH), jnp.float32(1.0), jnp.float32(0.0)
    )
    far_shifts = list(range(count - 1, half - 1, -1))
    inner = list(range(1, half))
    first = pack(me, 0, early, half)
    second = pack(after(me, first[0]), early, late, half)
    first_values = project(after(me, second[0]), 0, early, half)
    second_values = project(after(me, second[0]), early, late, half)

    arrived = {s: exchange(first[s - 1], s) for s in range(1, count)}
    late_arrived = {s: exchange(second[s - 1], s) for s in far_shifts}
    for s in inner:
        late_arrived[s] = exchange(after(second[s - 1], arrived[half]), s)
    values_here = [first_values[0]] + [
        exchange(after(first_values[s], arrived[half]), s) for s in inner
    ]
    late_values = [second_values[0]] + [
        exchange(after(second_values[s], arrived[1]), s) for s in inner
    ]

    arrived_mark = lax.ppermute(after(finish_mark, arrived[1]), "section", [(0, 1)])
    exponents, top, near = score(after(me, arrived_mark), 0, early, half, arrived)
    weights = weigh_all(exponents, top, near, exchange(near, half))
    shares = attend(0, early, half, [weights], values_here)

    exponents, top, near = score(me, early, late, half, late_arrived)
    far = exchange(near, half)
    shares = attend(early, late, half, [exponents, top, near, far], late_values, shares)

    guided = shares[0]
    for s in range(1, count):
        guided = guided + exchange(shares[s], s)
    updated = latent[0] + step_size[:, None, None] * guided
    taken = lax.ppermute(updated, "section", [(0, 1)])
    taking = (section_index == 1) & (arrived_mark > 0.5)
    next_latent = jnp.where(taking[:, None, None], taken, updated)
    return (guided[None], next_latent[None])


def solution(mesh):
    placed = (
        P("section", ("groups", "blk"), "sp", None),
        P("section", ("groups", "blk"), None, "sp", None),
        P("section", ("groups", "blk"), None, "sp", None),
        P("section", ("groups", "blk"), None, "sp", None),
        P("section", None, None),
        P("section", ("groups", "blk")),
        P(("groups", "blk")),
    )
    return jax.shard_map(
        functools.partial(on_device, mesh.shape["sp"]),
        mesh=mesh,
        in_specs=placed,
        out_specs=(
            P("section", ("groups", "blk"), "sp", None),
            P("section", ("groups", "blk"), "sp", None),
        ),
        check_vma=False,
    )
```

time: 101 us -> 97.7 us (0.967)
  starting transfers between devices: 27 us -> 36.4 us
  waiting for transfers between devices: 46.2 us -> 39.7 us
  Pallas kernels: 18.1 us -> 14.8 us
  local copies, waits for them, and re-layouts: 7.08 us -> 4.24 us
    ppermute x13, starting transfers between devices: 24.2 us -> 33.9 us  [exchange(): return lax.ppermute(array, 'sp', [(i, i ^ s) for i in range(count)])]
    ppermute x13, waiting for transfers between devices: 45.3 us -> 38.1 us  [exchange(): return lax.ppermute(array, 'sp', [(i, i ^ s) for i in range(count)])]
    pallas_call x6 -> x5, Pallas kernels: 11.5 us -> 7.88 us  [the longest x2 4.78 us: pack(): call(functools.partial(pack_kernel, 2 * first, group, width), [shape(2 *...]
    unnamed x30 -> x22, local copies, waits for them, and re-layouts: 7.08 us -> 4.24 us
  transfers between devices with their start and end apart: 15 -> 15, of which waited for: 8 -> 11; matrix products, arithmetic and copies ran while one was open for 0% -> 0% of each run, Pallas kernels for 15% -> 12%
where the time goes in v4:
time: 97.7 us; the launch traced here: 97.3 us
  waiting for transfers between devices  39.7 us (41%)
  starting transfers between devices  36.4 us (37%)
  Pallas kernels  14.8 us (15%)
  local copies, waits for them, and re-layouts  4.24 us (4%)
  other arithmetic  1.32 us (1%)
    ppermute x13, waiting for transfers between devices, exchange(): return lax.ppermute(array, 'sp', [(i, i ^ s) for i in range(count)])  38.1 us
    ppermute x13, starting transfers between devices, exchange(): return lax.ppermute(array, 'sp', [(i, i ^ s) for i in range(count)])  33.9 us
    pallas_call x2, Pallas kernels, score(): call(functools.partial(score_kernel, first, count, group, width), outs, [...  4.78 us
    pallas_call x2, Pallas kernels, pack(): call(functools.partial(pack_kernel, 2 * first, group, width), [shape(2 *...  4.78 us
    unnamed x22, local copies, waits for them, and re-layouts  4.24 us
    pallas_call x2, Pallas kernels, attend(): call(functools.partial(attend_kernel, first, count, group, len(weights)),...  2.55 us
    pallas_call x2, Pallas kernels, project(): call(functools.partial(project_kernel, first, group, width), [shape(many,...  2.17 us
  transfers between devices with their start and end apart: 15, of which 11 were waited for; matrix products, arithmetic and copies ran while one was open for 0% of the time, Pallas kernels for 12%

profile of v4, /device:TPU:0, one launch (start us, length us, event | category | flops | bytes accessed | tf_op | source)
XLA Modules:
  0.0 97.3 jit_solution(18299193316572966386)
XLA Ops:
  0.6 2.6 %pack.2 = (bf16[4,32,4096]{2,1,0:T(8,128)(2,1)}, bf16[4,32,2048]{2,1,0:T(8,128)(2,1)}, bf16[4,32,2048]{2,1,0:T(8,128)(2,1)}) custom-call(s32[1]{0:T(128)} %bitcast.1.me_ref, bf16[6,32,4096]{2,1,0:T(8,128)(2,1)} %bitcast.15, bf16[6,32,4096]{2,1,0:T(8,128)(2,1)} %bitcast.19), custom_call_target="tpu_custom_call" | custom-call | bytes 4194304 | tf_op jit(solution)/shard_map/pack/pallas_call | solution.py:258
  3.2 3.1 %collective-permute-start.5 = (bf16[4,32,4096]{2,1,0:T(8,128)(2,1)}, bf16[4,32,4096]{2,1,0:T(8,128)(2,1)}, u32[]{:S(2)}, u32[]{:S(2)}) collective-permute-start(bf16[4,32,4096]{2,1,0:T(8,128)(2,1)} %get-tuple-element.33), channel_id=1, source_target_pairs={{0,2},{2,0},{4,6},{6,4},{1,3},{3,1},{5,7},{7,5},{8,10},{10,8},{12,... | collective-permute-start | bytes 3145736 | tf_op jit(solution)/shard_map/ppermute | solution.py:246
  6.3 2.6 %collective-permute-start = (bf16[4,32,2048]{2,1,0:T(8,128)(2,1)}, bf16[4,32,2048]{2,1,0:T(8,128)(2,1)}, u32[]{:S(2)}, u32[]{:S(2)}) collective-permute-start(bf16[4,32,2048]{2,1,0:T(8,128)(2,1)} %get-tuple-element.36), channel_id=1, source_target_pairs={{0,4},{2,6},{4,0},{6,2},{1,5},{3,7},{5,1},{7,3},{8,12},{10,14},{12... | collective-permute-start | bytes 1572872 | tf_op jit(solution)/shard_map/ppermute | solution.py:246
  8.9 2.2 %pack.3 = (bf16[2,32,4096]{2,1,0:T(8,128)(2,1)}, bf16[2,32,2048]{2,1,0:T(8,128)(2,1)}, bf16[2,32,2048]{2,1,0:T(8,128)(2,1)}) custom-call(s32[1]{0:T(128)} %bitcast.1.me_ref, bf16[6,32,4096]{2,1,0:T(8,128)(2,1)} %bitcast.16, bf16[6,32,4096]{2,1,0:T(8,128)(2,1)} %bitcast.20), custom_call_target="tpu_custom_call" | custom-call | bytes 2097152 | tf_op jit(solution)/shard_map/pack/pallas_call | solution.py:258
  11.1 1.9 %collective-permute-start.2 = (bf16[2,32,2048]{2,1,0:T(8,128)(2,1)}, bf16[2,32,2048]{2,1,0:T(8,128)(2,1)S(1)}, u32[]{:S(2)}, u32[]{:S(2)}) collective-permute-start(bf16[2,32,2048]{2,1,0:T(8,128)(2,1)} %get-tuple-element.38), channel_id=1, source_target_pairs={{0,4},{2,6},{4,0},{6,2},{1,5},{3,7},{5,1},{7,3},{8,12},{10,14},{12... | collective-permute-start | bytes 786440 | tf_op jit(solution)/shard_map/ppermute | solution.py:246
  13.0 2.0 %collective-permute-start.3 = (bf16[2,32,2048]{2,1,0:T(8,128)(2,1)}, bf16[2,32,2048]{2,1,0:T(8,128)(2,1)}, u32[]{:S(2)}, u32[]{:S(2)}) collective-permute-start(bf16[2,32,2048]{2,1,0:T(8,128)(2,1)} %get-tuple-element.39), channel_id=1, source_target_pairs={{0,6},{2,4},{4,2},{6,0},{1,7},{3,5},{5,3},{7,1},{8,14},{10,12},{12... | collective-permute-start | bytes 786440 | tf_op jit(solution)/shard_map/ppermute | solution.py:246
  15.0 1.0 %copy-done.4 = bf16[1,64,4096]{2,1,0:T(8,128)(2,1)S(1)} copy-done((bf16[1,64,4096]{2,1,0:T(8,128)(2,1)S(1)}, bf16[1,64,4096]{2,1,0:T(8,128)(2,1)}, u32[]{:S(2)}) %copy-start.4) | copy-done | bytes 524312
  16.0 1.6 %project.3 = (bf16[2,2,4,64,128]{4,3,2,1,0:T(8,128)(2,1)S(1)}, bf16[2,2,4,64,128]{4,3,2,1,0:T(8,128)(2,1)}) custom-call(s32[1]{0:T(128)} %bitcast.1.me_ref, bf16[6,32,4096]{2,1,0:T(8,128)(2,1)S(1)} %bitcast.23, bf16[64,4096]{1,0:T(8,128)(2,1)S(1)} %bitcast.25), custom_call_target="tpu_custom_call" | custom-call | flops 268435456 | bytes 1572864 | tf_op jit(solution)/shard_map/project/pallas_call | solution.py:271
  18.4 23.1 %collective-permute-done.refs_1_ = bf16[4,32,2048]{2,1,0:T(8,128)(2,1)} collective-permute-done((bf16[4,32,2048]{2,1,0:T(8,128)(2,1)}, bf16[4,32,2048]{2,1,0:T(8,128)(2,1)}, u32[]{:S(2)}, u32[]{:S(2)}) %collective-permute-start) | collective-permute-done | bytes 524320 | tf_op jit(solution)/shard_map/ppermute | solution.py:246
  41.5 3.5 %collective-permute-start.1 = (bf16[2,32,4096]{2,1,0:T(8,128)(2,1)}, bf16[2,32,4096]{2,1,0:T(8,128)(2,1)}, u32[]{:S(2)}, u32[]{:S(2)}) collective-permute-start(bf16[2,32,4096]{2,1,0:T(8,128)(2,1)} %get-tuple-element.37), channel_id=1, source_target_pairs={{0,2},{2,0},{4,6},{6,4},{1,3},{3,1},{5,7},{7,5},{8,10},{10,8},{12,... | collective-permute-start | bytes 1572872 | tf_op jit(solution)/shard_map/ppermute | solution.py:246
  45.1 1.3 %collective-permute-start.7 = (f32[3]{0:T(128)S(1)}, f32[3]{0:T(128)S(1)}, u32[]{:S(2)}, u32[]{:S(2)}) collective-permute-start(f32[3]{0:T(128)S(1)} %get-tuple-element.47), channel_id=1, source_target_pairs={{0,8},{1,9},{2,10},{3,11},{4,12},{5,13},{6,14},{7,15},{16,24},{17,... | collective-permute-start | bytes 44 | tf_op jit(solution)/shard_map/ppermute | solution.py:350
  46.3 0.8 collective-permute-done.7
  47.2 1.4 %copy-done.3 = bf16[1,3,2,32,4096]{4,3,2,1,0:T(8,128)(2,1)S(1)} copy-done((bf16[1,3,2,32,4096]{4,3,2,1,0:T(8,128)(2,1)S(1)}, bf16[1,3,2,32,4096]{4,3,2,1,0:T(8,128)(2,1)}, u32[]{:S(2)}) %copy-start.3) | copy-done | bytes 1572888
  48.6 1.0 %copy-done.5 = bf16[1,64,4096]{2,1,0:T(8,128)(2,1)S(1)} copy-done((bf16[1,64,4096]{2,1,0:T(8,128)(2,1)S(1)}, bf16[1,64,4096]{2,1,0:T(8,128)(2,1)}, u32[]{:S(2)}) %copy-start.5) | copy-done | bytes 524312
  50.2 5.6 %collective-permute-done.8.refs_2_ = bf16[4,32,2048]{2,1,0:T(8,128)(2,1)} collective-permute-done((bf16[4,32,2048]{2,1,0:T(8,128)(2,1)}, bf16[4,32,2048]{2,1,0:T(8,128)(2,1)}, u32[]{:S(2)}, u32[]{:S(2)}) %collective-permute-start.8) | collective-permute-done | bytes 524320 | tf_op jit(solution)/shard_map/ppermute | solution.py:246
  55.7 3.0 %score.3 = (f32[4,4,2,128,128]{4,3,2,1,0:T(8,128)S(1)}, f32[4,16,128]{2,1,0:T(8,128)S(1)}, f32[4,16,128]{2,1,0:T(8,128)S(1)}) custom-call(s32[1]{0:T(128)} %bitcast.1.me_ref, bf16[6,32,4096]{2,1,0:T(8,128)(2,1)S(1)} %bitcast.17, bf16[6,32,4096]{2,1,0:T(8,128)(2,1)S(1)} %bitcast.21, bf16[4,32,4096]{2,1,0:T(8,128)(2,1)} %collective-permute-done.5.refs_0_, ...), custom_call_target="tpu_custom_call" | custom-call | flops 1073741824 | bytes 4194304 | tf_op jit(solution)/shard_map/score/pallas_call | solution.py:292
  58.7 13.3 %collective-permute-start.9 = (f32[4,16,128]{2,1,0:T(8,128)S(1)}, f32[4,16,128]{2,1,0:T(8,128)S(1)}, u32[]{:S(2)}, u32[]{:S(2)}) collective-permute-start(f32[4,16,128]{2,1,0:T(8,128)S(1)} %get-tuple-element.52.near_ref), channel_id=1, source_target_pairs={{0,4},{2,6},{4,0},{6,2},{1,5},{3,7},{5,1},{7,3},{8,12},{10,14},{12... | collective-permute-start | bytes 98312 | tf_op jit(solution)/shard_map/ppermute | solution.py:246
  72.0 0.9 collective-permute-done.2.refs_1_
  72.9 3.9 %collective-permute-done.1.refs_0_ = bf16[2,32,4096]{2,1,0:T(8,128)(2,1)} collective-permute-done((bf16[2,32,4096]{2,1,0:T(8,128)(2,1)}, bf16[2,32,4096]{2,1,0:T(8,128)(2,1)}, u32[]{:S(2)}, u32[]{:S(2)}) %collective-permute-start.1) | collective-permute-done | bytes 524320 | tf_op jit(solution)/shard_map/ppermute | solution.py:246
  76.9 1.8 %score.2 = (f32[2,4,2,128,128]{4,3,2,1,0:T(8,128)S(1)}, f32[2,16,128]{2,1,0:T(8,128)S(1)}, f32[2,16,128]{2,1,0:T(8,128)S(1)}) custom-call(s32[1]{0:T(128)} %bitcast.1.me_ref, bf16[6,32,4096]{2,1,0:T(8,128)(2,1)S(1)} %bitcast.18, bf16[6,32,4096]{2,1,0:T(8,128)(2,1)S(1)} %bitcast.22, bf16[2,32,4096]{2,1,0:T(8,128)(2,1)} %collective-permute-done.1.refs_0_, ...), custom_call_target="tpu_custom_call" | custom-call | flops 536870912 | bytes 2097152 | tf_op jit(solution)/shard_map/score/pallas_call | solution.py:292
  78.7 2.3 %collective-permute-start.4 = (f32[2,16,128]{2,1,0:T(8,128)S(1)}, f32[2,16,128]{2,1,0:T(8,128)S(1)}, u32[]{:S(2)}, u32[]{:S(2)}) collective-permute-start(f32[2,16,128]{2,1,0:T(8,128)S(1)} %get-tuple-element.42.refs_2_), channel_id=1, source_target_pairs={{0,4},{2,6},{4,0},{6,2},{1,5},{3,7},{5,1},{7,3},{8,12},{10,14},{12... | collective-permute-start | bytes 49160 | tf_op jit(solution)/shard_map/ppermute | solution.py:246
  82.3 0.7 collective-permute-done.10.refs_2_
  83.0 1.6 %attend.2 = (f32[2,16,128]{2,1,0:T(8,128)S(1)}, f32[2,16,128]{2,1,0:T(8,128)S(1)}, f32[2,16,128]{2,1,0:T(8,128)S(1)}, f32[2,16,128]{2,1,0:T(8,128)S(1)}) custom-call(f32[1]{0:T(128)} %bitcast.scale_ref, s32[3]{0:T(128)S(1)} %broadcast_select_fusion.skip_ref, bf16[4,1024,128]{2,1,0:T(8,128)(2,1)S(1)} %weigh.1.refs_0_, ...), custom_call_target="tpu_custom_call" | custom-call | flops 2147483648 | bytes 2097152 | tf_op jit(solution)/shard_map/attend/pallas_call | solution.py:306
  84.6 1.4 %collective-permute-done.6.refs_5_ = bf16[1,2,4,64,128]{4,3,2,1,0:T(8,128)(2,1)S(1)} collective-permute-done((bf16[1,2,4,64,128]{4,3,2,1,0:T(8,128)(2,1)S(1)}, bf16[1,2,4,64,128]{4,3,2,1,0:T(8,128)(2,1)S(1)}, u32[]{:S(2)}, u32[]{:S(2)}) %collective-permute-start.6) | collective-permute-done | bytes 131104 | tf_op jit(solution)/shard_map/ppermute | solution.py:246
  86.0 0.9 attend.3
  87.0 1.9 %collective-permute-start.13 = (f32[3,16,128]{2,1,0:T(8,128)S(1)}, f32[3,16,128]{2,1,0:T(8,128)S(1)}, u32[]{:S(2)}, u32[]{:S(2)}) collective-permute-start(f32[3,16,128]{2,1,0:T(8,128)S(1)} %get-tuple-element.63), channel_id=1, source_target_pairs={{0,6},{2,4},{4,2},{6,0},{1,7},{3,5},{5,3},{7,1},{8,14},{10,12},{12... | collective-permute-start | bytes 73736 | tf_op jit(solution)/shard_map/ppermute | solution.py:246
  88.9 1.2 %collective-permute-start.12 = (f32[3,16,128]{2,1,0:T(8,128)S(1)}, f32[3,16,128]{2,1,0:T(8,128)S(1)}, u32[]{:S(2)}, u32[]{:S(2)}) collective-permute-start(f32[3,16,128]{2,1,0:T(8,128)S(1)} %get-tuple-element.62), channel_id=1, source_target_pairs={{0,4},{2,6},{4,0},{6,2},{1,5},{3,7},{5,1},{7,3},{8,12},{10,14},{12... | collective-permute-start | bytes 73736 | tf_op jit(solution)/shard_map/ppermute | solution.py:246
  90.1 1.4 %collective-permute-start.11 = (f32[3,16,128]{2,1,0:T(8,128)S(1)}, f32[3,16,128]{2,1,0:T(8,128)S(1)}, u32[]{:S(2)}, u32[]{:S(2)}) collective-permute-start(f32[3,16,128]{2,1,0:T(8,128)S(1)} %get-tuple-element.61), channel_id=1, source_target_pairs={{0,2},{2,0},{4,6},{6,4},{1,3},{3,1},{5,7},{7,5},{8,10},{10,8},{12,... | collective-permute-start | bytes 73736 | tf_op jit(solution)/shard_map/ppermute | solution.py:246
  91.4 1.5 %collective-permute-done.13 = f32[3,16,128]{2,1,0:T(8,128)S(1)} collective-permute-done((f32[3,16,128]{2,1,0:T(8,128)S(1)}, f32[3,16,128]{2,1,0:T(8,128)S(1)}, u32[]{:S(2)}, u32[]{:S(2)}) %collective-permute-start.13) | collective-permute-done | bytes 24608 | tf_op jit(solution)/shard_map/ppermute | solution.py:246
  92.9 0.7 collective-permute-done.12
  94.5 1.3 %collective-permute-start.14 = (f32[3,16,128]{2,1,0:T(8,128)S(1)}, f32[3,16,128]{2,1,0:T(8,128)S(1)}, u32[]{:S(2)}, u32[]{:S(2)}) collective-permute-start(f32[3,16,128]{2,1,0:T(8,128)S(1)} %get-tuple-element.64), channel_id=1, source_target_pairs={{0,8},{1,9},{2,10},{3,11},{4,12},{5,13},{6,14},{7,15},{16,24},{17,... | collective-permute-start | bytes 73736 | tf_op jit(solution)/shard_map/ppermute | solution.py:363
  95.8 0.8 collective-permute-done.14
  (34 shorter events, 4.1 us)
Async XLA Ops:
  3.2 41.8 %collective-permute-start.5 = (bf16[4,32,4096]{2,1,0:T(8,128)(2,1)}, bf16[4,32,4096]{2,1,0:T(8,128)(2,1)}, u32[]{:S(2)}, u32[]{:S(2)}) collective-permute-start(bf16[4,32,4096]{2,1,0:T(8,128)(2,1)} %get-tuple-element.33), channel_id=1, source_target_pairs={{0,2},{2,0},{4,6},{6,4},{1,3},{3,1},{5,7},{7,5},{8,10},{10,8},{12,... | collective-permute-start | bytes 3145736 | tf_op jit(solution)/shard_map/ppermute | solution.py:246
  6.3 35.2 %collective-permute-start = (bf16[4,32,2048]{2,1,0:T(8,128)(2,1)}, bf16[4,32,2048]{2,1,0:T(8,128)(2,1)}, u32[]{:S(2)}, u32[]{:S(2)}) collective-permute-start(bf16[4,32,2048]{2,1,0:T(8,128)(2,1)} %get-tuple-element.36), channel_id=1, source_target_pairs={{0,4},{2,6},{4,0},{6,2},{1,5},{3,7},{5,1},{7,3},{8,12},{10,14},{12... | collective-permute-start | bytes 1572872 | tf_op jit(solution)/shard_map/ppermute | solution.py:246
  8.9 6.1 %copy-start.2 = (bf16[1,3,2,32,4096]{4,3,2,1,0:T(8,128)(2,1)S(1)}, bf16[1,3,2,32,4096]{4,3,2,1,0:T(8,128)(2,1)}, u32[]{:S(2)}) copy-start(bf16[1,3,2,32,4096]{4,3,2,1,0:T(8,128)(2,1)} %param.10) | copy-start | bytes 4718596
  8.9 46.8 %collective-permute-start.8 = (bf16[4,32,2048]{2,1,0:T(8,128)(2,1)}, bf16[4,32,2048]{2,1,0:T(8,128)(2,1)}, u32[]{:S(2)}, u32[]{:S(2)}) collective-permute-start(bf16[4,32,2048]{2,1,0:T(8,128)(2,1)} %get-tuple-element.49), channel_id=1, source_target_pairs={{0,6},{2,4},{4,2},{6,0},{1,7},{3,5},{5,3},{7,1},{8,14},{10,12},{12... | collective-permute-start | bytes 1572872 | tf_op jit(solution)/shard_map/ppermute | solution.py:246
  11.1 33.9 %copy-start.9 = (s32[1,3]{1,0:T(1,128)S(1)}, s32[1,3]{1,0:T(1,128)}, u32[]{:S(2)}) copy-start(s32[1,3]{1,0:T(1,128)} %param.12) | copy-start | bytes 40
  11.1 36.0 %copy-start.10 = (s32[3]{0:T(128)S(1)}, s32[3]{0:T(128)}, u32[]{:S(2)}) copy-start(s32[3]{0:T(128)} %param.13) | copy-start | bytes 40
  11.1 61.8 %collective-permute-start.2 = (bf16[2,32,2048]{2,1,0:T(8,128)(2,1)}, bf16[2,32,2048]{2,1,0:T(8,128)(2,1)S(1)}, u32[]{:S(2)}, u32[]{:S(2)}) collective-permute-start(bf16[2,32,2048]{2,1,0:T(8,128)(2,1)} %get-tuple-element.38), channel_id=1, source_target_pairs={{0,4},{2,6},{4,0},{6,2},{1,5},{3,7},{5,1},{7,3},{8,12},{10,14},{12... | collective-permute-start | bytes 786440 | tf_op jit(solution)/shard_map/ppermute | solution.py:246
  13.0 59.9 %collective-permute-start.3 = (bf16[2,32,2048]{2,1,0:T(8,128)(2,1)}, bf16[2,32,2048]{2,1,0:T(8,128)(2,1)}, u32[]{:S(2)}, u32[]{:S(2)}) collective-permute-start(bf16[2,32,2048]{2,1,0:T(8,128)(2,1)} %get-tuple-element.39), channel_id=1, source_target_pairs={{0,6},{2,4},{4,2},{6,0},{1,7},{3,5},{5,3},{7,1},{8,14},{10,12},{12... | collective-permute-start | bytes 786440 | tf_op jit(solution)/shard_map/ppermute | solution.py:246
  15.0 1.0 %copy-start.4 = (bf16[1,64,4096]{2,1,0:T(8,128)(2,1)S(1)}, bf16[1,64,4096]{2,1,0:T(8,128)(2,1)}, u32[]{:S(2)}) copy-start(bf16[1,64,4096]{2,1,0:T(8,128)(2,1)} %param.11) | copy-start | bytes 1572868
  16.0 39.7 %copy-start.1 = (bf16[1,3,2,32,4096]{4,3,2,1,0:T(8,128)(2,1)S(1)}, bf16[1,3,2,32,4096]{4,3,2,1,0:T(8,128)(2,1)}, u32[]{:S(2)}) copy-start(bf16[1,3,2,32,4096]{4,3,2,1,0:T(8,128)(2,1)} %param.9) | copy-start | bytes 4718596
  17.7 0.7 copy-start.6
  18.4 37.4 %copy-start = (bf16[1,3,2,32,4096]{4,3,2,1,0:T(8,128)(2,1)S(1)}, bf16[1,3,2,32,4096]{4,3,2,1,0:T(8,128)(2,1)}, u32[]{:S(2)}) copy-start(bf16[1,3,2,32,4096]{4,3,2,1,0:T(8,128)(2,1)} %param.8) | copy-start | bytes 4718596
  41.5 35.4 %collective-permute-start.1 = (bf16[2,32,4096]{2,1,0:T(8,128)(2,1)}, bf16[2,32,4096]{2,1,0:T(8,128)(2,1)}, u32[]{:S(2)}, u32[]{:S(2)}) collective-permute-start(bf16[2,32,4096]{2,1,0:T(8,128)(2,1)} %get-tuple-element.37), channel_id=1, source_target_pairs={{0,2},{2,0},{4,6},{6,4},{1,3},{3,1},{5,7},{7,5},{8,10},{10,8},{12,... | collective-permute-start | bytes 1572872 | tf_op jit(solution)/shard_map/ppermute | solution.py:246
  45.1 2.1 %collective-permute-start.7 = (f32[3]{0:T(128)S(1)}, f32[3]{0:T(128)S(1)}, u32[]{:S(2)}, u32[]{:S(2)}) collective-permute-start(f32[3]{0:T(128)S(1)} %get-tuple-element.47), channel_id=1, source_target_pairs={{0,8},{1,9},{2,10},{3,11},{4,12},{5,13},{6,14},{7,15},{16,24},{17,... | collective-permute-start | bytes 44 | tf_op jit(solution)/shard_map/ppermute | solution.py:350
  47.1 35.9 %collective-permute-start.10 = (bf16[2,2,4,64,128]{4,3,2,1,0:T(8,128)(2,1)}, bf16[2,2,4,64,128]{4,3,2,1,0:T(8,128)(2,1)}, u32[]{:S(2)}, u32[]{:S(2)}) collective-permute-start(bf16[2,2,4,64,128]{4,3,2,1,0:T(8,128)(2,1)} %get-tuple-element.55), channel_id=1, source_target_pairs={{0,2},{2,0},{4,6},{6,4},{1,3},{3,1},{5,7},{7,5},{8,10},{10,8},{12,... | collective-permute-start | bytes 786440 | tf_op jit(solution)/shard_map/ppermute | solution.py:246
  47.2 1.4 %copy-start.3 = (bf16[1,3,2,32,4096]{4,3,2,1,0:T(8,128)(2,1)S(1)}, bf16[1,3,2,32,4096]{4,3,2,1,0:T(8,128)(2,1)}, u32[]{:S(2)}) copy-start(bf16[1,3,2,32,4096]{4,3,2,1,0:T(8,128)(2,1)} %param.10) | copy-start | bytes 4718596
  48.6 1.0 %copy-start.5 = (bf16[1,64,4096]{2,1,0:T(8,128)(2,1)S(1)}, bf16[1,64,4096]{2,1,0:T(8,128)(2,1)}, u32[]{:S(2)}) copy-start(bf16[1,64,4096]{2,1,0:T(8,128)(2,1)} %param.11) | copy-start | bytes 1572868
  58.7 23.0 %collective-permute-start.9 = (f32[4,16,128]{2,1,0:T(8,128)S(1)}, f32[4,16,128]{2,1,0:T(8,128)S(1)}, u32[]{:S(2)}, u32[]{:S(2)}) collective-permute-start(f32[4,16,128]{2,1,0:T(8,128)S(1)} %get-tuple-element.52.near_ref), channel_id=1, source_target_pairs={{0,4},{2,6},{4,0},{6,2},{1,5},{3,7},{5,1},{7,3},{8,12},{10,14},{12... | collective-permute-start | bytes 98312 | tf_op jit(solution)/shard_map/ppermute | solution.py:246
  78.7 5.9 %collective-permute-start.4 = (f32[2,16,128]{2,1,0:T(8,128)S(1)}, f32[2,16,128]{2,1,0:T(8,128)S(1)}, u32[]{:S(2)}, u32[]{:S(2)}) collective-permute-start(f32[2,16,128]{2,1,0:T(8,128)S(1)} %get-tuple-element.42.refs_2_), channel_id=1, source_target_pairs={{0,4},{2,6},{4,0},{6,2},{1,5},{3,7},{5,1},{7,3},{8,12},{10,14},{12... | collective-permute-start | bytes 49160 | tf_op jit(solution)/shard_map/ppermute | solution.py:246
  81.0 5.0 %collective-permute-start.6 = (bf16[1,2,4,64,128]{4,3,2,1,0:T(8,128)(2,1)S(1)}, bf16[1,2,4,64,128]{4,3,2,1,0:T(8,128)(2,1)S(1)}, u32[]{:S(2)}, u32[]{:S(2)}) collective-permute-start(bf16[1,2,4,64,128]{4,3,2,1,0:T(8,128)(2,1)S(1)} %get-tuple-element.46), channel_id=1, source_target_pairs={{0,2},{2,0},{4,6},{6,4},{1,3},{3,1},{5,7},{7,5},{8,10},{10,8},{12,... | collective-permute-start | bytes 393224 | tf_op jit(solution)/shard_map/ppermute | solution.py:246
  81.7 1.3 %copy-start.7 = (bf16[2,2,4,64,128]{4,3,2,1,0:T(8,128)(2,1)S(1)}, bf16[2,2,4,64,128]{4,3,2,1,0:T(8,128)(2,1)}, u32[]{:S(2)}) copy-start(bf16[2,2,4,64,128]{4,3,2,1,0:T(8,128)(2,1)} %copy-done.6) | copy-start | bytes 786436
  86.0 7.9 %copy-start.8 = (f32[1,3,16,128]{3,2,1,0:T(8,128)S(1)}, f32[1,3,16,128]{3,2,1,0:T(8,128)}, u32[]{:S(2)}) copy-start(f32[1,3,16,128]{3,2,1,0:T(8,128)} %param.7) | copy-start | bytes 73732
  87.0 5.9 %collective-permute-start.13 = (f32[3,16,128]{2,1,0:T(8,128)S(1)}, f32[3,16,128]{2,1,0:T(8,128)S(1)}, u32[]{:S(2)}, u32[]{:S(2)}) collective-permute-start(f32[3,16,128]{2,1,0:T(8,128)S(1)} %get-tuple-element.63), channel_id=1, source_target_pairs={{0,6},{2,4},{4,2},{6,0},{1,7},{3,5},{5,3},{7,1},{8,14},{10,12},{12... | collective-permute-start | bytes 73736 | tf_op jit(solution)/shard_map/ppermute | solution.py:246
  88.9 4.7 %collective-permute-start.12 = (f32[3,16,128]{2,1,0:T(8,128)S(1)}, f32[3,16,128]{2,1,0:T(8,128)S(1)}, u32[]{:S(2)}, u32[]{:S(2)}) collective-permute-start(f32[3,16,128]{2,1,0:T(8,128)S(1)} %get-tuple-element.62), channel_id=1, source_target_pairs={{0,4},{2,6},{4,0},{6,2},{1,5},{3,7},{5,1},{7,3},{8,12},{10,14},{12... | collective-permute-start | bytes 73736 | tf_op jit(solution)/shard_map/ppermute | solution.py:246
  90.1 3.8 %collective-permute-start.11 = (f32[3,16,128]{2,1,0:T(8,128)S(1)}, f32[3,16,128]{2,1,0:T(8,128)S(1)}, u32[]{:S(2)}, u32[]{:S(2)}) collective-permute-start(f32[3,16,128]{2,1,0:T(8,128)S(1)} %get-tuple-element.61), channel_id=1, source_target_pairs={{0,2},{2,0},{4,6},{6,4},{1,3},{3,1},{5,7},{7,5},{8,10},{10,8},{12,... | collective-permute-start | bytes 73736 | tf_op jit(solution)/shard_map/ppermute | solution.py:246
  94.5 2.1 %collective-permute-start.14 = (f32[3,16,128]{2,1,0:T(8,128)S(1)}, f32[3,16,128]{2,1,0:T(8,128)S(1)}, u32[]{:S(2)}, u32[]{:S(2)}) collective-permute-start(f32[3,16,128]{2,1,0:T(8,128)S(1)} %get-tuple-element.64), channel_id=1, source_target_pairs={{0,8},{1,9},{2,10},{3,11},{4,12},{5,13},{6,14},{7,15},{16,24},{17,... | collective-permute-start | bytes 73736 | tf_op jit(solution)/shard_map/ppermute | solution.py:363

commit v5 on v4

--- a/solution.py
+++ b/solution.py
@@ -356,10 +356,9 @@
     far = exchange(near, half)
     shares = attend(early, late, half, [exponents, top, near, far], late_values, shares)
 
-    guided = shares[0]
-    for s in range(1, count):
-        guided = guided + exchange(shares[s], s)
-    updated = latent[0] + step_size[:, None, None] * guided
+    parts = [exchange(shares[s], s) for s in range(count - 1, 0, -1)] + [shares[0]]
+    guided = functools.reduce(jnp.add, lax.optimization_barrier(parts))
+    updated = latent[0] + step_size[:, None, None] * functools.reduce(jnp.add, parts)
     taken = lax.ppermute(updated, "section", [(0, 1)])
     taking = (section_index == 1) & (arrived_mark > 0.5)
     next_latent = jnp.where(taking[:, None, None], taken, updated)

time: 97.7 us -> 97.2 us (level)
  transfers between devices with their start and end apart: 15 -> 15, of which waited for: 11 -> 11; matrix products, arithmetic and copies ran while one was open for 0% -> 1% of each run, Pallas kernels for 12% -> 12%
where the time goes in v5:
time: 97.2 us; the launch traced here: 96.8 us
  waiting for transfers between devices  39.1 us (40%)
  starting transfers between devices  36.4 us (37%)
  Pallas kernels  14.9 us (15%)
  local copies, waits for them, and re-layouts  4.25 us (4%)
  other arithmetic  1.39 us (1%)
    ppermute x13, waiting for transfers between devices, exchange(): return lax.ppermute(array, 'sp', [(i, i ^ s) for i in range(count)])  38.1 us
    ppermute x13, starting transfers between devices, exchange(): return lax.ppermute(array, 'sp', [(i, i ^ s) for i in range(count)])  33.8 us
    pallas_call x2, Pallas kernels, pack(): call(functools.partial(pack_kernel, 2 * first, group, width), [shape(2 *...  4.86 us
    pallas_call x2, Pallas kernels, score(): call(functools.partial(score_kernel, first, count, group, width), outs, [...  4.79 us
    unnamed x22, local copies, waits for them, and re-layouts  4.25 us
    pallas_call x2, Pallas kernels, attend(): call(functools.partial(attend_kernel, first, count, group, len(weights)),...  2.55 us
    pallas_call x2, Pallas kernels, project(): call(functools.partial(project_kernel, first, group, width), [shape(many,...  2.16 us
  transfers between devices with their start and end apart: 15, of which 11 were waited for; matrix products, arithmetic and copies ran while one was open for 1% of the time, Pallas kernels for 12%

profile of v5, /device:TPU:0, one launch (start us, length us, event | category | flops | bytes accessed | tf_op | source)
XLA Modules:
  0.0 96.8 jit_solution(16398229073672777530)
XLA Ops:
  0.6 2.6 %pack.2 = (bf16[4,32,4096]{2,1,0:T(8,128)(2,1)}, bf16[4,32,2048]{2,1,0:T(8,128)(2,1)}, bf16[4,32,2048]{2,1,0:T(8,128)(2,1)}) custom-call(s32[1]{0:T(128)} %bitcast.1.me_ref, bf16[6,32,4096]{2,1,0:T(8,128)(2,1)} %bitcast.16, bf16[6,32,4096]{2,1,0:T(8,128)(2,1)} %bitcast.20), custom_call_target="tpu_custom_call" | custom-call | bytes 4194304 | tf_op jit(solution)/shard_map/pack/pallas_call | solution.py:258
  3.3 3.1 %collective-permute-start.5 = (bf16[4,32,4096]{2,1,0:T(8,128)(2,1)}, bf16[4,32,4096]{2,1,0:T(8,128)(2,1)}, u32[]{:S(2)}, u32[]{:S(2)}) collective-permute-start(bf16[4,32,4096]{2,1,0:T(8,128)(2,1)} %get-tuple-element.37), channel_id=1, source_target_pairs={{0,2},{2,0},{4,6},{6,4},{1,3},{3,1},{5,7},{7,5},{8,10},{10,8},{12,... | collective-permute-start | bytes 3145736 | tf_op jit(solution)/shard_map/ppermute | solution.py:246
  6.4 2.6 %collective-permute-start = (bf16[4,32,2048]{2,1,0:T(8,128)(2,1)}, bf16[4,32,2048]{2,1,0:T(8,128)(2,1)}, u32[]{:S(2)}, u32[]{:S(2)}) collective-permute-start(bf16[4,32,2048]{2,1,0:T(8,128)(2,1)} %get-tuple-element.40), channel_id=1, source_target_pairs={{0,4},{2,6},{4,0},{6,2},{1,5},{3,7},{5,1},{7,3},{8,12},{10,14},{12... | collective-permute-start | bytes 1572872 | tf_op jit(solution)/shard_map/ppermute | solution.py:246
  9.0 2.2 %pack.3 = (bf16[2,32,4096]{2,1,0:T(8,128)(2,1)}, bf16[2,32,2048]{2,1,0:T(8,128)(2,1)}, bf16[2,32,2048]{2,1,0:T(8,128)(2,1)}) custom-call(s32[1]{0:T(128)} %bitcast.1.me_ref, bf16[6,32,4096]{2,1,0:T(8,128)(2,1)} %bitcast.17, bf16[6,32,4096]{2,1,0:T(8,128)(2,1)} %bitcast.21), custom_call_target="tpu_custom_call" | custom-call | bytes 2097152 | tf_op jit(solution)/shard_map/pack/pallas_call | solution.py:258
  11.2 1.9 %collective-permute-start.2 = (bf16[2,32,2048]{2,1,0:T(8,128)(2,1)}, bf16[2,32,2048]{2,1,0:T(8,128)(2,1)S(1)}, u32[]{:S(2)}, u32[]{:S(2)}) collective-permute-start(bf16[2,32,2048]{2,1,0:T(8,128)(2,1)} %get-tuple-element.42), channel_id=1, source_target_pairs={{0,4},{2,6},{4,0},{6,2},{1,5},{3,7},{5,1},{7,3},{8,12},{10,14},{12... | collective-permute-start | bytes 786440 | tf_op jit(solution)/shard_map/ppermute | solution.py:246
  13.1 2.0 %collective-permute-start.3 = (bf16[2,32,2048]{2,1,0:T(8,128)(2,1)}, bf16[2,32,2048]{2,1,0:T(8,128)(2,1)}, u32[]{:S(2)}, u32[]{:S(2)}) collective-permute-start(bf16[2,32,2048]{2,1,0:T(8,128)(2,1)} %get-tuple-element.43), channel_id=1, source_target_pairs={{0,6},{2,4},{4,2},{6,0},{1,7},{3,5},{5,3},{7,1},{8,14},{10,12},{12... | collective-permute-start | bytes 786440 | tf_op jit(solution)/shard_map/ppermute | solution.py:246
  15.1 1.0 %copy-done.4 = bf16[1,64,4096]{2,1,0:T(8,128)(2,1)S(1)} copy-done((bf16[1,64,4096]{2,1,0:T(8,128)(2,1)S(1)}, bf16[1,64,4096]{2,1,0:T(8,128)(2,1)}, u32[]{:S(2)}) %copy-start.4) | copy-done | bytes 524312
  16.1 1.6 %project.3 = (bf16[2,2,4,64,128]{4,3,2,1,0:T(8,128)(2,1)S(1)}, bf16[2,2,4,64,128]{4,3,2,1,0:T(8,128)(2,1)}) custom-call(s32[1]{0:T(128)} %bitcast.1.me_ref, bf16[6,32,4096]{2,1,0:T(8,128)(2,1)S(1)} %bitcast.24, bf16[64,4096]{1,0:T(8,128)(2,1)S(1)} %bitcast.26), custom_call_target="tpu_custom_call" | custom-call | flops 268435456 | bytes 1572864 | tf_op jit(solution)/shard_map/project/pallas_call | solution.py:271
  17.7 0.7 copy-done.6
  18.5 23.1 %collective-permute-done.refs_1_ = bf16[4,32,2048]{2,1,0:T(8,128)(2,1)} collective-permute-done((bf16[4,32,2048]{2,1,0:T(8,128)(2,1)}, bf16[4,32,2048]{2,1,0:T(8,128)(2,1)}, u32[]{:S(2)}, u32[]{:S(2)}) %collective-permute-start) | collective-permute-done | bytes 524320 | tf_op jit(solution)/shard_map/ppermute | solution.py:246
  41.5 3.5 %collective-permute-start.1 = (bf16[2,32,4096]{2,1,0:T(8,128)(2,1)}, bf16[2,32,4096]{2,1,0:T(8,128)(2,1)}, u32[]{:S(2)}, u32[]{:S(2)}) collective-permute-start(bf16[2,32,4096]{2,1,0:T(8,128)(2,1)} %get-tuple-element.41), channel_id=1, source_target_pairs={{0,2},{2,0},{4,6},{6,4},{1,3},{3,1},{5,7},{7,5},{8,10},{10,8},{12,... | collective-permute-start | bytes 1572872 | tf_op jit(solution)/shard_map/ppermute | solution.py:246
  45.1 1.3 %collective-permute-start.7 = (f32[3]{0:T(128)S(1)}, f32[3]{0:T(128)S(1)}, u32[]{:S(2)}, u32[]{:S(2)}) collective-permute-start(f32[3]{0:T(128)S(1)} %get-tuple-element.51), channel_id=1, source_target_pairs={{0,8},{1,9},{2,10},{3,11},{4,12},{5,13},{6,14},{7,15},{16,24},{17,... | collective-permute-start | bytes 44 | tf_op jit(solution)/shard_map/ppermute | solution.py:350
  46.4 0.8 collective-permute-done.7
  47.2 1.4 %copy-done.3 = bf16[1,3,2,32,4096]{4,3,2,1,0:T(8,128)(2,1)S(1)} copy-done((bf16[1,3,2,32,4096]{4,3,2,1,0:T(8,128)(2,1)S(1)}, bf16[1,3,2,32,4096]{4,3,2,1,0:T(8,128)(2,1)}, u32[]{:S(2)}) %copy-start.3) | copy-done | bytes 1572888
  48.6 1.0 %copy-done.5 = bf16[1,64,4096]{2,1,0:T(8,128)(2,1)S(1)} copy-done((bf16[1,64,4096]{2,1,0:T(8,128)(2,1)S(1)}, bf16[1,64,4096]{2,1,0:T(8,128)(2,1)}, u32[]{:S(2)}) %copy-start.5) | copy-done | bytes 524312
  50.2 5.6 %collective-permute-done.8.refs_2_ = bf16[4,32,2048]{2,1,0:T(8,128)(2,1)} collective-permute-done((bf16[4,32,2048]{2,1,0:T(8,128)(2,1)}, bf16[4,32,2048]{2,1,0:T(8,128)(2,1)}, u32[]{:S(2)}, u32[]{:S(2)}) %collective-permute-start.8) | collective-permute-done | bytes 524320 | tf_op jit(solution)/shard_map/ppermute | solution.py:246
  55.8 3.0 %score.3 = (f32[4,4,2,128,128]{4,3,2,1,0:T(8,128)S(1)}, f32[4,16,128]{2,1,0:T(8,128)S(1)}, f32[4,16,128]{2,1,0:T(8,128)S(1)}) custom-call(s32[1]{0:T(128)} %bitcast.1.me_ref, bf16[6,32,4096]{2,1,0:T(8,128)(2,1)S(1)} %bitcast.18, bf16[6,32,4096]{2,1,0:T(8,128)(2,1)S(1)} %bitcast.22, bf16[4,32,4096]{2,1,0:T(8,128)(2,1)} %collective-permute-done.5.refs_0_, ...), custom_call_target="tpu_custom_call" | custom-call | flops 1073741824 | bytes 4194304 | tf_op jit(solution)/shard_map/score/pallas_call | solution.py:292
  58.8 13.3 %collective-permute-start.9 = (f32[4,16,128]{2,1,0:T(8,128)S(1)}, f32[4,16,128]{2,1,0:T(8,128)S(1)}, u32[]{:S(2)}, u32[]{:S(2)}) collective-permute-start(f32[4,16,128]{2,1,0:T(8,128)S(1)} %get-tuple-element.56.near_ref), channel_id=1, source_target_pairs={{0,4},{2,6},{4,0},{6,2},{1,5},{3,7},{5,1},{7,3},{8,12},{10,14},{12... | collective-permute-start | bytes 98312 | tf_op jit(solution)/shard_map/ppermute | solution.py:246
  72.1 0.9 collective-permute-done.2.refs_1_
  73.0 3.9 %collective-permute-done.1.refs_0_ = bf16[2,32,4096]{2,1,0:T(8,128)(2,1)} collective-permute-done((bf16[2,32,4096]{2,1,0:T(8,128)(2,1)}, bf16[2,32,4096]{2,1,0:T(8,128)(2,1)}, u32[]{:S(2)}, u32[]{:S(2)}) %collective-permute-start.1) | collective-permute-done | bytes 524320 | tf_op jit(solution)/shard_map/ppermute | solution.py:246
  76.9 1.8 %score.2 = (f32[2,4,2,128,128]{4,3,2,1,0:T(8,128)S(1)}, f32[2,16,128]{2,1,0:T(8,128)S(1)}, f32[2,16,128]{2,1,0:T(8,128)S(1)}) custom-call(s32[1]{0:T(128)} %bitcast.1.me_ref, bf16[6,32,4096]{2,1,0:T(8,128)(2,1)S(1)} %bitcast.19, bf16[6,32,4096]{2,1,0:T(8,128)(2,1)S(1)} %bitcast.23, bf16[2,32,4096]{2,1,0:T(8,128)(2,1)} %collective-permute-done.1.refs_0_, ...), custom_call_target="tpu_custom_call" | custom-call | flops 536870912 | bytes 2097152 | tf_op jit(solution)/shard_map/score/pallas_call | solution.py:292
  78.8 2.3 %collective-permute-start.4 = (f32[2,16,128]{2,1,0:T(8,128)S(1)}, f32[2,16,128]{2,1,0:T(8,128)S(1)}, u32[]{:S(2)}, u32[]{:S(2)}) collective-permute-start(f32[2,16,128]{2,1,0:T(8,128)S(1)} %get-tuple-element.46.refs_2_), channel_id=1, source_target_pairs={{0,4},{2,6},{4,0},{6,2},{1,5},{3,7},{5,1},{7,3},{8,12},{10,14},{12... | collective-permute-start | bytes 49160 | tf_op jit(solution)/shard_map/ppermute | solution.py:246
  82.3 0.7 collective-permute-done.10.refs_2_
  83.1 1.6 %attend.2 = (f32[2,16,128]{2,1,0:T(8,128)S(1)}, f32[2,16,128]{2,1,0:T(8,128)S(1)}, f32[2,16,128]{2,1,0:T(8,128)S(1)}, f32[2,16,128]{2,1,0:T(8,128)S(1)}) custom-call(f32[1]{0:T(128)} %bitcast.scale_ref, s32[3]{0:T(128)S(1)} %broadcast_select_fusion.skip_ref, bf16[4,1024,128]{2,1,0:T(8,128)(2,1)S(1)} %weigh.1.refs_0_, ...), custom_call_target="tpu_custom_call" | custom-call | flops 2147483648 | bytes 2097152 | tf_op jit(solution)/shard_map/attend/pallas_call | solution.py:306
  84.7 1.4 %collective-permute-done.6.refs_5_ = bf16[1,2,4,64,128]{4,3,2,1,0:T(8,128)(2,1)S(1)} collective-permute-done((bf16[1,2,4,64,128]{4,3,2,1,0:T(8,128)(2,1)S(1)}, bf16[1,2,4,64,128]{4,3,2,1,0:T(8,128)(2,1)S(1)}, u32[]{:S(2)}, u32[]{:S(2)}) %collective-permute-start.6) | collective-permute-done | bytes 131104 | tf_op jit(solution)/shard_map/ppermute | solution.py:246
  86.1 0.9 attend.3
  87.0 1.9 %collective-permute-start.11 = (f32[3,16,128]{2,1,0:T(8,128)S(1)}, f32[3,16,128]{2,1,0:T(8,128)S(1)}, u32[]{:S(2)}, u32[]{:S(2)}) collective-permute-start(f32[3,16,128]{2,1,0:T(8,128)S(1)} %get-tuple-element.64), channel_id=1, source_target_pairs={{0,6},{2,4},{4,2},{6,0},{1,7},{3,5},{5,3},{7,1},{8,14},{10,12},{12... | collective-permute-start | bytes 73736 | tf_op jit(solution)/shard_map/ppermute | solution.py:246
  88.9 1.2 %collective-permute-start.12 = (f32[3,16,128]{2,1,0:T(8,128)S(1)}, f32[3,16,128]{2,1,0:T(8,128)S(1)}, u32[]{:S(2)}, u32[]{:S(2)}) collective-permute-start(f32[3,16,128]{2,1,0:T(8,128)S(1)} %get-tuple-element.65), channel_id=1, source_target_pairs={{0,4},{2,6},{4,0},{6,2},{1,5},{3,7},{5,1},{7,3},{8,12},{10,14},{12... | collective-permute-start | bytes 73736 | tf_op jit(solution)/shard_map/ppermute | solution.py:246
  90.1 1.4 %collective-permute-start.13 = (f32[3,16,128]{2,1,0:T(8,128)S(1)}, f32[3,16,128]{2,1,0:T(8,128)S(1)}, u32[]{:S(2)}, u32[]{:S(2)}) collective-permute-start(f32[3,16,128]{2,1,0:T(8,128)S(1)} %get-tuple-element.66), channel_id=1, source_target_pairs={{0,2},{2,0},{4,6},{6,4},{1,3},{3,1},{5,7},{7,5},{8,10},{10,8},{12,... | collective-permute-start | bytes 73736 | tf_op jit(solution)/shard_map/ppermute | solution.py:246
  91.5 1.4 %collective-permute-done.11 = f32[3,16,128]{2,1,0:T(8,128)S(1)} collective-permute-done((f32[3,16,128]{2,1,0:T(8,128)S(1)}, f32[3,16,128]{2,1,0:T(8,128)S(1)}, u32[]{:S(2)}, u32[]{:S(2)}) %collective-permute-start.11) | collective-permute-done | bytes 24608 | tf_op jit(solution)/shard_map/ppermute | solution.py:246
  92.9 0.7 collective-permute-done.12
  94.0 1.3 %collective-permute-start.14 = (f32[3,16,128]{2,1,0:T(8,128)S(1)}, f32[3,16,128]{2,1,0:T(8,128)S(1)}, u32[]{:S(2)}, u32[]{:S(2)}) collective-permute-start(f32[3,16,128]{2,1,0:T(8,128)S(1)} %bitcast_add_fusion), channel_id=1, source_target_pairs={{0,8},{1,9},{2,10},{3,11},{4,12},{5,13},{6,14},{7,15},{16,24},{17,... | collective-permute-start | bytes 73736 | tf_op jit(solution)/shard_map/ppermute | solution.py:362
  (35 shorter events, 3.7 us)
Async XLA Ops:
  3.3 41.8 %collective-permute-start.5 = (bf16[4,32,4096]{2,1,0:T(8,128)(2,1)}, bf16[4,32,4096]{2,1,0:T(8,128)(2,1)}, u32[]{:S(2)}, u32[]{:S(2)}) collective-permute-start(bf16[4,32,4096]{2,1,0:T(8,128)(2,1)} %get-tuple-element.37), channel_id=1, source_target_pairs={{0,2},{2,0},{4,6},{6,4},{1,3},{3,1},{5,7},{7,5},{8,10},{10,8},{12,... | collective-permute-start | bytes 3145736 | tf_op jit(solution)/shard_map/ppermute | solution.py:246
  6.4 35.2 %collective-permute-start = (bf16[4,32,2048]{2,1,0:T(8,128)(2,1)}, bf16[4,32,2048]{2,1,0:T(8,128)(2,1)}, u32[]{:S(2)}, u32[]{:S(2)}) collective-permute-start(bf16[4,32,2048]{2,1,0:T(8,128)(2,1)} %get-tuple-element.40), channel_id=1, source_target_pairs={{0,4},{2,6},{4,0},{6,2},{1,5},{3,7},{5,1},{7,3},{8,12},{10,14},{12... | collective-permute-start | bytes 1572872 | tf_op jit(solution)/shard_map/ppermute | solution.py:246
  9.0 6.1 %copy-start.2 = (bf16[1,3,2,32,4096]{4,3,2,1,0:T(8,128)(2,1)S(1)}, bf16[1,3,2,32,4096]{4,3,2,1,0:T(8,128)(2,1)}, u32[]{:S(2)}) copy-start(bf16[1,3,2,32,4096]{4,3,2,1,0:T(8,128)(2,1)} %param.10) | copy-start | bytes 4718596
  9.0 46.8 %collective-permute-start.8 = (bf16[4,32,2048]{2,1,0:T(8,128)(2,1)}, bf16[4,32,2048]{2,1,0:T(8,128)(2,1)}, u32[]{:S(2)}, u32[]{:S(2)}) collective-permute-start(bf16[4,32,2048]{2,1,0:T(8,128)(2,1)} %get-tuple-element.53), channel_id=1, source_target_pairs={{0,6},{2,4},{4,2},{6,0},{1,7},{3,5},{5,3},{7,1},{8,14},{10,12},{12... | collective-permute-start | bytes 1572872 | tf_op jit(solution)/shard_map/ppermute | solution.py:246
  11.2 33.9 %copy-start.9 = (s32[1,3]{1,0:T(1,128)S(1)}, s32[1,3]{1,0:T(1,128)}, u32[]{:S(2)}) copy-start(s32[1,3]{1,0:T(1,128)} %param.12) | copy-start | bytes 40
  11.2 36.0 %copy-start.10 = (s32[3]{0:T(128)S(1)}, s32[3]{0:T(128)}, u32[]{:S(2)}) copy-start(s32[3]{0:T(128)} %param.13) | copy-start | bytes 40
  11.2 61.8 %collective-permute-start.2 = (bf16[2,32,2048]{2,1,0:T(8,128)(2,1)}, bf16[2,32,2048]{2,1,0:T(8,128)(2,1)S(1)}, u32[]{:S(2)}, u32[]{:S(2)}) collective-permute-start(bf16[2,32,2048]{2,1,0:T(8,128)(2,1)} %get-tuple-element.42), channel_id=1, source_target_pairs={{0,4},{2,6},{4,0},{6,2},{1,5},{3,7},{5,1},{7,3},{8,12},{10,14},{12... | collective-permute-start | bytes 786440 | tf_op jit(solution)/shard_map/ppermute | solution.py:246
  13.1 59.9 %collective-permute-start.3 = (bf16[2,32,2048]{2,1,0:T(8,128)(2,1)}, bf16[2,32,2048]{2,1,0:T(8,128)(2,1)}, u32[]{:S(2)}, u32[]{:S(2)}) collective-permute-start(bf16[2,32,2048]{2,1,0:T(8,128)(2,1)} %get-tuple-element.43), channel_id=1, source_target_pairs={{0,6},{2,4},{4,2},{6,0},{1,7},{3,5},{5,3},{7,1},{8,14},{10,12},{12... | collective-permute-start | bytes 786440 | tf_op jit(solution)/shard_map/ppermute | solution.py:246
  15.1 1.0 %copy-start.4 = (bf16[1,64,4096]{2,1,0:T(8,128)(2,1)S(1)}, bf16[1,64,4096]{2,1,0:T(8,128)(2,1)}, u32[]{:S(2)}) copy-start(bf16[1,64,4096]{2,1,0:T(8,128)(2,1)} %param.11) | copy-start | bytes 1572868
  16.1 39.7 %copy-start.1 = (bf16[1,3,2,32,4096]{4,3,2,1,0:T(8,128)(2,1)S(1)}, bf16[1,3,2,32,4096]{4,3,2,1,0:T(8,128)(2,1)}, u32[]{:S(2)}) copy-start(bf16[1,3,2,32,4096]{4,3,2,1,0:T(8,128)(2,1)} %param.9) | copy-start | bytes 4718596
  17.7 0.7 copy-start.6
  18.5 37.3 %copy-start = (bf16[1,3,2,32,4096]{4,3,2,1,0:T(8,128)(2,1)S(1)}, bf16[1,3,2,32,4096]{4,3,2,1,0:T(8,128)(2,1)}, u32[]{:S(2)}) copy-start(bf16[1,3,2,32,4096]{4,3,2,1,0:T(8,128)(2,1)} %param.8) | copy-start | bytes 4718596
  41.5 35.4 %collective-permute-start.1 = (bf16[2,32,4096]{2,1,0:T(8,128)(2,1)}, bf16[2,32,4096]{2,1,0:T(8,128)(2,1)}, u32[]{:S(2)}, u32[]{:S(2)}) collective-permute-start(bf16[2,32,4096]{2,1,0:T(8,128)(2,1)} %get-tuple-element.41), channel_id=1, source_target_pairs={{0,2},{2,0},{4,6},{6,4},{1,3},{3,1},{5,7},{7,5},{8,10},{10,8},{12,... | collective-permute-start | bytes 1572872 | tf_op jit(solution)/shard_map/ppermute | solution.py:246
  45.1 2.1 %collective-permute-start.7 = (f32[3]{0:T(128)S(1)}, f32[3]{0:T(128)S(1)}, u32[]{:S(2)}, u32[]{:S(2)}) collective-permute-start(f32[3]{0:T(128)S(1)} %get-tuple-element.51), channel_id=1, source_target_pairs={{0,8},{1,9},{2,10},{3,11},{4,12},{5,13},{6,14},{7,15},{16,24},{17,... | collective-permute-start | bytes 44 | tf_op jit(solution)/shard_map/ppermute | solution.py:350
  47.2 35.9 %collective-permute-start.10 = (bf16[2,2,4,64,128]{4,3,2,1,0:T(8,128)(2,1)}, bf16[2,2,4,64,128]{4,3,2,1,0:T(8,128)(2,1)}, u32[]{:S(2)}, u32[]{:S(2)}) collective-permute-start(bf16[2,2,4,64,128]{4,3,2,1,0:T(8,128)(2,1)} %get-tuple-element.59), channel_id=1, source_target_pairs={{0,2},{2,0},{4,6},{6,4},{1,3},{3,1},{5,7},{7,5},{8,10},{10,8},{12,... | collective-permute-start | bytes 786440 | tf_op jit(solution)/shard_map/ppermute | solution.py:246
  47.2 1.4 %copy-start.3 = (bf16[1,3,2,32,4096]{4,3,2,1,0:T(8,128)(2,1)S(1)}, bf16[1,3,2,32,4096]{4,3,2,1,0:T(8,128)(2,1)}, u32[]{:S(2)}) copy-start(bf16[1,3,2,32,4096]{4,3,2,1,0:T(8,128)(2,1)} %param.10) | copy-start | bytes 4718596
  48.6 1.0 %copy-start.5 = (bf16[1,64,4096]{2,1,0:T(8,128)(2,1)S(1)}, bf16[1,64,4096]{2,1,0:T(8,128)(2,1)}, u32[]{:S(2)}) copy-start(bf16[1,64,4096]{2,1,0:T(8,128)(2,1)} %param.11) | copy-start | bytes 1572868
  58.8 23.0 %collective-permute-start.9 = (f32[4,16,128]{2,1,0:T(8,128)S(1)}, f32[4,16,128]{2,1,0:T(8,128)S(1)}, u32[]{:S(2)}, u32[]{:S(2)}) collective-permute-start(f32[4,16,128]{2,1,0:T(8,128)S(1)} %get-tuple-element.56.near_ref), channel_id=1, source_target_pairs={{0,4},{2,6},{4,0},{6,2},{1,5},{3,7},{5,1},{7,3},{8,12},{10,14},{12... | collective-permute-start | bytes 98312 | tf_op jit(solution)/shard_map/ppermute | solution.py:246
  78.8 5.9 %collective-permute-start.4 = (f32[2,16,128]{2,1,0:T(8,128)S(1)}, f32[2,16,128]{2,1,0:T(8,128)S(1)}, u32[]{:S(2)}, u32[]{:S(2)}) collective-permute-start(f32[2,16,128]{2,1,0:T(8,128)S(1)} %get-tuple-element.46.refs_2_), channel_id=1, source_target_pairs={{0,4},{2,6},{4,0},{6,2},{1,5},{3,7},{5,1},{7,3},{8,12},{10,14},{12... | collective-permute-start | bytes 49160 | tf_op jit(solution)/shard_map/ppermute | solution.py:246
  81.1 5.0 %collective-permute-start.6 = (bf16[1,2,4,64,128]{4,3,2,1,0:T(8,128)(2,1)S(1)}, bf16[1,2,4,64,128]{4,3,2,1,0:T(8,128)(2,1)S(1)}, u32[]{:S(2)}, u32[]{:S(2)}) collective-permute-start(bf16[1,2,4,64,128]{4,3,2,1,0:T(8,128)(2,1)S(1)} %get-tuple-element.50), channel_id=1, source_target_pairs={{0,2},{2,0},{4,6},{6,4},{1,3},{3,1},{5,7},{7,5},{8,10},{10,8},{12,... | collective-permute-start | bytes 393224 | tf_op jit(solution)/shard_map/ppermute | solution.py:246
  81.8 1.3 %copy-start.7 = (bf16[2,2,4,64,128]{4,3,2,1,0:T(8,128)(2,1)S(1)}, bf16[2,2,4,64,128]{4,3,2,1,0:T(8,128)(2,1)}, u32[]{:S(2)}) copy-start(bf16[2,2,4,64,128]{4,3,2,1,0:T(8,128)(2,1)} %copy-done.6) | copy-start | bytes 786436
  86.1 7.9 %copy-start.8 = (f32[1,3,16,128]{3,2,1,0:T(8,128)S(1)}, f32[1,3,16,128]{3,2,1,0:T(8,128)}, u32[]{:S(2)}) copy-start(f32[1,3,16,128]{3,2,1,0:T(8,128)} %param.7) | copy-start | bytes 73732
  87.0 5.9 %collective-permute-start.11 = (f32[3,16,128]{2,1,0:T(8,128)S(1)}, f32[3,16,128]{2,1,0:T(8,128)S(1)}, u32[]{:S(2)}, u32[]{:S(2)}) collective-permute-start(f32[3,16,128]{2,1,0:T(8,128)S(1)} %get-tuple-element.64), channel_id=1, source_target_pairs={{0,6},{2,4},{4,2},{6,0},{1,7},{3,5},{5,3},{7,1},{8,14},{10,12},{12... | collective-permute-start | bytes 73736 | tf_op jit(solution)/shard_map/ppermute | solution.py:246
  88.9 4.7 %collective-permute-start.12 = (f32[3,16,128]{2,1,0:T(8,128)S(1)}, f32[3,16,128]{2,1,0:T(8,128)S(1)}, u32[]{:S(2)}, u32[]{:S(2)}) collective-permute-start(f32[3,16,128]{2,1,0:T(8,128)S(1)} %get-tuple-element.65), channel_id=1, source_target_pairs={{0,4},{2,6},{4,0},{6,2},{1,5},{3,7},{5,1},{7,3},{8,12},{10,14},{12... | collective-permute-start | bytes 73736 | tf_op jit(solution)/shard_map/ppermute | solution.py:246
  90.1 3.8 %collective-permute-start.13 = (f32[3,16,128]{2,1,0:T(8,128)S(1)}, f32[3,16,128]{2,1,0:T(8,128)S(1)}, u32[]{:S(2)}, u32[]{:S(2)}) collective-permute-start(f32[3,16,128]{2,1,0:T(8,128)S(1)} %get-tuple-element.66), channel_id=1, source_target_pairs={{0,2},{2,0},{4,6},{6,4},{1,3},{3,1},{5,7},{7,5},{8,10},{10,8},{12,... | collective-permute-start | bytes 73736 | tf_op jit(solution)/shard_map/ppermute | solution.py:246
  94.0 2.1 %collective-permute-start.14 = (f32[3,16,128]{2,1,0:T(8,128)S(1)}, f32[3,16,128]{2,1,0:T(8,128)S(1)}, u32[]{:S(2)}, u32[]{:S(2)}) collective-permute-start(f32[3,16,128]{2,1,0:T(8,128)S(1)} %bitcast_add_fusion), channel_id=1, source_target_pairs={{0,8},{1,9},{2,10},{3,11},{4,12},{5,13},{6,14},{7,15},{16,24},{17,... | collective-permute-start | bytes 73736 | tf_op jit(solution)/shard_map/ppermute | solution.py:362

commit v6 on v5

--- a/solution.py
+++ b/solution.py
@@ -66,11 +66,11 @@
     for s, out_ref in enumerate(out_refs, 1):
         start = pl.multiple_of(((me_ref[0] ^ s) & (group - 1)) * width, width)
         for n, ref in enumerate([q_ref, k_ref] if s < group else [q_ref]):
-            for i in range(out_ref.shape[0]):
+            for i in range(0, out_ref.shape[0], 2):
                 moves.append(
                     (
-                        ref.at[first + i, :, pl.ds(start, width)],
-                        out_ref.at[i, :, pl.ds(n * width, width)],
+                        ref.at[pl.ds(first + i, 2), :, pl.ds(start, width)],
+                        out_ref.at[pl.ds(i, 2), :, pl.ds(n * width, width)],
                     )
                 )
     through(moves, *scratch)
@@ -247,7 +247,7 @@
 
     def staging(number, width):
         return [
-            pltpu.VMEM((number, rows, width), jnp.bfloat16),
+            pltpu.VMEM((number, 2, rows, width), jnp.bfloat16),
             pltpu.SemaphoreType.DMA((number,)),
             pltpu.SemaphoreType.DMA((number,)),
         ]
@@ -260,7 +260,7 @@
             [shape(2 * many, rows, w) for w in wide],
             [SMEM, HBM, HBM],
             "pack",
-            scratch=staging(2 * many * (count + group - 2), width),
+            scratch=staging(many * (count + group - 2), width),
             moved=8 * many * rows * sum(wide),
             space=HBM,
             limit=None,
@@ -356,7 +356,7 @@
     far = exchange(near, half)
     shares = attend(early, late, half, [exponents, top, near, far], late_values, shares)
 
-    parts = [exchange(shares[s], s) for s in range(count - 1, 0, -1)] + [shares[0]]
+    parts = [exchange(shares[s], s) for s in [*range(count - 1, half, -1), *range(half - 1, 0, -1), half]] + [shares[0]]
     guided = functools.reduce(jnp.add, lax.optimization_barrier(parts))
     updated = latent[0] + step_size[:, None, None] * functools.reduce(jnp.add, parts)
     taken = lax.ppermute(updated, "section", [(0, 1)])

time: 97.2 us -> 96.8 us (level)
  transfers between devices with their start and end apart: 15 -> 15, of which waited for: 11 -> 10; matrix products, arithmetic and copies ran while one was open for 1% -> 1% of each run, Pallas kernels for 12% -> 12%
where the time goes in v6:
time: 96.8 us; the launch traced here: 96.4 us
  waiting for transfers between devices  38.9 us (40%)
  starting transfers between devices  36.4 us (38%)
  Pallas kernels  14.7 us (15%)
  local copies, waits for them, and re-layouts  4.25 us (4%)
  other arithmetic  1.39 us (1%)
    ppermute x13, waiting for transfers between devices, exchange(): return lax.ppermute(array, 'sp', [(i, i ^ s) for i in range(count)])  37.8 us
    ppermute x13, starting transfers between devices, exchange(): return lax.ppermute(array, 'sp', [(i, i ^ s) for i in range(count)])  33.8 us
    pallas_call x2, Pallas kernels, score(): call(functools.partial(score_kernel, first, count, group, width), outs, [...  4.78 us
    pallas_call x2, Pallas kernels, pack(): call(functools.partial(pack_kernel, 2 * first, group, width), [shape(2 *...  4.62 us
    unnamed x22, local copies, waits for them, and re-layouts  4.25 us
    pallas_call x2, Pallas kernels, attend(): call(functools.partial(attend_kernel, first, count, group, len(weights)),...  2.55 us
    pallas_call x2, Pallas kernels, project(): call(functools.partial(project_kernel, first, group, width), [shape(many,...  2.18 us
  transfers between devices with their start and end apart: 15, of which 10 were waited for; matrix products, arithmetic and copies ran while one was open for 1% of the time, Pallas kernels for 12%

profile of v6, /device:TPU:0, one launch (start us, length us, event | category | flops | bytes accessed | tf_op | source)
XLA Modules:
  0.0 96.4 jit_solution(6340883926202200859)
XLA Ops:
  0.6 2.5 %pack.2 = (bf16[4,32,4096]{2,1,0:T(8,128)(2,1)}, bf16[4,32,2048]{2,1,0:T(8,128)(2,1)}, bf16[4,32,2048]{2,1,0:T(8,128)(2,1)}) custom-call(s32[1]{0:T(128)} %bitcast.1.me_ref, bf16[6,32,4096]{2,1,0:T(8,128)(2,1)} %bitcast.16, bf16[6,32,4096]{2,1,0:T(8,128)(2,1)} %bitcast.20), custom_call_target="tpu_custom_call" | custom-call | bytes 4194304 | tf_op jit(solution)/shard_map/pack/pallas_call | solution.py:258
  3.1 3.1 %collective-permute-start.5 = (bf16[4,32,4096]{2,1,0:T(8,128)(2,1)}, bf16[4,32,4096]{2,1,0:T(8,128)(2,1)}, u32[]{:S(2)}, u32[]{:S(2)}) collective-permute-start(bf16[4,32,4096]{2,1,0:T(8,128)(2,1)} %get-tuple-element.37), channel_id=1, source_target_pairs={{0,2},{2,0},{4,6},{6,4},{1,3},{3,1},{5,7},{7,5},{8,10},{10,8},{12,... | collective-permute-start | bytes 3145736 | tf_op jit(solution)/shard_map/ppermute | solution.py:246
  6.2 2.6 %collective-permute-start = (bf16[4,32,2048]{2,1,0:T(8,128)(2,1)}, bf16[4,32,2048]{2,1,0:T(8,128)(2,1)}, u32[]{:S(2)}, u32[]{:S(2)}) collective-permute-start(bf16[4,32,2048]{2,1,0:T(8,128)(2,1)} %get-tuple-element.40), channel_id=1, source_target_pairs={{0,4},{2,6},{4,0},{6,2},{1,5},{3,7},{5,1},{7,3},{8,12},{10,14},{12... | collective-permute-start | bytes 1572872 | tf_op jit(solution)/shard_map/ppermute | solution.py:246
  8.8 2.2 %pack.3 = (bf16[2,32,4096]{2,1,0:T(8,128)(2,1)}, bf16[2,32,2048]{2,1,0:T(8,128)(2,1)}, bf16[2,32,2048]{2,1,0:T(8,128)(2,1)}) custom-call(s32[1]{0:T(128)} %bitcast.1.me_ref, bf16[6,32,4096]{2,1,0:T(8,128)(2,1)} %bitcast.17, bf16[6,32,4096]{2,1,0:T(8,128)(2,1)} %bitcast.21), custom_call_target="tpu_custom_call" | custom-call | bytes 2097152 | tf_op jit(solution)/shard_map/pack/pallas_call | solution.py:258
  11.0 1.9 %collective-permute-start.2 = (bf16[2,32,2048]{2,1,0:T(8,128)(2,1)}, bf16[2,32,2048]{2,1,0:T(8,128)(2,1)S(1)}, u32[]{:S(2)}, u32[]{:S(2)}) collective-permute-start(bf16[2,32,2048]{2,1,0:T(8,128)(2,1)} %get-tuple-element.42), channel_id=1, source_target_pairs={{0,4},{2,6},{4,0},{6,2},{1,5},{3,7},{5,1},{7,3},{8,12},{10,14},{12... | collective-permute-start | bytes 786440 | tf_op jit(solution)/shard_map/ppermute | solution.py:246
  12.8 2.0 %collective-permute-start.3 = (bf16[2,32,2048]{2,1,0:T(8,128)(2,1)}, bf16[2,32,2048]{2,1,0:T(8,128)(2,1)}, u32[]{:S(2)}, u32[]{:S(2)}) collective-permute-start(bf16[2,32,2048]{2,1,0:T(8,128)(2,1)} %get-tuple-element.43), channel_id=1, source_target_pairs={{0,6},{2,4},{4,2},{6,0},{1,7},{3,5},{5,3},{7,1},{8,14},{10,12},{12... | collective-permute-start | bytes 786440 | tf_op jit(solution)/shard_map/ppermute | solution.py:246
  14.8 1.0 %copy-done.4 = bf16[1,64,4096]{2,1,0:T(8,128)(2,1)S(1)} copy-done((bf16[1,64,4096]{2,1,0:T(8,128)(2,1)S(1)}, bf16[1,64,4096]{2,1,0:T(8,128)(2,1)}, u32[]{:S(2)}) %copy-start.4) | copy-done | bytes 524312
  15.9 1.6 %project.3 = (bf16[2,2,4,64,128]{4,3,2,1,0:T(8,128)(2,1)S(1)}, bf16[2,2,4,64,128]{4,3,2,1,0:T(8,128)(2,1)}) custom-call(s32[1]{0:T(128)} %bitcast.1.me_ref, bf16[6,32,4096]{2,1,0:T(8,128)(2,1)S(1)} %bitcast.24, bf16[64,4096]{1,0:T(8,128)(2,1)S(1)} %bitcast.26), custom_call_target="tpu_custom_call" | custom-call | flops 268435456 | bytes 1572864 | tf_op jit(solution)/shard_map/project/pallas_call | solution.py:271
  17.5 0.7 copy-done.6
  18.2 23.1 %collective-permute-done.refs_1_ = bf16[4,32,2048]{2,1,0:T(8,128)(2,1)} collective-permute-done((bf16[4,32,2048]{2,1,0:T(8,128)(2,1)}, bf16[4,32,2048]{2,1,0:T(8,128)(2,1)}, u32[]{:S(2)}, u32[]{:S(2)}) %collective-permute-start) | collective-permute-done | bytes 524320 | tf_op jit(solution)/shard_map/ppermute | solution.py:246
  41.4 3.5 %collective-permute-start.1 = (bf16[2,32,4096]{2,1,0:T(8,128)(2,1)}, bf16[2,32,4096]{2,1,0:T(8,128)(2,1)}, u32[]{:S(2)}, u32[]{:S(2)}) collective-permute-start(bf16[2,32,4096]{2,1,0:T(8,128)(2,1)} %get-tuple-element.41), channel_id=1, source_target_pairs={{0,2},{2,0},{4,6},{6,4},{1,3},{3,1},{5,7},{7,5},{8,10},{10,8},{12,... | collective-permute-start | bytes 1572872 | tf_op jit(solution)/shard_map/ppermute | solution.py:246
  44.9 1.3 %collective-permute-start.7 = (f32[3]{0:T(128)S(1)}, f32[3]{0:T(128)S(1)}, u32[]{:S(2)}, u32[]{:S(2)}) collective-permute-start(f32[3]{0:T(128)S(1)} %get-tuple-element.51), channel_id=1, source_target_pairs={{0,8},{1,9},{2,10},{3,11},{4,12},{5,13},{6,14},{7,15},{16,24},{17,... | collective-permute-start | bytes 44 | tf_op jit(solution)/shard_map/ppermute | solution.py:350
  46.2 0.8 collective-permute-done.7
  47.1 1.4 %copy-done.3 = bf16[1,3,2,32,4096]{4,3,2,1,0:T(8,128)(2,1)S(1)} copy-done((bf16[1,3,2,32,4096]{4,3,2,1,0:T(8,128)(2,1)S(1)}, bf16[1,3,2,32,4096]{4,3,2,1,0:T(8,128)(2,1)}, u32[]{:S(2)}) %copy-start.3) | copy-done | bytes 1572888
  48.5 1.0 %copy-done.5 = bf16[1,64,4096]{2,1,0:T(8,128)(2,1)S(1)} copy-done((bf16[1,64,4096]{2,1,0:T(8,128)(2,1)S(1)}, bf16[1,64,4096]{2,1,0:T(8,128)(2,1)}, u32[]{:S(2)}) %copy-start.5) | copy-done | bytes 524312
  50.1 5.6 %collective-permute-done.8.refs_2_ = bf16[4,32,2048]{2,1,0:T(8,128)(2,1)} collective-permute-done((bf16[4,32,2048]{2,1,0:T(8,128)(2,1)}, bf16[4,32,2048]{2,1,0:T(8,128)(2,1)}, u32[]{:S(2)}, u32[]{:S(2)}) %collective-permute-start.8) | collective-permute-done | bytes 524320 | tf_op jit(solution)/shard_map/ppermute | solution.py:246
  55.6 3.0 %score.3 = (f32[4,4,2,128,128]{4,3,2,1,0:T(8,128)S(1)}, f32[4,16,128]{2,1,0:T(8,128)S(1)}, f32[4,16,128]{2,1,0:T(8,128)S(1)}) custom-call(s32[1]{0:T(128)} %bitcast.1.me_ref, bf16[6,32,4096]{2,1,0:T(8,128)(2,1)S(1)} %bitcast.18, bf16[6,32,4096]{2,1,0:T(8,128)(2,1)S(1)} %bitcast.22, bf16[4,32,4096]{2,1,0:T(8,128)(2,1)} %collective-permute-done.5.refs_0_, ...), custom_call_target="tpu_custom_call" | custom-call | flops 1073741824 | bytes 4194304 | tf_op jit(solution)/shard_map/score/pallas_call | solution.py:292
  58.6 13.3 %collective-permute-start.9 = (f32[4,16,128]{2,1,0:T(8,128)S(1)}, f32[4,16,128]{2,1,0:T(8,128)S(1)}, u32[]{:S(2)}, u32[]{:S(2)}) collective-permute-start(f32[4,16,128]{2,1,0:T(8,128)S(1)} %get-tuple-element.56.near_ref), channel_id=1, source_target_pairs={{0,4},{2,6},{4,0},{6,2},{1,5},{3,7},{5,1},{7,3},{8,12},{10,14},{12... | collective-permute-start | bytes 98312 | tf_op jit(solution)/shard_map/ppermute | solution.py:246
  71.9 0.9 collective-permute-done.2.refs_1_
  72.8 3.9 %collective-permute-done.1.refs_0_ = bf16[2,32,4096]{2,1,0:T(8,128)(2,1)} collective-permute-done((bf16[2,32,4096]{2,1,0:T(8,128)(2,1)}, bf16[2,32,4096]{2,1,0:T(8,128)(2,1)}, u32[]{:S(2)}, u32[]{:S(2)}) %collective-permute-start.1) | collective-permute-done | bytes 524320 | tf_op jit(solution)/shard_map/ppermute | solution.py:246
  76.8 1.8 %score.2 = (f32[2,4,2,128,128]{4,3,2,1,0:T(8,128)S(1)}, f32[2,16,128]{2,1,0:T(8,128)S(1)}, f32[2,16,128]{2,1,0:T(8,128)S(1)}) custom-call(s32[1]{0:T(128)} %bitcast.1.me_ref, bf16[6,32,4096]{2,1,0:T(8,128)(2,1)S(1)} %bitcast.19, bf16[6,32,4096]{2,1,0:T(8,128)(2,1)S(1)} %bitcast.23, bf16[2,32,4096]{2,1,0:T(8,128)(2,1)} %collective-permute-done.1.refs_0_, ...), custom_call_target="tpu_custom_call" | custom-call | flops 536870912 | bytes 2097152 | tf_op jit(solution)/shard_map/score/pallas_call | solution.py:292
  78.6 2.3 %collective-permute-start.4 = (f32[2,16,128]{2,1,0:T(8,128)S(1)}, f32[2,16,128]{2,1,0:T(8,128)S(1)}, u32[]{:S(2)}, u32[]{:S(2)}) collective-permute-start(f32[2,16,128]{2,1,0:T(8,128)S(1)} %get-tuple-element.46.refs_2_), channel_id=1, source_target_pairs={{0,4},{2,6},{4,0},{6,2},{1,5},{3,7},{5,1},{7,3},{8,12},{10,14},{12... | collective-permute-start | bytes 49160 | tf_op jit(solution)/shard_map/ppermute | solution.py:246
  82.2 0.7 collective-permute-done.10.refs_2_
  82.9 1.6 %attend.2 = (f32[2,16,128]{2,1,0:T(8,128)S(1)}, f32[2,16,128]{2,1,0:T(8,128)S(1)}, f32[2,16,128]{2,1,0:T(8,128)S(1)}, f32[2,16,128]{2,1,0:T(8,128)S(1)}) custom-call(f32[1]{0:T(128)} %bitcast.scale_ref, s32[3]{0:T(128)S(1)} %broadcast_select_fusion.skip_ref, bf16[4,1024,128]{2,1,0:T(8,128)(2,1)S(1)} %weigh.1.refs_0_, ...), custom_call_target="tpu_custom_call" | custom-call | flops 2147483648 | bytes 2097152 | tf_op jit(solution)/shard_map/attend/pallas_call | solution.py:306
  84.5 1.4 %collective-permute-done.6.refs_5_ = bf16[1,2,4,64,128]{4,3,2,1,0:T(8,128)(2,1)S(1)} collective-permute-done((bf16[1,2,4,64,128]{4,3,2,1,0:T(8,128)(2,1)S(1)}, bf16[1,2,4,64,128]{4,3,2,1,0:T(8,128)(2,1)S(1)}, u32[]{:S(2)}, u32[]{:S(2)}) %collective-permute-start.6) | collective-permute-done | bytes 131104 | tf_op jit(solution)/shard_map/ppermute | solution.py:246
  85.9 0.9 attend.3
  86.9 1.9 %collective-permute-start.11 = (f32[3,16,128]{2,1,0:T(8,128)S(1)}, f32[3,16,128]{2,1,0:T(8,128)S(1)}, u32[]{:S(2)}, u32[]{:S(2)}) collective-permute-start(f32[3,16,128]{2,1,0:T(8,128)S(1)} %get-tuple-element.64), channel_id=1, source_target_pairs={{0,6},{2,4},{4,2},{6,0},{1,7},{3,5},{5,3},{7,1},{8,14},{10,12},{12... | collective-permute-start | bytes 73736 | tf_op jit(solution)/shard_map/ppermute | solution.py:246
  88.8 2.5 %collective-permute-start.13 = (f32[3,16,128]{2,1,0:T(8,128)S(1)}, f32[3,16,128]{2,1,0:T(8,128)S(1)}, u32[]{:S(2)}, u32[]{:S(2)}) collective-permute-start(f32[3,16,128]{2,1,0:T(8,128)S(1)} %get-tuple-element.66), channel_id=1, source_target_pairs={{0,4},{2,6},{4,0},{6,2},{1,5},{3,7},{5,1},{7,3},{8,12},{10,14},{12... | collective-permute-start | bytes 73736 | tf_op jit(solution)/shard_map/ppermute | solution.py:246
  91.3 1.5 %collective-permute-done.11 = f32[3,16,128]{2,1,0:T(8,128)S(1)} collective-permute-done((f32[3,16,128]{2,1,0:T(8,128)S(1)}, f32[3,16,128]{2,1,0:T(8,128)S(1)}, u32[]{:S(2)}, u32[]{:S(2)}) %collective-permute-start.11) | collective-permute-done | bytes 24608 | tf_op jit(solution)/shard_map/ppermute | solution.py:246
  92.8 0.7 collective-permute-done.13
  93.6 1.3 %collective-permute-start.14 = (f32[3,16,128]{2,1,0:T(8,128)S(1)}, f32[3,16,128]{2,1,0:T(8,128)S(1)}, u32[]{:S(2)}, u32[]{:S(2)}) collective-permute-start(f32[3,16,128]{2,1,0:T(8,128)S(1)} %bitcast_add_fusion), channel_id=1, source_target_pairs={{0,8},{1,9},{2,10},{3,11},{4,12},{5,13},{6,14},{7,15},{16,24},{17,... | collective-permute-start | bytes 73736 | tf_op jit(solution)/shard_map/ppermute | solution.py:362
  95.7 0.7 select_bitcast_fusion
  (35 shorter events, 2.8 us)
Async XLA Ops:
  3.1 41.8 %collective-permute-start.5 = (bf16[4,32,4096]{2,1,0:T(8,128)(2,1)}, bf16[4,32,4096]{2,1,0:T(8,128)(2,1)}, u32[]{:S(2)}, u32[]{:S(2)}) collective-permute-start(bf16[4,32,4096]{2,1,0:T(8,128)(2,1)} %get-tuple-element.37), channel_id=1, source_target_pairs={{0,2},{2,0},{4,6},{6,4},{1,3},{3,1},{5,7},{7,5},{8,10},{10,8},{12,... | collective-permute-start | bytes 3145736 | tf_op jit(solution)/shard_map/ppermute | solution.py:246
  6.2 35.2 %collective-permute-start = (bf16[4,32,2048]{2,1,0:T(8,128)(2,1)}, bf16[4,32,2048]{2,1,0:T(8,128)(2,1)}, u32[]{:S(2)}, u32[]{:S(2)}) collective-permute-start(bf16[4,32,2048]{2,1,0:T(8,128)(2,1)} %get-tuple-element.40), channel_id=1, source_target_pairs={{0,4},{2,6},{4,0},{6,2},{1,5},{3,7},{5,1},{7,3},{8,12},{10,14},{12... | collective-permute-start | bytes 1572872 | tf_op jit(solution)/shard_map/ppermute | solution.py:246
  8.8 6.0 %copy-start.2 = (bf16[1,3,2,32,4096]{4,3,2,1,0:T(8,128)(2,1)S(1)}, bf16[1,3,2,32,4096]{4,3,2,1,0:T(8,128)(2,1)}, u32[]{:S(2)}) copy-start(bf16[1,3,2,32,4096]{4,3,2,1,0:T(8,128)(2,1)} %param.10) | copy-start | bytes 4718596
  8.8 46.8 %collective-permute-start.8 = (bf16[4,32,2048]{2,1,0:T(8,128)(2,1)}, bf16[4,32,2048]{2,1,0:T(8,128)(2,1)}, u32[]{:S(2)}, u32[]{:S(2)}) collective-permute-start(bf16[4,32,2048]{2,1,0:T(8,128)(2,1)} %get-tuple-element.53), channel_id=1, source_target_pairs={{0,6},{2,4},{4,2},{6,0},{1,7},{3,5},{5,3},{7,1},{8,14},{10,12},{12... | collective-permute-start | bytes 1572872 | tf_op jit(solution)/shard_map/ppermute | solution.py:246
  11.0 34.0 %copy-start.9 = (s32[1,3]{1,0:T(1,128)S(1)}, s32[1,3]{1,0:T(1,128)}, u32[]{:S(2)}) copy-start(s32[1,3]{1,0:T(1,128)} %param.12) | copy-start | bytes 40
  11.0 36.1 %copy-start.10 = (s32[3]{0:T(128)S(1)}, s32[3]{0:T(128)}, u32[]{:S(2)}) copy-start(s32[3]{0:T(128)} %param.13) | copy-start | bytes 40
  11.0 61.8 %collective-permute-start.2 = (bf16[2,32,2048]{2,1,0:T(8,128)(2,1)}, bf16[2,32,2048]{2,1,0:T(8,128)(2,1)S(1)}, u32[]{:S(2)}, u32[]{:S(2)}) collective-permute-start(bf16[2,32,2048]{2,1,0:T(8,128)(2,1)} %get-tuple-element.42), channel_id=1, source_target_pairs={{0,4},{2,6},{4,0},{6,2},{1,5},{3,7},{5,1},{7,3},{8,12},{10,14},{12... | collective-permute-start | bytes 786440 | tf_op jit(solution)/shard_map/ppermute | solution.py:246
  12.8 60.0 %collective-permute-start.3 = (bf16[2,32,2048]{2,1,0:T(8,128)(2,1)}, bf16[2,32,2048]{2,1,0:T(8,128)(2,1)}, u32[]{:S(2)}, u32[]{:S(2)}) collective-permute-start(bf16[2,32,2048]{2,1,0:T(8,128)(2,1)} %get-tuple-element.43), channel_id=1, source_target_pairs={{0,6},{2,4},{4,2},{6,0},{1,7},{3,5},{5,3},{7,1},{8,14},{10,12},{12... | collective-permute-start | bytes 786440 | tf_op jit(solution)/shard_map/ppermute | solution.py:246
  14.8 1.0 %copy-start.4 = (bf16[1,64,4096]{2,1,0:T(8,128)(2,1)S(1)}, bf16[1,64,4096]{2,1,0:T(8,128)(2,1)}, u32[]{:S(2)}) copy-start(bf16[1,64,4096]{2,1,0:T(8,128)(2,1)} %param.11) | copy-start | bytes 1572868
  15.9 39.8 %copy-start.1 = (bf16[1,3,2,32,4096]{4,3,2,1,0:T(8,128)(2,1)S(1)}, bf16[1,3,2,32,4096]{4,3,2,1,0:T(8,128)(2,1)}, u32[]{:S(2)}) copy-start(bf16[1,3,2,32,4096]{4,3,2,1,0:T(8,128)(2,1)} %param.9) | copy-start | bytes 4718596
  17.5 0.7 copy-start.6
  18.2 37.4 %copy-start = (bf16[1,3,2,32,4096]{4,3,2,1,0:T(8,128)(2,1)S(1)}, bf16[1,3,2,32,4096]{4,3,2,1,0:T(8,128)(2,1)}, u32[]{:S(2)}) copy-start(bf16[1,3,2,32,4096]{4,3,2,1,0:T(8,128)(2,1)} %param.8) | copy-start | bytes 4718596
  41.4 35.4 %collective-permute-start.1 = (bf16[2,32,4096]{2,1,0:T(8,128)(2,1)}, bf16[2,32,4096]{2,1,0:T(8,128)(2,1)}, u32[]{:S(2)}, u32[]{:S(2)}) collective-permute-start(bf16[2,32,4096]{2,1,0:T(8,128)(2,1)} %get-tuple-element.41), channel_id=1, source_target_pairs={{0,2},{2,0},{4,6},{6,4},{1,3},{3,1},{5,7},{7,5},{8,10},{10,8},{12,... | collective-permute-start | bytes 1572872 | tf_op jit(solution)/shard_map/ppermute | solution.py:246
  44.9 2.1 %collective-permute-start.7 = (f32[3]{0:T(128)S(1)}, f32[3]{0:T(128)S(1)}, u32[]{:S(2)}, u32[]{:S(2)}) collective-permute-start(f32[3]{0:T(128)S(1)} %get-tuple-element.51), channel_id=1, source_target_pairs={{0,8},{1,9},{2,10},{3,11},{4,12},{5,13},{6,14},{7,15},{16,24},{17,... | collective-permute-start | bytes 44 | tf_op jit(solution)/shard_map/ppermute | solution.py:350
  47.0 35.9 %collective-permute-start.10 = (bf16[2,2,4,64,128]{4,3,2,1,0:T(8,128)(2,1)}, bf16[2,2,4,64,128]{4,3,2,1,0:T(8,128)(2,1)}, u32[]{:S(2)}, u32[]{:S(2)}) collective-permute-start(bf16[2,2,4,64,128]{4,3,2,1,0:T(8,128)(2,1)} %get-tuple-element.59), channel_id=1, source_target_pairs={{0,2},{2,0},{4,6},{6,4},{1,3},{3,1},{5,7},{7,5},{8,10},{10,8},{12,... | collective-permute-start | bytes 786440 | tf_op jit(solution)/shard_map/ppermute | solution.py:246
  47.1 1.4 %copy-start.3 = (bf16[1,3,2,32,4096]{4,3,2,1,0:T(8,128)(2,1)S(1)}, bf16[1,3,2,32,4096]{4,3,2,1,0:T(8,128)(2,1)}, u32[]{:S(2)}) copy-start(bf16[1,3,2,32,4096]{4,3,2,1,0:T(8,128)(2,1)} %param.10) | copy-start | bytes 4718596
  48.5 1.0 %copy-start.5 = (bf16[1,64,4096]{2,1,0:T(8,128)(2,1)S(1)}, bf16[1,64,4096]{2,1,0:T(8,128)(2,1)}, u32[]{:S(2)}) copy-start(bf16[1,64,4096]{2,1,0:T(8,128)(2,1)} %param.11) | copy-start | bytes 1572868
  58.6 23.0 %collective-permute-start.9 = (f32[4,16,128]{2,1,0:T(8,128)S(1)}, f32[4,16,128]{2,1,0:T(8,128)S(1)}, u32[]{:S(2)}, u32[]{:S(2)}) collective-permute-start(f32[4,16,128]{2,1,0:T(8,128)S(1)} %get-tuple-element.56.near_ref), channel_id=1, source_target_pairs={{0,4},{2,6},{4,0},{6,2},{1,5},{3,7},{5,1},{7,3},{8,12},{10,14},{12... | collective-permute-start | bytes 98312 | tf_op jit(solution)/shard_map/ppermute | solution.py:246
  78.6 5.9 %collective-permute-start.4 = (f32[2,16,128]{2,1,0:T(8,128)S(1)}, f32[2,16,128]{2,1,0:T(8,128)S(1)}, u32[]{:S(2)}, u32[]{:S(2)}) collective-permute-start(f32[2,16,128]{2,1,0:T(8,128)S(1)} %get-tuple-element.46.refs_2_), channel_id=1, source_target_pairs={{0,4},{2,6},{4,0},{6,2},{1,5},{3,7},{5,1},{7,3},{8,12},{10,14},{12... | collective-permute-start | bytes 49160 | tf_op jit(solution)/shard_map/ppermute | solution.py:246
  80.9 5.0 %collective-permute-start.6 = (bf16[1,2,4,64,128]{4,3,2,1,0:T(8,128)(2,1)S(1)}, bf16[1,2,4,64,128]{4,3,2,1,0:T(8,128)(2,1)S(1)}, u32[]{:S(2)}, u32[]{:S(2)}) collective-permute-start(bf16[1,2,4,64,128]{4,3,2,1,0:T(8,128)(2,1)S(1)} %get-tuple-element.50), channel_id=1, source_target_pairs={{0,2},{2,0},{4,6},{6,4},{1,3},{3,1},{5,7},{7,5},{8,10},{10,8},{12,... | collective-permute-start | bytes 393224 | tf_op jit(solution)/shard_map/ppermute | solution.py:246
  81.6 1.3 %copy-start.7 = (bf16[2,2,4,64,128]{4,3,2,1,0:T(8,128)(2,1)S(1)}, bf16[2,2,4,64,128]{4,3,2,1,0:T(8,128)(2,1)}, u32[]{:S(2)}) copy-start(bf16[2,2,4,64,128]{4,3,2,1,0:T(8,128)(2,1)} %copy-done.6) | copy-start | bytes 786436
  85.9 7.6 %copy-start.8 = (f32[1,3,16,128]{3,2,1,0:T(8,128)S(1)}, f32[1,3,16,128]{3,2,1,0:T(8,128)}, u32[]{:S(2)}) copy-start(f32[1,3,16,128]{3,2,1,0:T(8,128)} %param.7) | copy-start | bytes 73732
  86.9 5.9 %collective-permute-start.11 = (f32[3,16,128]{2,1,0:T(8,128)S(1)}, f32[3,16,128]{2,1,0:T(8,128)S(1)}, u32[]{:S(2)}, u32[]{:S(2)}) collective-permute-start(f32[3,16,128]{2,1,0:T(8,128)S(1)} %get-tuple-element.64), channel_id=1, source_target_pairs={{0,6},{2,4},{4,2},{6,0},{1,7},{3,5},{5,3},{7,1},{8,14},{10,12},{12... | collective-permute-start | bytes 73736 | tf_op jit(solution)/shard_map/ppermute | solution.py:246
  88.8 4.0 %collective-permute-start.12 = (f32[3,16,128]{2,1,0:T(8,128)S(1)}, f32[3,16,128]{2,1,0:T(8,128)S(1)}, u32[]{:S(2)}, u32[]{:S(2)}) collective-permute-start(f32[3,16,128]{2,1,0:T(8,128)S(1)} %get-tuple-element.65), channel_id=1, source_target_pairs={{0,2},{2,0},{4,6},{6,4},{1,3},{3,1},{5,7},{7,5},{8,10},{10,8},{12,... | collective-permute-start | bytes 73736 | tf_op jit(solution)/shard_map/ppermute | solution.py:246
  88.8 4.7 %collective-permute-start.13 = (f32[3,16,128]{2,1,0:T(8,128)S(1)}, f32[3,16,128]{2,1,0:T(8,128)S(1)}, u32[]{:S(2)}, u32[]{:S(2)}) collective-permute-start(f32[3,16,128]{2,1,0:T(8,128)S(1)} %get-tuple-element.66), channel_id=1, source_target_pairs={{0,4},{2,6},{4,0},{6,2},{1,5},{3,7},{5,1},{7,3},{8,12},{10,14},{12... | collective-permute-start | bytes 73736 | tf_op jit(solution)/shard_map/ppermute | solution.py:246
  93.6 2.1 %collective-permute-start.14 = (f32[3,16,128]{2,1,0:T(8,128)S(1)}, f32[3,16,128]{2,1,0:T(8,128)S(1)}, u32[]{:S(2)}, u32[]{:S(2)}) collective-permute-start(f32[3,16,128]{2,1,0:T(8,128)S(1)} %bitcast_add_fusion), channel_id=1, source_target_pairs={{0,8},{1,9},{2,10},{3,11},{4,12},{5,13},{6,14},{7,15},{16,24},{17,... | collective-permute-start | bytes 73736 | tf_op jit(solution)/shard_map/ppermute | solution.py:362

commit v7 on v6

--- a/solution.py
+++ b/solution.py
@@ -195,16 +195,17 @@
         conditional, unconditional = sums
         guided = unconditional + scale_ref[0] * (conditional - unconditional)
         guided = jnp.where(skip_ref[first + v] == 1, conditional, guided)
-        scratch[...] = jnp.concatenate([guided, guided], axis=0).T
-        even = scratch[pl.ds(0, length // 2, stride=2), :]
-        odd = scratch[pl.ds(1, length // 2, stride=2), :]
+        scratch[v] = jnp.concatenate([guided, guided], axis=0).T
+        even = scratch[v, pl.ds(0, length // 2, stride=2), :]
+        odd = scratch[v, pl.ds(1, length // 2, stride=2), :]
         column = lax.broadcasted_iota(jnp.int32, even.shape, 1)
         both = jnp.where(column < CH, even, odd)
         for s in range(count):
             out_refs[s][offset + v] = both[s * rows // 2 : (s + 1) * rows // 2]
         return carry
 
-    lax.fori_loop(0, items // 2, one, 0)
+    for v in range(items // 2):
+        one(v, 0)
     for before_ref, out_ref in zip(before_refs, out_refs):
         out_ref[0:first] = before_ref[...]
 
@@ -308,7 +309,7 @@
             [shape(total, rows // 2, 2 * CH, dtype=jnp.float32)] * count,
             [SMEM, SMEM] + [VMEM] * (len(weights) + group + len(before)),
             "attend",
-            scratch=[pltpu.VMEM((length, 2 * CH), jnp.float32)],
+            scratch=[pltpu.VMEM((many, length, 2 * CH), jnp.float32)],
             flops=16 * many * feature_all * length * HD,
             moved=8 * many * rows * feature_all,
         )(guidance[None], skipping, *weights, *projected, *before)

time: 96.8 us -> 96.8 us (level)
  transfers between devices with their start and end apart: 15 -> 15, of which waited for: 10 -> 10; matrix products, arithmetic and copies ran while one was open for 1% -> 1% of each run, Pallas kernels for 12% -> 11%
where the time goes in v7:
time: 96.8 us; the launch traced here: 96.4 us
  waiting for transfers between devices  39.1 us (40%)
  starting transfers between devices  36.4 us (38%)
  Pallas kernels  14.5 us (15%)
  local copies, waits for them, and re-layouts  4.25 us (4%)
  other arithmetic  1.39 us (1%)
    ppermute x13, waiting for transfers between devices, exchange(): return lax.ppermute(array, 'sp', [(i, i ^ s) for i in range(count)])  38.1 us
    ppermute x13, starting transfers between devices, exchange(): return lax.ppermute(array, 'sp', [(i, i ^ s) for i in range(count)])  33.8 us
    pallas_call x2, Pallas kernels, score(): call(functools.partial(score_kernel, first, count, group, width), outs, [...  4.78 us
    pallas_call x2, Pallas kernels, pack(): call(functools.partial(pack_kernel, 2 * first, group, width), [shape(2 *...  4.62 us
    unnamed x22, local copies, waits for them, and re-layouts  4.25 us
    pallas_call x2, Pallas kernels, attend(): call(functools.partial(attend_kernel, first, count, group, len(weights)),...  2.34 us
    pallas_call x2, Pallas kernels, project(): call(functools.partial(project_kernel, first, group, width), [shape(many,...  2.18 us
  transfers between devices with their start and end apart: 15, of which 10 were waited for; matrix products, arithmetic and copies ran while one was open for 1% of the time, Pallas kernels for 11%

profile of v7, /device:TPU:0, one launch (start us, length us, event | category | flops | bytes accessed | tf_op | source)
XLA Modules:
  0.0 96.4 jit_solution(12954503621354683010)
XLA Ops:
  0.6 2.5 %pack.2 = (bf16[4,32,4096]{2,1,0:T(8,128)(2,1)}, bf16[4,32,2048]{2,1,0:T(8,128)(2,1)}, bf16[4,32,2048]{2,1,0:T(8,128)(2,1)}) custom-call(s32[1]{0:T(128)} %bitcast.1.me_ref, bf16[6,32,4096]{2,1,0:T(8,128)(2,1)} %bitcast.16, bf16[6,32,4096]{2,1,0:T(8,128)(2,1)} %bitcast.20), custom_call_target="tpu_custom_call" | custom-call | bytes 4194304 | tf_op jit(solution)/shard_map/pack/pallas_call | solution.py:259
  3.1 3.1 %collective-permute-start.5 = (bf16[4,32,4096]{2,1,0:T(8,128)(2,1)}, bf16[4,32,4096]{2,1,0:T(8,128)(2,1)}, u32[]{:S(2)}, u32[]{:S(2)}) collective-permute-start(bf16[4,32,4096]{2,1,0:T(8,128)(2,1)} %get-tuple-element.37), channel_id=1, source_target_pairs={{0,2},{2,0},{4,6},{6,4},{1,3},{3,1},{5,7},{7,5},{8,10},{10,8},{12,... | collective-permute-start | bytes 3145736 | tf_op jit(solution)/shard_map/ppermute | solution.py:247
  6.2 2.6 %collective-permute-start = (bf16[4,32,2048]{2,1,0:T(8,128)(2,1)}, bf16[4,32,2048]{2,1,0:T(8,128)(2,1)}, u32[]{:S(2)}, u32[]{:S(2)}) collective-permute-start(bf16[4,32,2048]{2,1,0:T(8,128)(2,1)} %get-tuple-element.40), channel_id=1, source_target_pairs={{0,4},{2,6},{4,0},{6,2},{1,5},{3,7},{5,1},{7,3},{8,12},{10,14},{12... | collective-permute-start | bytes 1572872 | tf_op jit(solution)/shard_map/ppermute | solution.py:247
  8.8 2.2 %pack.3 = (bf16[2,32,4096]{2,1,0:T(8,128)(2,1)}, bf16[2,32,2048]{2,1,0:T(8,128)(2,1)}, bf16[2,32,2048]{2,1,0:T(8,128)(2,1)}) custom-call(s32[1]{0:T(128)} %bitcast.1.me_ref, bf16[6,32,4096]{2,1,0:T(8,128)(2,1)} %bitcast.17, bf16[6,32,4096]{2,1,0:T(8,128)(2,1)} %bitcast.21), custom_call_target="tpu_custom_call" | custom-call | bytes 2097152 | tf_op jit(solution)/shard_map/pack/pallas_call | solution.py:259
  11.0 1.9 %collective-permute-start.2 = (bf16[2,32,2048]{2,1,0:T(8,128)(2,1)}, bf16[2,32,2048]{2,1,0:T(8,128)(2,1)S(1)}, u32[]{:S(2)}, u32[]{:S(2)}) collective-permute-start(bf16[2,32,2048]{2,1,0:T(8,128)(2,1)} %get-tuple-element.42), channel_id=1, source_target_pairs={{0,4},{2,6},{4,0},{6,2},{1,5},{3,7},{5,1},{7,3},{8,12},{10,14},{12... | collective-permute-start | bytes 786440 | tf_op jit(solution)/shard_map/ppermute | solution.py:247
  12.8 2.0 %collective-permute-start.3 = (bf16[2,32,2048]{2,1,0:T(8,128)(2,1)}, bf16[2,32,2048]{2,1,0:T(8,128)(2,1)}, u32[]{:S(2)}, u32[]{:S(2)}) collective-permute-start(bf16[2,32,2048]{2,1,0:T(8,128)(2,1)} %get-tuple-element.43), channel_id=1, source_target_pairs={{0,6},{2,4},{4,2},{6,0},{1,7},{3,5},{5,3},{7,1},{8,14},{10,12},{12... | collective-permute-start | bytes 786440 | tf_op jit(solution)/shard_map/ppermute | solution.py:247
  14.8 1.0 %copy-done.4 = bf16[1,64,4096]{2,1,0:T(8,128)(2,1)S(1)} copy-done((bf16[1,64,4096]{2,1,0:T(8,128)(2,1)S(1)}, bf16[1,64,4096]{2,1,0:T(8,128)(2,1)}, u32[]{:S(2)}) %copy-start.4) | copy-done | bytes 524312
  15.9 1.6 %project.3 = (bf16[2,2,4,64,128]{4,3,2,1,0:T(8,128)(2,1)S(1)}, bf16[2,2,4,64,128]{4,3,2,1,0:T(8,128)(2,1)}) custom-call(s32[1]{0:T(128)} %bitcast.1.me_ref, bf16[6,32,4096]{2,1,0:T(8,128)(2,1)S(1)} %bitcast.24, bf16[64,4096]{1,0:T(8,128)(2,1)S(1)} %bitcast.26), custom_call_target="tpu_custom_call" | custom-call | flops 268435456 | bytes 1572864 | tf_op jit(solution)/shard_map/project/pallas_call | solution.py:272
  17.5 0.7 copy-done.6
  18.2 23.1 %collective-permute-done.refs_1_ = bf16[4,32,2048]{2,1,0:T(8,128)(2,1)} collective-permute-done((bf16[4,32,2048]{2,1,0:T(8,128)(2,1)}, bf16[4,32,2048]{2,1,0:T(8,128)(2,1)}, u32[]{:S(2)}, u32[]{:S(2)}) %collective-permute-start) | collective-permute-done | bytes 524320 | tf_op jit(solution)/shard_map/ppermute | solution.py:247
  41.4 3.5 %collective-permute-start.1 = (bf16[2,32,4096]{2,1,0:T(8,128)(2,1)}, bf16[2,32,4096]{2,1,0:T(8,128)(2,1)}, u32[]{:S(2)}, u32[]{:S(2)}) collective-permute-start(bf16[2,32,4096]{2,1,0:T(8,128)(2,1)} %get-tuple-element.41), channel_id=1, source_target_pairs={{0,2},{2,0},{4,6},{6,4},{1,3},{3,1},{5,7},{7,5},{8,10},{10,8},{12,... | collective-permute-start | bytes 1572872 | tf_op jit(solution)/shard_map/ppermute | solution.py:247
  44.9 1.3 %collective-permute-start.7 = (f32[3]{0:T(128)S(1)}, f32[3]{0:T(128)S(1)}, u32[]{:S(2)}, u32[]{:S(2)}) collective-permute-start(f32[3]{0:T(128)S(1)} %get-tuple-element.51), channel_id=1, source_target_pairs={{0,8},{1,9},{2,10},{3,11},{4,12},{5,13},{6,14},{7,15},{16,24},{17,... | collective-permute-start | bytes 44 | tf_op jit(solution)/shard_map/ppermute | solution.py:351
  46.2 0.8 collective-permute-done.7
  47.1 1.4 %copy-done.3 = bf16[1,3,2,32,4096]{4,3,2,1,0:T(8,128)(2,1)S(1)} copy-done((bf16[1,3,2,32,4096]{4,3,2,1,0:T(8,128)(2,1)S(1)}, bf16[1,3,2,32,4096]{4,3,2,1,0:T(8,128)(2,1)}, u32[]{:S(2)}) %copy-start.3) | copy-done | bytes 1572888
  48.5 1.0 %copy-done.5 = bf16[1,64,4096]{2,1,0:T(8,128)(2,1)S(1)} copy-done((bf16[1,64,4096]{2,1,0:T(8,128)(2,1)S(1)}, bf16[1,64,4096]{2,1,0:T(8,128)(2,1)}, u32[]{:S(2)}) %copy-start.5) | copy-done | bytes 524312
  50.1 5.6 %collective-permute-done.8.refs_2_ = bf16[4,32,2048]{2,1,0:T(8,128)(2,1)} collective-permute-done((bf16[4,32,2048]{2,1,0:T(8,128)(2,1)}, bf16[4,32,2048]{2,1,0:T(8,128)(2,1)}, u32[]{:S(2)}, u32[]{:S(2)}) %collective-permute-start.8) | collective-permute-done | bytes 524320 | tf_op jit(solution)/shard_map/ppermute | solution.py:247
  55.6 3.0 %score.3 = (f32[4,4,2,128,128]{4,3,2,1,0:T(8,128)S(1)}, f32[4,16,128]{2,1,0:T(8,128)S(1)}, f32[4,16,128]{2,1,0:T(8,128)S(1)}) custom-call(s32[1]{0:T(128)} %bitcast.1.me_ref, bf16[6,32,4096]{2,1,0:T(8,128)(2,1)S(1)} %bitcast.18, bf16[6,32,4096]{2,1,0:T(8,128)(2,1)S(1)} %bitcast.22, bf16[4,32,4096]{2,1,0:T(8,128)(2,1)} %collective-permute-done.5.refs_0_, ...), custom_call_target="tpu_custom_call" | custom-call | flops 1073741824 | bytes 4194304 | tf_op jit(solution)/shard_map/score/pallas_call | solution.py:293
  58.6 13.3 %collective-permute-start.9 = (f32[4,16,128]{2,1,0:T(8,128)S(1)}, f32[4,16,128]{2,1,0:T(8,128)S(1)}, u32[]{:S(2)}, u32[]{:S(2)}) collective-permute-start(f32[4,16,128]{2,1,0:T(8,128)S(1)} %get-tuple-element.56.near_ref), channel_id=1, source_target_pairs={{0,4},{2,6},{4,0},{6,2},{1,5},{3,7},{5,1},{7,3},{8,12},{10,14},{12... | collective-permute-start | bytes 98312 | tf_op jit(solution)/shard_map/ppermute | solution.py:247
  71.9 0.9 collective-permute-done.2.refs_1_
  72.8 3.9 %collective-permute-done.1.refs_0_ = bf16[2,32,4096]{2,1,0:T(8,128)(2,1)} collective-permute-done((bf16[2,32,4096]{2,1,0:T(8,128)(2,1)}, bf16[2,32,4096]{2,1,0:T(8,128)(2,1)}, u32[]{:S(2)}, u32[]{:S(2)}) %collective-permute-start.1) | collective-permute-done | bytes 524320 | tf_op jit(solution)/shard_map/ppermute | solution.py:247
  76.8 1.8 %score.2 = (f32[2,4,2,128,128]{4,3,2,1,0:T(8,128)S(1)}, f32[2,16,128]{2,1,0:T(8,128)S(1)}, f32[2,16,128]{2,1,0:T(8,128)S(1)}) custom-call(s32[1]{0:T(128)} %bitcast.1.me_ref, bf16[6,32,4096]{2,1,0:T(8,128)(2,1)S(1)} %bitcast.19, bf16[6,32,4096]{2,1,0:T(8,128)(2,1)S(1)} %bitcast.23, bf16[2,32,4096]{2,1,0:T(8,128)(2,1)} %collective-permute-done.1.refs_0_, ...), custom_call_target="tpu_custom_call" | custom-call | flops 536870912 | bytes 2097152 | tf_op jit(solution)/shard_map/score/pallas_call | solution.py:293
  78.6 2.3 %collective-permute-start.4 = (f32[2,16,128]{2,1,0:T(8,128)S(1)}, f32[2,16,128]{2,1,0:T(8,128)S(1)}, u32[]{:S(2)}, u32[]{:S(2)}) collective-permute-start(f32[2,16,128]{2,1,0:T(8,128)S(1)} %get-tuple-element.46.refs_2_), channel_id=1, source_target_pairs={{0,4},{2,6},{4,0},{6,2},{1,5},{3,7},{5,1},{7,3},{8,12},{10,14},{12... | collective-permute-start | bytes 49160 | tf_op jit(solution)/shard_map/ppermute | solution.py:247
  82.2 0.7 collective-permute-done.10.refs_2_
  82.9 1.4 %attend.2 = (f32[2,16,128]{2,1,0:T(8,128)S(1)}, f32[2,16,128]{2,1,0:T(8,128)S(1)}, f32[2,16,128]{2,1,0:T(8,128)S(1)}, f32[2,16,128]{2,1,0:T(8,128)S(1)}) custom-call(f32[1]{0:T(128)} %bitcast.scale_ref, s32[3]{0:T(128)S(1)} %broadcast_select_fusion.skip_ref, bf16[4,1024,128]{2,1,0:T(8,128)(2,1)S(1)} %weigh.1.refs_0_, ...), custom_call_target="tpu_custom_call" | custom-call | flops 2147483648 | bytes 2097152 | tf_op jit(solution)/shard_map/attend/pallas_call | solution.py:307
  84.3 1.6 %collective-permute-done.6.refs_5_ = bf16[1,2,4,64,128]{4,3,2,1,0:T(8,128)(2,1)S(1)} collective-permute-done((bf16[1,2,4,64,128]{4,3,2,1,0:T(8,128)(2,1)S(1)}, bf16[1,2,4,64,128]{4,3,2,1,0:T(8,128)(2,1)S(1)}, u32[]{:S(2)}, u32[]{:S(2)}) %collective-permute-start.6) | collective-permute-done | bytes 131104 | tf_op jit(solution)/shard_map/ppermute | solution.py:247
  85.9 0.9 attend.3
  86.9 1.9 %collective-permute-start.11 = (f32[3,16,128]{2,1,0:T(8,128)S(1)}, f32[3,16,128]{2,1,0:T(8,128)S(1)}, u32[]{:S(2)}, u32[]{:S(2)}) collective-permute-start(f32[3,16,128]{2,1,0:T(8,128)S(1)} %get-tuple-element.64), channel_id=1, source_target_pairs={{0,6},{2,4},{4,2},{6,0},{1,7},{3,5},{5,3},{7,1},{8,14},{10,12},{12... | collective-permute-start | bytes 73736 | tf_op jit(solution)/shard_map/ppermute | solution.py:247
  88.8 2.5 %collective-permute-start.13 = (f32[3,16,128]{2,1,0:T(8,128)S(1)}, f32[3,16,128]{2,1,0:T(8,128)S(1)}, u32[]{:S(2)}, u32[]{:S(2)}) collective-permute-start(f32[3,16,128]{2,1,0:T(8,128)S(1)} %get-tuple-element.66), channel_id=1, source_target_pairs={{0,4},{2,6},{4,0},{6,2},{1,5},{3,7},{5,1},{7,3},{8,12},{10,14},{12... | collective-permute-start | bytes 73736 | tf_op jit(solution)/shard_map/ppermute | solution.py:247
  91.3 1.5 %collective-permute-done.11 = f32[3,16,128]{2,1,0:T(8,128)S(1)} collective-permute-done((f32[3,16,128]{2,1,0:T(8,128)S(1)}, f32[3,16,128]{2,1,0:T(8,128)S(1)}, u32[]{:S(2)}, u32[]{:S(2)}) %collective-permute-start.11) | collective-permute-done | bytes 24608 | tf_op jit(solution)/shard_map/ppermute | solution.py:247
  92.8 0.7 collective-permute-done.13
  93.6 1.3 %collective-permute-start.14 = (f32[3,16,128]{2,1,0:T(8,128)S(1)}, f32[3,16,128]{2,1,0:T(8,128)S(1)}, u32[]{:S(2)}, u32[]{:S(2)}) collective-permute-start(f32[3,16,128]{2,1,0:T(8,128)S(1)} %bitcast_add_fusion), channel_id=1, source_target_pairs={{0,8},{1,9},{2,10},{3,11},{4,12},{5,13},{6,14},{7,15},{16,24},{17,... | collective-permute-start | bytes 73736 | tf_op jit(solution)/shard_map/ppermute | solution.py:363
  95.7 0.7 select_bitcast_fusion
  (35 shorter events, 2.8 us)
Async XLA Ops:
  3.1 41.8 %collective-permute-start.5 = (bf16[4,32,4096]{2,1,0:T(8,128)(2,1)}, bf16[4,32,4096]{2,1,0:T(8,128)(2,1)}, u32[]{:S(2)}, u32[]{:S(2)}) collective-permute-start(bf16[4,32,4096]{2,1,0:T(8,128)(2,1)} %get-tuple-element.37), channel_id=1, source_target_pairs={{0,2},{2,0},{4,6},{6,4},{1,3},{3,1},{5,7},{7,5},{8,10},{10,8},{12,... | collective-permute-start | bytes 3145736 | tf_op jit(solution)/shard_map/ppermute | solution.py:247
  6.2 35.2 %collective-permute-start = (bf16[4,32,2048]{2,1,0:T(8,128)(2,1)}, bf16[4,32,2048]{2,1,0:T(8,128)(2,1)}, u32[]{:S(2)}, u32[]{:S(2)}) collective-permute-start(bf16[4,32,2048]{2,1,0:T(8,128)(2,1)} %get-tuple-element.40), channel_id=1, source_target_pairs={{0,4},{2,6},{4,0},{6,2},{1,5},{3,7},{5,1},{7,3},{8,12},{10,14},{12... | collective-permute-start | bytes 1572872 | tf_op jit(solution)/shard_map/ppermute | solution.py:247
  8.8 6.0 %copy-start.2 = (bf16[1,3,2,32,4096]{4,3,2,1,0:T(8,128)(2,1)S(1)}, bf16[1,3,2,32,4096]{4,3,2,1,0:T(8,128)(2,1)}, u32[]{:S(2)}) copy-start(bf16[1,3,2,32,4096]{4,3,2,1,0:T(8,128)(2,1)} %param.10) | copy-start | bytes 4718596
  8.8 46.8 %collective-permute-start.8 = (bf16[4,32,2048]{2,1,0:T(8,128)(2,1)}, bf16[4,32,2048]{2,1,0:T(8,128)(2,1)}, u32[]{:S(2)}, u32[]{:S(2)}) collective-permute-start(bf16[4,32,2048]{2,1,0:T(8,128)(2,1)} %get-tuple-element.53), channel_id=1, source_target_pairs={{0,6},{2,4},{4,2},{6,0},{1,7},{3,5},{5,3},{7,1},{8,14},{10,12},{12... | collective-permute-start | bytes 1572872 | tf_op jit(solution)/shard_map/ppermute | solution.py:247
  11.0 34.0 %copy-start.9 = (s32[1,3]{1,0:T(1,128)S(1)}, s32[1,3]{1,0:T(1,128)}, u32[]{:S(2)}) copy-start(s32[1,3]{1,0:T(1,128)} %param.12) | copy-start | bytes 40
  11.0 36.1 %copy-start.10 = (s32[3]{0:T(128)S(1)}, s32[3]{0:T(128)}, u32[]{:S(2)}) copy-start(s32[3]{0:T(128)} %param.13) | copy-start | bytes 40
  11.0 61.8 %collective-permute-start.2 = (bf16[2,32,2048]{2,1,0:T(8,128)(2,1)}, bf16[2,32,2048]{2,1,0:T(8,128)(2,1)S(1)}, u32[]{:S(2)}, u32[]{:S(2)}) collective-permute-start(bf16[2,32,2048]{2,1,0:T(8,128)(2,1)} %get-tuple-element.42), channel_id=1, source_target_pairs={{0,4},{2,6},{4,0},{6,2},{1,5},{3,7},{5,1},{7,3},{8,12},{10,14},{12... | collective-permute-start | bytes 786440 | tf_op jit(solution)/shard_map/ppermute | solution.py:247
  12.8 60.0 %collective-permute-start.3 = (bf16[2,32,2048]{2,1,0:T(8,128)(2,1)}, bf16[2,32,2048]{2,1,0:T(8,128)(2,1)}, u32[]{:S(2)}, u32[]{:S(2)}) collective-permute-start(bf16[2,32,2048]{2,1,0:T(8,128)(2,1)} %get-tuple-element.43), channel_id=1, source_target_pairs={{0,6},{2,4},{4,2},{6,0},{1,7},{3,5},{5,3},{7,1},{8,14},{10,12},{12... | collective-permute-start | bytes 786440 | tf_op jit(solution)/shard_map/ppermute | solution.py:247
  14.8 1.0 %copy-start.4 = (bf16[1,64,4096]{2,1,0:T(8,128)(2,1)S(1)}, bf16[1,64,4096]{2,1,0:T(8,128)(2,1)}, u32[]{:S(2)}) copy-start(bf16[1,64,4096]{2,1,0:T(8,128)(2,1)} %param.11) | copy-start | bytes 1572868
  15.9 39.8 %copy-start.1 = (bf16[1,3,2,32,4096]{4,3,2,1,0:T(8,128)(2,1)S(1)}, bf16[1,3,2,32,4096]{4,3,2,1,0:T(8,128)(2,1)}, u32[]{:S(2)}) copy-start(bf16[1,3,2,32,4096]{4,3,2,1,0:T(8,128)(2,1)} %param.9) | copy-start | bytes 4718596
  17.5 0.7 copy-start.6
  18.2 37.4 %copy-start = (bf16[1,3,2,32,4096]{4,3,2,1,0:T(8,128)(2,1)S(1)}, bf16[1,3,2,32,4096]{4,3,2,1,0:T(8,128)(2,1)}, u32[]{:S(2)}) copy-start(bf16[1,3,2,32,4096]{4,3,2,1,0:T(8,128)(2,1)} %param.8) | copy-start | bytes 4718596
  41.4 35.4 %collective-permute-start.1 = (bf16[2,32,4096]{2,1,0:T(8,128)(2,1)}, bf16[2,32,4096]{2,1,0:T(8,128)(2,1)}, u32[]{:S(2)}, u32[]{:S(2)}) collective-permute-start(bf16[2,32,4096]{2,1,0:T(8,128)(2,1)} %get-tuple-element.41), channel_id=1, source_target_pairs={{0,2},{2,0},{4,6},{6,4},{1,3},{3,1},{5,7},{7,5},{8,10},{10,8},{12,... | collective-permute-start | bytes 1572872 | tf_op jit(solution)/shard_map/ppermute | solution.py:247
  44.9 2.1 %collective-permute-start.7 = (f32[3]{0:T(128)S(1)}, f32[3]{0:T(128)S(1)}, u32[]{:S(2)}, u32[]{:S(2)}) collective-permute-start(f32[3]{0:T(128)S(1)} %get-tuple-element.51), channel_id=1, source_target_pairs={{0,8},{1,9},{2,10},{3,11},{4,12},{5,13},{6,14},{7,15},{16,24},{17,... | collective-permute-start | bytes 44 | tf_op jit(solution)/shard_map/ppermute | solution.py:351
  47.0 35.9 %collective-permute-start.10 = (bf16[2,2,4,64,128]{4,3,2,1,0:T(8,128)(2,1)}, bf16[2,2,4,64,128]{4,3,2,1,0:T(8,128)(2,1)}, u32[]{:S(2)}, u32[]{:S(2)}) collective-permute-start(bf16[2,2,4,64,128]{4,3,2,1,0:T(8,128)(2,1)} %get-tuple-element.59), channel_id=1, source_target_pairs={{0,2},{2,0},{4,6},{6,4},{1,3},{3,1},{5,7},{7,5},{8,10},{10,8},{12,... | collective-permute-start | bytes 786440 | tf_op jit(solution)/shard_map/ppermute | solution.py:247
  47.1 1.4 %copy-start.3 = (bf16[1,3,2,32,4096]{4,3,2,1,0:T(8,128)(2,1)S(1)}, bf16[1,3,2,32,4096]{4,3,2,1,0:T(8,128)(2,1)}, u32[]{:S(2)}) copy-start(bf16[1,3,2,32,4096]{4,3,2,1,0:T(8,128)(2,1)} %param.10) | copy-start | bytes 4718596
  48.5 1.0 %copy-start.5 = (bf16[1,64,4096]{2,1,0:T(8,128)(2,1)S(1)}, bf16[1,64,4096]{2,1,0:T(8,128)(2,1)}, u32[]{:S(2)}) copy-start(bf16[1,64,4096]{2,1,0:T(8,128)(2,1)} %param.11) | copy-start | bytes 1572868
  58.6 23.0 %collective-permute-start.9 = (f32[4,16,128]{2,1,0:T(8,128)S(1)}, f32[4,16,128]{2,1,0:T(8,128)S(1)}, u32[]{:S(2)}, u32[]{:S(2)}) collective-permute-start(f32[4,16,128]{2,1,0:T(8,128)S(1)} %get-tuple-element.56.near_ref), channel_id=1, source_target_pairs={{0,4},{2,6},{4,0},{6,2},{1,5},{3,7},{5,1},{7,3},{8,12},{10,14},{12... | collective-permute-start | bytes 98312 | tf_op jit(solution)/shard_map/ppermute | solution.py:247
  78.6 5.7 %collective-permute-start.4 = (f32[2,16,128]{2,1,0:T(8,128)S(1)}, f32[2,16,128]{2,1,0:T(8,128)S(1)}, u32[]{:S(2)}, u32[]{:S(2)}) collective-permute-start(f32[2,16,128]{2,1,0:T(8,128)S(1)} %get-tuple-element.46.refs_2_), channel_id=1, source_target_pairs={{0,4},{2,6},{4,0},{6,2},{1,5},{3,7},{5,1},{7,3},{8,12},{10,14},{12... | collective-permute-start | bytes 49160 | tf_op jit(solution)/shard_map/ppermute | solution.py:247
  80.9 5.0 %collective-permute-start.6 = (bf16[1,2,4,64,128]{4,3,2,1,0:T(8,128)(2,1)S(1)}, bf16[1,2,4,64,128]{4,3,2,1,0:T(8,128)(2,1)S(1)}, u32[]{:S(2)}, u32[]{:S(2)}) collective-permute-start(bf16[1,2,4,64,128]{4,3,2,1,0:T(8,128)(2,1)S(1)} %get-tuple-element.50), channel_id=1, source_target_pairs={{0,2},{2,0},{4,6},{6,4},{1,3},{3,1},{5,7},{7,5},{8,10},{10,8},{12,... | collective-permute-start | bytes 393224 | tf_op jit(solution)/shard_map/ppermute | solution.py:247
  81.6 1.3 %copy-start.7 = (bf16[2,2,4,64,128]{4,3,2,1,0:T(8,128)(2,1)S(1)}, bf16[2,2,4,64,128]{4,3,2,1,0:T(8,128)(2,1)}, u32[]{:S(2)}) copy-start(bf16[2,2,4,64,128]{4,3,2,1,0:T(8,128)(2,1)} %copy-done.6) | copy-start | bytes 786436
  85.9 7.6 %copy-start.8 = (f32[1,3,16,128]{3,2,1,0:T(8,128)S(1)}, f32[1,3,16,128]{3,2,1,0:T(8,128)}, u32[]{:S(2)}) copy-start(f32[1,3,16,128]{3,2,1,0:T(8,128)} %param.7) | copy-start | bytes 73732
  86.9 5.9 %collective-permute-start.11 = (f32[3,16,128]{2,1,0:T(8,128)S(1)}, f32[3,16,128]{2,1,0:T(8,128)S(1)}, u32[]{:S(2)}, u32[]{:S(2)}) collective-permute-start(f32[3,16,128]{2,1,0:T(8,128)S(1)} %get-tuple-element.64), channel_id=1, source_target_pairs={{0,6},{2,4},{4,2},{6,0},{1,7},{3,5},{5,3},{7,1},{8,14},{10,12},{12... | collective-permute-start | bytes 73736 | tf_op jit(solution)/shard_map/ppermute | solution.py:247
  88.8 4.0 %collective-permute-start.12 = (f32[3,16,128]{2,1,0:T(8,128)S(1)}, f32[3,16,128]{2,1,0:T(8,128)S(1)}, u32[]{:S(2)}, u32[]{:S(2)}) collective-permute-start(f32[3,16,128]{2,1,0:T(8,128)S(1)} %get-tuple-element.65), channel_id=1, source_target_pairs={{0,2},{2,0},{4,6},{6,4},{1,3},{3,1},{5,7},{7,5},{8,10},{10,8},{12,... | collective-permute-start | bytes 73736 | tf_op jit(solution)/shard_map/ppermute | solution.py:247
  88.8 4.7 %collective-permute-start.13 = (f32[3,16,128]{2,1,0:T(8,128)S(1)}, f32[3,16,128]{2,1,0:T(8,128)S(1)}, u32[]{:S(2)}, u32[]{:S(2)}) collective-permute-start(f32[3,16,128]{2,1,0:T(8,128)S(1)} %get-tuple-element.66), channel_id=1, source_target_pairs={{0,4},{2,6},{4,0},{6,2},{1,5},{3,7},{5,1},{7,3},{8,12},{10,14},{12... | collective-permute-start | bytes 73736 | tf_op jit(solution)/shard_map/ppermute | solution.py:247
  93.6 2.1 %collective-permute-start.14 = (f32[3,16,128]{2,1,0:T(8,128)S(1)}, f32[3,16,128]{2,1,0:T(8,128)S(1)}, u32[]{:S(2)}, u32[]{:S(2)}) collective-permute-start(f32[3,16,128]{2,1,0:T(8,128)S(1)} %bitcast_add_fusion), channel_id=1, source_target_pairs={{0,8},{1,9},{2,10},{3,11},{4,12},{5,13},{6,14},{7,15},{16,24},{17,... | collective-permute-start | bytes 73736 | tf_op jit(solution)/shard_map/ppermute | solution.py:363
